TPU v7x, 32 devices: a whole 2x2x4 slice. The times are simulated.
32 devices in a mesh: crop: 4 (over z), scene: 8 (over y, x, core).
Axes of the slice: x: 2, y: 2, z: 4, core: 2. Of those that a mesh axis runs over, the one named last changes fastest.
Arguments:
- fine_feats: bfloat16 [4, 49152, 128], P('crop', 'scene'), may hold values from -6 to 6
- out_grad: bfloat16 [4, 49152, 128], P('crop', 'scene'), may hold values from -6 to 6
- pre_act: bfloat16 [4, 8, 8, 8, 64, 256], P('crop', 'scene'), may hold values from -6 to 6
- deep_grad: bfloat16 [4, 8, 8, 8, 64, 256], P('crop', 'scene'), may hold values from -6 to 6
- down_weight: bfloat16 [8, 128, 256], replicated, may hold values from -0.3125 to 0.3125
- up_weight: bfloat16 [8, 256, 128], replicated, may hold values from -0.375 to 0.375
- block_owner: int32 [4, 256, 1], P('crop', 'scene'), may hold values from 0 to 7; in each aligned block of 32 rows (0 to 31, 32 to 63, ..., all dimensions but the last counted through in order) at most 8 rows name the same one
- parent_slot: int32 [4, 49152], P('crop', 'scene'), may hold values from 0 to 63, as said below
- child_offset: int32 [4, 49152], P('crop', 'scene'), may hold values from 0 to 7, as said below
Outputs:
- fine_grad: bfloat16 [4, 49152, 128], P('crop', 'scene')
- down_grad: float32 [8, 128, 256], replicated
- up_grad: float32 [8, 256, 128], replicated
- bias_grad: float32 [256], replicated
Inputs may be any that keep to these rules, and one draw needn't show every extreme that they name: `parent_slot`: within each aligned block of 192 fine sites the parent index never falls and each of the 64 parents has 1 to 8 sites. `child_offset`: offsets strictly rise within one parent. `block_owner`: among the 32 blocks of one scene index no owner is named more than 8 times, a bound that some block reaches.
All inputs are finite; a program needn't handle non-finite values.
Results may differ from a plain program's by a relative error of at most 0.005.
Values may be sent and summed in bfloat16 or wider, within the bound.
No kernel may reach another device: no remote copies, remote signals or barrier semaphores. Data moves between devices by JAX's collectives and lax.ppermute only.
A program may use at most 128 MiB of HBM per device.

v0:
```python
import jax
import jax.numpy as jnp
from jax import lax
from jax.sharding import PartitionSpec as P


def silu_parts(pre_value):
    pre_float = pre_value.astype(jnp.float32)
    sig_value = jax.nn.sigmoid(pre_float)
    return (pre_float * sig_value, sig_value * (1.0 + pre_float * (1.0 - sig_value)))


def pick_rows(row_ids, total_rows, table):
    selector = (row_ids[:, None] == jnp.arange(total_rows, dtype=jnp.int32)[None, :]).astype(
        table.dtype
    )
    picked = jnp.dot(selector, table.reshape(total_rows, -1), preferred_element_type=jnp.float32)
    return picked.astype(table.dtype).reshape((row_ids.shape[0],) + table.shape[1:])


def local_grads(feats, cotan, places, parent_pre, parent_deep, wu_mat, wd_mat):
    block_total, rows_block, width = feats.shape
    parents_block = parent_pre.shape[1]
    out_width = parent_pre.shape[2]
    slot_ids = jnp.arange(parents_block * 8, dtype=jnp.int32)
    chooser = (places[:, :, None] == slot_ids[None, None, :]).astype(jnp.bfloat16)
    feat_slots = (
        jnp.einsum("brs,brc->bsc", chooser, feats, preferred_element_type=jnp.float32)
        .astype(feats.dtype)
        .reshape(-1, 8 * width)
    )
    cot_slots = (
        jnp.einsum("brs,brc->bsc", chooser, cotan, preferred_element_type=jnp.float32)
        .astype(cotan.dtype)
        .reshape(-1, 8 * width)
    )
    act_value, slope_value = silu_parts(parent_pre.reshape(-1, out_width))
    act_grad = parent_deep.reshape(-1, out_width).astype(jnp.float32) + jnp.dot(
        cot_slots, wu_mat, preferred_element_type=jnp.float32
    )
    pre_grad = act_grad * slope_value
    pre_grad = pre_grad.astype(jnp.bfloat16)
    slot_grads = jnp.dot(pre_grad, wd_mat, preferred_element_type=jnp.float32).astype(jnp.bfloat16)
    slot_grads = slot_grads.reshape(block_total, parents_block * 8, width)
    fine_part = jnp.einsum(
        "brs,bsc->brc", chooser, slot_grads, preferred_element_type=jnp.float32
    ).astype(jnp.bfloat16)
    contract = (((0,), (0,)), ((), ()))
    up_term = lax.dot_general(
        act_value.astype(jnp.bfloat16), cot_slots, contract, preferred_element_type=jnp.float32
    )
    down_term = lax.dot_general(feat_slots, pre_grad, contract, preferred_element_type=jnp.float32)
    bias_term = jnp.sum(pre_grad.astype(jnp.float32), axis=0)
    return (fine_part, up_term, down_term, bias_term)


def on_device(
    fine_feats,
    out_grad,
    pre_act,
    deep_grad,
    down_weight,
    up_weight,
    block_owner,
    parent_slot,
    child_offset,
):
    scene_count = lax.axis_size("scene")
    crop_count = lax.axis_size("crop")
    width = fine_feats.shape[2]
    out_width = pre_act.shape[5]
    capacity = pre_act.shape[3]
    parents_block = pre_act.shape[4]
    owners = block_owner[0, :, 0]
    block_count = owners.shape[0]
    rows_block = fine_feats.shape[1] // block_count
    wu_mat = jnp.transpose(up_weight, (0, 2, 1)).reshape(8 * width, out_width)
    wd_mat = jnp.transpose(down_weight, (2, 0, 1)).reshape(out_width, 8 * width)
    earlier = jnp.arange(block_count)[None, :] < jnp.arange(block_count)[:, None]
    same_owner = owners[:, None] == owners[None, :]
    slot_rank = jnp.sum(same_owner & earlier, axis=1)
    target = owners * capacity + slot_rank
    places = (parent_slot[0] * 8 + child_offset[0]).reshape(block_count, rows_block)
    feats = fine_feats[0].reshape(block_count, rows_block, width)
    cotan = out_grad[0].reshape(block_count, rows_block, width)
    slot_total = scene_count * capacity
    pre_here, deep_here = (
        lax.all_to_all(pre_act[0, 0], "scene", split_axis=0, concat_axis=0, tiled=True),
        lax.all_to_all(deep_grad[0, 0], "scene", split_axis=0, concat_axis=0, tiled=True),
    )
    pre_blocks = pick_rows(
        target, slot_total, pre_here.reshape(slot_total, parents_block, out_width)
    )
    deep_blocks = pick_rows(
        target, slot_total, deep_here.reshape(slot_total, parents_block, out_width)
    )
    fine_part, up_term, down_term, bias_term = local_grads(
        feats, cotan, places, pre_blocks, deep_blocks, wu_mat, wd_mat
    )
    up_total, down_total, bias_total = lax.psum((up_term, down_term, bias_term), ("crop", "scene"))
    grad_scale = float(crop_count * scene_count * fine_feats.shape[1]) ** (-0.5)
    up_grad = jnp.transpose((up_total * grad_scale).reshape(out_width, 8, width), (1, 0, 2))
    down_grad = (down_total * grad_scale).reshape(8, width, out_width)
    return (fine_part.reshape(1, -1, width), down_grad, up_grad, bias_total * grad_scale)


def solution(mesh):
    return jax.shard_map(
        on_device,
        mesh=mesh,
        in_specs=(
            P("crop", "scene", None),
            P("crop", "scene", None),
            P("crop", "scene", None, None, None, None),
            P("crop", "scene", None, None, None, None),
            P(),
            P(),
            P("crop", "scene", None),
            P("crop", "scene"),
            P("crop", "scene"),
        ),
        out_specs=(P("crop", "scene", None), P(), P(), P()),
        check_vma=False,
    )
```

profile of v0, /device:TPU:0, one launch (start us, length us, event | category | flops | bytes accessed | tf_op | source)
XLA Modules:
  0.0 248.8 jit_solution(13823868329120480726)
XLA Ops:
  7.2 32.0 %all_to_all.10 = bf16[8,8,64,256]{3,2,1,0:T(8,128)(2,1)} all-to-all(bf16[8,8,64,256]{3,2,1,0:T(8,128)(2,1)} %bitcast.42), channel_id=1, replica_groups=mesh['crop'=4,'scene'=8] {'scene'}, dimensions={0} | all-to-all | bytes 4194304 | tf_op jit(solution)/shard_map/all_to_all | solution.py:88
  39.2 4.5 %all-to-all-start = ((bf16[8,8,64,256]{3,2,1,0:T(8,128)(2,1)}), bf16[8,8,64,256]{3,2,1,0:T(8,128)(2,1)}, u32[]{:S(2)}, u32[]{:S(2)}) async-start(bf16[8,8,64,256]{3,2,1,0:T(8,128)(2,1)} %bitcast.43), calls=%async_computation | async-start | bytes 4194304 | tf_op jit(solution)/shard_map/all_to_all | solution.py:89
  43.9 7.1 %fusion.8 = bf16[32,512,128]{2,1,0:T(8,128)(2,1)} fusion(bf16[32,192,128]{2,1,0:T(8,128)(2,1)S(1)} %bitcast.40, s32[32,192]{1,0:T(8,128)S(1)} %add.36), kind=kOutput, calls=%fused_computation.12 | convolution fusion | flops 810549248 | bytes 5791744 | tf_op jit(solution)/shard_map/brs,brc->bsc/dot_general | solution.py:33
  51.0 7.3 %reshape.60 = bf16[2048,1024]{1,0:T(8,128)(2,1)} reshape(bf16[32,512,128]{2,1,0:T(8,128)(2,1)} %fusion.8) | data formatting | bytes 8388608 | tf_op jit(solution)/shard_map/reshape | solution.py:35
  58.6 8.1 %fusion.9 = bf16[32,512,128]{2,1,0:T(8,128)(2,1)} fusion(bf16[32,192,128]{2,1,0:T(8,128)(2,1)} %bitcast.48, s32[32,192]{1,0:T(8,128)S(1)} %add.36), kind=kOutput, calls=%fused_computation.13 | convolution fusion | flops 810549248 | bytes 5791744 | tf_op jit(solution)/shard_map/brs,brc->bsc/dot_general | solution.py:28
  66.7 7.3 %reshape.65 = bf16[2048,1024]{1,0:T(8,128)(2,1)} reshape(bf16[32,512,128]{2,1,0:T(8,128)(2,1)} %fusion.9) | data formatting | bytes 8388608 | tf_op jit(solution)/shard_map/reshape | solution.py:30
  74.2 2.9 %copy.20 = bf16[8,8,64,256]{3,1,2,0:T(8,128)(2,1)S(1)} copy(bf16[8,8,64,256]{3,2,1,0:T(8,128)(2,1)} %all_to_all.10) | data formatting | bytes 4194304
  77.1 2.0 multiply_convert_fusion
  79.1 2.7 %reshape.69 = f32[2048,256]{1,0:T(8,128)} reshape(f32[32,16384]{1,0:T(8,128)} %get-tuple-element.7) | data formatting | bytes 4194304 | tf_op jit(solution)/shard_map/convert_element_type | solution.py:8
  81.9 2.9 %copy.19 = bf16[8,8,64,256]{3,1,2,0:T(8,128)(2,1)S(1)} copy(bf16[8,8,64,256]{3,2,1,0:T(8,128)(2,1)} %all-to-all-done) | data formatting | bytes 4194304
  84.7 1.8 fusion.1
  86.6 2.7 %reshape.68 = f32[2048,256]{1,0:T(8,128)} reshape(f32[32,16384]{1,0:T(8,128)} %fusion.1) | data formatting | bytes 4194304 | tf_op jit(solution)/shard_map/convert_element_type | solution.py:38
  89.3 1.3 convert_element_type.65
  90.6 4.9 %fusion.17 = f32[256,1024]{1,0:T(8,128)} fusion(bf16[2048,256]{1,0:T(8,128)(2,1)} %convert_element_type.65, bf16[2048,1024]{1,0:T(8,128)(2,1)} %reshape.60), kind=kOutput, calls=%fused_computation.33 | convolution fusion | flops 1073741824 | bytes 6291456 | tf_op jit(solution)/shard_map/dot_general | solution.py:49
  95.5 3.5 %convert_reduce_fusion = (f32[256]{0:T(256)S(1)}, bf16[2048,256]{1,0:T(8,128)(2,1)S(1)}) fusion(f32[2048,256]{1,0:T(8,128)S(1)} %copy-done.3, f32[2048,256]{1,0:T(8,128)} %reshape.68, bf16[2048,1024]{1,0:T(8,128)(2,1)S(1)} %copy-done.2, bf16[1024,256]{1,0:T(8,128)(2,1)S(1)} %bitcast.47), kind=kOutput, calls=%fused_computation.17 | convolution fusion | flops 1080033024 | bytes 9962496 | tf_op jit(solution)/shard_map/dot_general | solution.py:38
  99.0 2.3 fusion.16
  101.3 1.0 copy-done.5
  102.3 3.2 %convolution_convert_fusion.2 = bf16[2048,1024]{1,0:T(8,128)(2,1)} fusion(bf16[2048,256]{1,0:T(8,128)(2,1)S(1)} %get-tuple-element.9, bf16[256,1024]{0,1:T(8,128)(2,1)S(1)} %bitcast.46), kind=kOutput, calls=%fused_computation.11 | convolution fusion | flops 1075838976 | bytes 5767168 | tf_op jit(solution)/shard_map/dot_general | solution.py:43
  105.6 7.4 %reshape.63 = bf16[32,512,128]{2,1,0:T(8,128)(2,1)} reshape(bf16[2048,1024]{1,0:T(8,128)(2,1)} %convolution_convert_fusion.2) | data formatting | bytes 8388608 | tf_op jit(solution)/shard_map/reshape | solution.py:44
  112.9 41.4 %psum.23 = f32[256]{0:T(256)S(1)} all-reduce(f32[256]{0:T(256)S(1)} %get-tuple-element.8), channel_id=1, replica_groups=mesh['crop'=4,'scene'=8] {'crop','scene'}, use_global_device_ids=true, to_apply=%region_4.0 | all-reduce | flops 256 | bytes 2048 | tf_op jit(solution)/shard_map/psum | solution.py:100
  154.9 4.9 %fusion.12 = bf16[32,192,128]{2,1,0:T(8,128)(2,1)} fusion(bf16[32,512,128]{2,1,0:T(8,128)(2,1)} %reshape.63, s32[32,192]{1,0:T(8,128)S(1)} %add.36), kind=kOutput, calls=%fused_computation.19 | convolution fusion | flops 809238528 | bytes 5791744 | tf_op jit(solution)/shard_map/brs,bsc->brc/dot_general | solution.py:45
  159.8 78.7 %all-reduce.3.cloned.1.call-done = (f32[1024,256]{1,0:T(8,128)}, f32[256,1024]{1,0:T(8,128)}) async-done(((f32[1024,256]{1,0:T(8,128)}, f32[256,1024]{1,0:T(8,128)}), (f32[1024,256]{1,0:T(8,128)}, f32[256,1024]{1,0:T(8,128)})) %all-reduce.3.cloned.1.call-update) | async-done | bytes 2097168 | tf_op jit(solution)/shard_map/psum | solution.py:100
  238.5 2.4 broadcast_multiply_fusion
  240.9 1.1 bitcast_bitcast_fusion
  (28 shorter events, 1.2 us)
Async XLA Ops:
  7.2 36.8 %copy-start = (bf16[1,6144,128]{2,1,0:T(8,128)(2,1)S(1)}, bf16[1,6144,128]{2,1,0:T(8,128)(2,1)}, u32[]{:S(2)}) copy-start(bf16[1,6144,128]{2,1,0:T(8,128)(2,1)} %param.10) | copy-start | bytes 4718596
  39.2 4.6 %copy-start.7 = (s32[1,6144]{1,0:T(1,128)S(1)}, s32[1,6144]{1,0:T(1,128)}, u32[]{:S(2)}) copy-start(s32[1,6144]{1,0:T(1,128)} %param.17) | copy-start | bytes 73732
  39.2 4.6 %copy-start.8 = (s32[1,6144]{1,0:T(1,128)S(1)}, s32[1,6144]{1,0:T(1,128)}, u32[]{:S(2)}) copy-start(s32[1,6144]{1,0:T(1,128)} %param.16) | copy-start | bytes 73732
  39.2 42.7 %all-to-all-start = ((bf16[8,8,64,256]{3,2,1,0:T(8,128)(2,1)}), bf16[8,8,64,256]{3,2,1,0:T(8,128)(2,1)}, u32[]{:S(2)}, u32[]{:S(2)}) async-start(bf16[8,8,64,256]{3,2,1,0:T(8,128)(2,1)} %bitcast.43), calls=%async_computation | async-start | bytes 4194304 | tf_op jit(solution)/shard_map/all_to_all | solution.py:89
  43.7 194.8 %all-reduce.3.cloned.1.call-start = ((), (), s32[]{:S(2)}) async-start(), calls=%async_computation.2 | async-start | bytes 4194304 | tf_op jit(solution)/shard_map/psum | solution.py:100
  51.0 7.3 %copy-start.6 = (bf16[8,256,128]{2,1,0:T(8,128)(2,1)S(1)}, bf16[8,256,128]{2,1,0:T(8,128)(2,1)}, u32[]{:S(2)}) copy-start(bf16[8,256,128]{2,1,0:T(8,128)(2,1)} %param.14) | copy-start | bytes 1572868
  66.7 7.3 %copy-start.9 = (s32[1,32,1]{1,2,0:T(1,128)S(1)}, s32[1,32,1]{1,2,0:T(1,128)}, u32[]{:S(2)}) copy-start(s32[1,32,1]{1,2,0:T(1,128)} %param.15) | copy-start | bytes 388
  90.6 4.9 %copy-start.2 = (bf16[2048,1024]{1,0:T(8,128)(2,1)S(1)}, bf16[2048,1024]{1,0:T(8,128)(2,1)}, u32[]{:S(2)}) copy-start(bf16[2048,1024]{1,0:T(8,128)(2,1)} %reshape.60) | copy-start | bytes 12582916
  90.6 4.9 %copy-start.3 = (f32[2048,256]{1,0:T(8,128)S(1)}, f32[2048,256]{1,0:T(8,128)}, u32[]{:S(2)}) copy-start(f32[2048,256]{1,0:T(8,128)} %reshape.69) | copy-start | bytes 6291460
  95.5 3.6 %copy-start.1 = (bf16[2048,1024]{1,0:T(8,128)(2,1)S(1)}, bf16[2048,1024]{1,0:T(8,128)(2,1)}, u32[]{:S(2)}) copy-start(bf16[2048,1024]{1,0:T(8,128)(2,1)} %reshape.65) | copy-start | bytes 12582916
  101.3 1.0 copy-start.5
  238.5 2.4 copy-start.4
Sparse Core Ops, SparseCore 0:
  101.5 136.9 all-reduce.2
where the time goes:
time: 250 us; the launch traced here: 249 us
  waiting for transfers between devices  78.7 us (31%)
  blocking collectives  73.4 us (29%)
  matrix products  37.9 us (15%)
  local copies, waits for them, and re-layouts  35.8 us (14%)
  between operations  14.1 us (6%)
  starting transfers between devices  4.54 us (2%)
  other arithmetic  4.26 us (2%)
    psum x1, waiting for transfers between devices, on_device(): lax.psum((up_term, down_term, bias_term), ('crop', 'scene'))  78.7 us
    psum x1, blocking collectives, on_device(): lax.psum((up_term, down_term, bias_term), ('crop', 'scene'))  41.4 us
    all_to_all x1, blocking collectives, on_device(): lax.all_to_all(pre_act[0, 0], 'scene', split_axis=0, concat_axis=0, tiled...  32 us
    dot_general x1, matrix products, local_grads(): jnp.einsum('brs,brc->bsc', chooser, feats, preferred_element_type=jnp.flo...  8.09 us
    reshape x1, local copies, waits for them, and re-layouts, local_grads(): slot_grads = slot_grads.reshape(block_total, parents_block * 8, width)  7.36 us
    reshape x1, local copies, waits for them, and re-layouts, local_grads(): cot_slots = jnp.einsum('brs,brc->bsc', chooser, cotan, preferred_element_...  7.34 us
    reshape x1, local copies, waits for them, and re-layouts, local_grads(): feat_slots = jnp.einsum('brs,brc->bsc', chooser, feats, preferred_element...  7.34 us
    dot_general x1, matrix products, local_grads(): jnp.einsum('brs,brc->bsc', chooser, cotan, preferred_element_type=jnp.flo...  7.12 us
  transfers between devices with their start and end apart: 2, of which 1 were waited for; matrix products, arithmetic and copies ran while one was open for 22% of the time, Pallas kernels for 0%

commit v1 on v0

v1 whole, which is shorter than its diff:
```python
import jax
import jax.numpy as jnp
from jax import lax
from jax.experimental import pallas as pl
from jax.experimental.pallas import tpu as pltpu
from jax.sharding import PartitionSpec as P


F32 = jnp.float32
BF16 = jnp.bfloat16
NT = (((1,), (1,)), ((), ()))
TN = (((0,), (0,)), ((), ()))
BIAS_ROWS = 16
FINE_PARTS = 4


def swap(value, axis, step):
    size = lax.axis_size(axis)
    return lax.ppermute(value, axis, [(i, i ^ step) for i in range(size)])


def expand_kernel(places, feats, cotan, up_weight, feat_slots, cot_slots, conv, wide, slot_rows):
    step = pl.program_id(0)
    group = places.shape[1]
    rows, width = feats.shape[0] // group, feats.shape[1]
    parents = slot_rows.shape[0] // group
    slots = slot_rows.shape[0]

    @pl.when(step == 0)
    def _():
        for k in range(8):
            wide[:, k * width : (k + 1) * width] = up_weight[k]

    at = pl.ds(pl.multiple_of(step * slots, slots), slots)
    for i in range(group):
        place = places[0, i : i + 1, :]
        ids = lax.broadcasted_iota(jnp.int32, (parents * 8, rows), 0)
        chooser = jnp.where(ids == place, 1.0, 0.0).astype(BF16)
        both = jnp.concatenate(
            [feats[i * rows : (i + 1) * rows, :], cotan[i * rows : (i + 1) * rows, :]], axis=1
        )
        spread = jnp.dot(chooser, both, preferred_element_type=F32).astype(BF16)
        for k in range(8):
            to = (slice(i * parents, (i + 1) * parents), slice(k * width, (k + 1) * width))
            slot_rows[to] = spread[k * parents : (k + 1) * parents, :width]
            cot_slots[
                pl.ds(pl.multiple_of(step * slots + i * parents, parents), parents),
                k * width : (k + 1) * width,
            ] = spread[k * parents : (k + 1) * parents, width:]
    feat_slots[:, at] = jnp.transpose(slot_rows[...])
    conv[at, :] = lax.dot_general(cot_slots[at, :], wide[...], NT, preferred_element_type=F32)


def each_block(table, received, body):
    capacity = received[0].shape[0]
    for k, ref in enumerate(received):
        count = table[len(received) * capacity + k]

        def one(j, _, k=k, ref=ref):
            body(ref, j, table[k * capacity + j])

        lax.fori_loop(0, count, one, None)


def deal(tiles, ids, mine, other, extra=None):
    for m, tile in enumerate(tiles):
        rows = tile.shape[0]

        @pl.when(ids[1] == m % 2)
        def _():
            mine[m // 2, :rows, :] = tile
            if extra is not None:
                mine[m // 2, rows:, :] = extra

        @pl.when(ids[1] != m % 2)
        def _():
            other[m // 2, :rows, :] = tile.astype(BF16)
            if extra is not None:
                other[m // 2, rows:, :] = extra.astype(BF16)


def act_kernel(count, table, ids, *refs):
    received, (cot_slots, slope, mine, other, act, total) = refs[:count], refs[count:]
    parents = received[0].shape[1]

    def silu(ref, j, block):
        pre = ref[j].astype(F32)
        sig = 0.5 * jnp.tanh(0.5 * pre) + 0.5
        at = pl.ds(pl.multiple_of(block * parents, parents), parents)
        slope[at, :] = sig * (1.0 + pre * (1.0 - sig))
        act[at, :] = (pre * sig).astype(BF16)

    each_block(table, received, silu)
    total[...] = lax.dot_general(act[...], cot_slots[...], TN, preferred_element_type=F32)
    pieces, rows, width = 2 * mine.shape[0], mine.shape[1], mine.shape[2]
    per = pieces // 8
    tiles = [
        total[(m % per) * rows : (m % per + 1) * rows, m // per * width : (m // per + 1) * width]
        for m in range(pieces)
    ]
    deal(tiles, ids, mine, other)


def pre_kernel(count, table, ids, *refs):
    received, rest = refs[:count], refs[count:]
    feat_slots, conv, slope, pre_grad, mine, other, total, bias = rest
    bias[...] = jnp.zeros_like(bias)
    parents = received[0].shape[1]

    def one(ref, j, block):
        at = pl.ds(pl.multiple_of(block * parents, parents), parents)
        grad = ((ref[j].astype(F32) + conv[at, :]) * slope[at, :]).astype(BF16)
        pre_grad[at, :] = grad
        wide = grad.astype(F32)
        bias[...] += jnp.sum(wide.reshape(-1, 8, wide.shape[1]), axis=0)

    each_block(table, received, one)
    total[...] = jnp.dot(feat_slots[...], pre_grad[...], preferred_element_type=F32)
    pieces = 2 * mine.shape[0]
    rows = total.shape[0] // pieces
    tiles = [total[m * rows : (m + 1) * rows, :] for m in range(pieces)]
    line = jnp.sum(bias[...], axis=0, keepdims=True)
    row = lax.broadcasted_iota(jnp.int32, (BIAS_ROWS, line.shape[1]), 0)
    high = line.astype(BF16).astype(F32)
    extra = jnp.where(row == 0, high, jnp.where(row == 1, line - high, 0.0))
    deal(tiles, ids, mine, other, extra)


def fine_kernel(places, pre_grad, down_weight, *refs):
    fine = refs[-1]
    group = places.shape[2]
    rows, width = fine.shape[0] // group, fine.shape[1]
    parents = pre_grad.shape[0] // group
    slot_grads = lax.dot_general(
        pre_grad[...], down_weight[...], NT, preferred_element_type=F32
    ).astype(BF16)
    for i in range(group):
        slots = lax.broadcasted_iota(jnp.int32, (rows, parents * 8), 1)
        chooser = jnp.where(slots == places[0, :, i : i + 1], 1.0, 0.0).astype(BF16)
        tall = jnp.concatenate(
            [
                slot_grads[i * parents : (i + 1) * parents, k * width : (k + 1) * width]
                for k in range(8)
            ],
            axis=0,
        )
        fine[i * rows : (i + 1) * rows, :] = jnp.dot(
            chooser, tall, preferred_element_type=F32
        ).astype(BF16)


def tree(values):
    while len(values) > 1:
        values = [values[i] + values[i + 1] for i in range(0, len(values), 2)]
    return values[0]


def finish_kernel(scale, with_bias, ids, *refs):
    pieces = len(refs) - 1 - with_bias
    out = refs[pieces]
    for i in range(pieces):
        m = ids[0] ^ i
        rows = out.shape[1]
        out[m] = refs[i][:rows, :].astype(F32) * scale
        if with_bias:

            @pl.when(m == 0)
            def _():
                pair = refs[i][rows : rows + 8, :].astype(F32)
                refs[-1][...] = (pair[0:1] + pair[1:2]) * scale


def grant(mebibytes):
    return pltpu.CompilerParams(vmem_limit_bytes=mebibytes << 20)


def whole_spec(shape):
    return pl.BlockSpec(shape, lambda *_: (0,) * len(shape))


def finish(scale, ids, pieces, shape, with_bias):
    outputs = [jax.ShapeDtypeStruct(shape, F32)]
    if with_bias:
        outputs.append(jax.ShapeDtypeStruct((1, shape[2]), F32))
    return pl.pallas_call(
        lambda *refs: finish_kernel(scale, with_bias, *refs),
        grid_spec=pltpu.PrefetchScalarGridSpec(
            num_scalar_prefetch=1,
            grid=(1,),
            in_specs=[whole_spec(x.shape) for x in pieces],
            out_specs=[whole_spec(x.shape) for x in outputs],
        ),
        out_shape=outputs,
        compiler_params=grant(12),
    )(ids, *pieces)


def row_of(array, index):
    start = (index,) + (jnp.uint32(0),) * (array.ndim - 1)
    return lax.dynamic_slice(array, start, (1,) + array.shape[1:])[0]


def sum_plane(peers, mine, other):
    chips = mine.shape[0]
    arrived = swap(other, "scene", 1)

    def both(peer):
        return row_of(mine, peer) + row_of(arrived, peer).astype(F32)

    sends = {d: both(peers[d]).astype(BF16) for d in range(1, chips)}
    parts = {d: swap(sends[d], "scene", 2 * d) for d in far_first(chips)}
    return tree([both(peers[0])] + [parts[d].astype(F32) for d in range(1, chips)]).astype(BF16)


def far_first(count):
    return sorted(range(1, count), key=lambda d: -bin(d).count("1"))


def sum_crops(part):
    crops = lax.axis_size("crop")
    parts = {d: swap(part, "crop", d) for d in far_first(crops)}
    return tree([part.astype(F32)] + [parts[d].astype(F32) for d in range(1, crops)]).astype(BF16)


def spread(done):
    chips = lax.axis_size("scene") // 2
    even = {d: swap(done, "scene", 2 * d) for d in far_first(chips)}
    even[0] = done
    odd = {d: swap(even[d], "scene", 1) for d in range(chips)}
    return [x for d in range(chips) for x in (even[d], odd[d])]


def exchange(array, peers):
    count = array.shape[0]
    order = exchange_order(count)
    out = {}
    for group in (order[:2], order[2:] + [0]):
        sends = {k: row_of(array, peers[k]) for k in group}
        array, *held = lax.optimization_barrier((array, *sends.values()))
        for k, send in zip(group, held):
            out[k] = send if k == 0 else swap(send, "scene", k)
    return [out[k] for k in range(count)]


def exchange_order(count):
    return [6, 2, 4, 7, 3, 5, 1] if count == 8 else list(range(1, count))


def on_device(
    fine_feats,
    out_grad,
    pre_act,
    deep_grad,
    down_weight,
    up_weight,
    block_owner,
    parent_slot,
    child_offset,
):
    scene_count = lax.axis_size("scene")
    crop_count = lax.axis_size("crop")
    width = fine_feats.shape[2]
    out_width = pre_act.shape[5]
    capacity = pre_act.shape[3]
    parents = pre_act.shape[4]
    owners = block_owner[0, :, 0]
    blocks = owners.shape[0]
    fine_rows = fine_feats.shape[1]
    rows = fine_rows // blocks
    group = 256 // parents
    steps = blocks // group
    slots = group * parents
    me = lax.axis_index("scene").astype(jnp.uint32)
    peers = [me ^ jnp.uint32(k) for k in range(scene_count)]
    chip_peers = [(me >> 1) ^ jnp.uint32(k) for k in range(scene_count // 2)]
    whole_me = me.astype(jnp.int32)
    ids = jnp.stack([whole_me, whole_me & 1])
    pre_received = exchange(pre_act[0, 0], peers)

    earlier = jnp.arange(blocks)[None, :] < jnp.arange(blocks)[:, None]
    same_owner = owners[:, None] == owners[None, :]
    slot_rank = jnp.sum(same_owner & earlier, axis=1).astype(jnp.int32)
    distance = owners ^ whole_me
    target = distance * capacity + slot_rank
    hit = target[None, :] == jnp.arange(scene_count * capacity, dtype=jnp.int32)[:, None]
    table = jnp.max(jnp.where(hit, jnp.arange(blocks, dtype=jnp.int32)[None, :], -1), axis=1)
    counts = jnp.sum(
        distance[None, :] == jnp.arange(scene_count, dtype=jnp.int32)[:, None], axis=1
    ).astype(jnp.int32)
    table = jnp.concatenate([table, counts])

    places = (child_offset[0] * parents + parent_slot[0]).reshape(steps, group, rows)
    columns = places.transpose(0, 2, 1)
    column_spec = pl.BlockSpec((1, rows, group), lambda g, *_: (g, 0, 0))
    place_spec = pl.BlockSpec((1, group, rows), lambda g, *_: (g, 0, 0))
    fine_spec = pl.BlockSpec((group * rows, width), lambda g, *_: (g, 0))
    coarse_spec = pl.BlockSpec((slots, out_width), lambda g, *_: (g, 0))
    total_rows = blocks * parents
    coarse_f32 = pltpu.VMEM((total_rows, out_width), F32)

    places, columns, ids, table, peers, chip_peers = lax.optimization_barrier(
        (places, columns, ids, table, peers, chip_peers)
    )
    hbm = pl.BlockSpec(memory_space=pltpu.HBM)
    vmem = pl.BlockSpec(memory_space=pltpu.VMEM)
    smem = pl.BlockSpec(memory_space=pltpu.SMEM)
    feat_slots, cot_slots, conv = pl.pallas_call(
        expand_kernel,
        grid=(steps,),
        in_specs=[place_spec, fine_spec, fine_spec, whole_spec(up_weight.shape)],
        out_specs=[vmem] * 3,
        out_shape=[
            pltpu.VMEM((8 * width, total_rows), BF16),
            pltpu.VMEM((total_rows, 8 * width), BF16),
            coarse_f32,
        ],
        scratch_shapes=[
            pltpu.VMEM((out_width, 8 * width), BF16),
            pltpu.VMEM((slots, 8 * width), BF16),
        ],
        compiler_params=grant(12),
    )(places, fine_feats[0], out_grad[0], up_weight)
    deep_whole, conv = lax.optimization_barrier((deep_grad[0, 0], conv))
    deep_received = exchange(deep_whole, peers)

    chips = scene_count // 2

    def dealt(rows, columns):
        shape = (chips, rows, columns)
        return [pltpu.VMEM(shape, F32), pltpu.VMEM(shape, BF16)]

    up_rows, down_rows = 8 * out_width // scene_count, 8 * width // scene_count
    slope, up_mine, up_other = pl.pallas_call(
        lambda *refs: act_kernel(scene_count, *refs),
        in_specs=[smem, smem] + [vmem] * (scene_count + 1),
        out_specs=[vmem] * 3,
        out_shape=[coarse_f32] + dealt(up_rows, width),
        scratch_shapes=[
            pltpu.VMEM((total_rows, out_width), BF16),
            pltpu.VMEM((out_width, 8 * width), F32),
        ],
        compiler_params=grant(12),
    )(table, ids, *pre_received, cot_slots)
    up_part = sum_plane(chip_peers, up_mine, up_other)
    slope, up_part = lax.optimization_barrier((slope, up_part))
    up_done = sum_crops(up_part)

    pre_grad, down_mine, down_other = pl.pallas_call(
        lambda *refs: pre_kernel(scene_count, *refs),
        in_specs=[smem, smem] + [vmem] * (scene_count + 3),
        out_specs=[vmem] * 3,
        out_shape=[pltpu.VMEM((total_rows, out_width), BF16)]
        + dealt(down_rows + BIAS_ROWS, out_width),
        scratch_shapes=[pltpu.VMEM((8 * width, out_width), F32), pltpu.VMEM((8, out_width), F32)],
        compiler_params=grant(12),
    )(table, ids, *deep_received, feat_slots, conv, slope)
    down_part = sum_plane(chip_peers, down_mine, down_other)
    down_done = sum_crops(down_part)
    up_pieces = spread(up_done)
    down_pieces = spread(down_done)

    fine = None
    flat_down = down_weight.reshape(8 * width, out_width)
    for part in range(FINE_PARTS):
        first, count = part * steps // FINE_PARTS, steps // FINE_PARTS
        at = lambda spec: pl.BlockSpec(
            spec.block_shape, lambda g, first=first: (g + first,) + (0,) * (len(spec.block_shape) - 1)
        )
        fine = pl.pallas_call(
            fine_kernel,
            grid=(count,),
            in_specs=[at(column_spec), at(coarse_spec), whole_spec(flat_down.shape)]
            + ([] if part == 0 else [hbm]),
            out_specs=at(fine_spec),
            out_shape=jax.ShapeDtypeStruct((fine_rows, width), BF16),
            input_output_aliases={} if part == 0 else {3: 0},
            compiler_params=grant(12),
        )(columns, pre_grad, flat_down, *([] if part == 0 else [fine]))

    scale = float(crop_count * scene_count * fine_rows) ** (-0.5)
    (up_grad,) = finish(scale, ids, up_pieces, (scene_count, up_rows, width), 0)
    down_grad, bias_grad = finish(scale, ids, down_pieces, (scene_count, down_rows, out_width), 1)
    return (
        fine[None],
        down_grad.reshape(8, width, out_width),
        up_grad.reshape(8, out_width, width),
        bias_grad.reshape(out_width),
    )


def solution(mesh):
    return jax.shard_map(
        on_device,
        mesh=mesh,
        in_specs=(
            P("crop", "scene", None),
            P("crop", "scene", None),
            P("crop", "scene", None, None, None, None),
            P("crop", "scene", None, None, None, None),
            P(),
            P(),
            P("crop", "scene", None),
            P("crop", "scene"),
            P("crop", "scene"),
        ),
        out_specs=(P("crop", "scene", None), P(), P(), P()),
        check_vma=False,
    )
```

time: 250 us -> 121 us (0.48)
  blocking collectives: 73.4 us -> 0 us
  starting transfers between devices: 4.54 us -> 44 us
  matrix products: 37.9 us -> 0 us
  waiting for transfers between devices: 78.7 us -> 42 us
  local copies, waits for them, and re-layouts: 35.8 us -> 7.01 us
  Pallas kernels: 0 us -> 25.8 us
  between operations: 14.1 us -> 0.88 us
  other arithmetic: 4.26 us -> 0.91 us
    psum x1 -> x0, waiting for transfers between devices: 78.7 us -> none  [on_device(): lax.psum((up_term, down_term, bias_term), ('crop', 'scene'))]
    ppermute x0 -> x42, starting transfers between devices: none -> 44 us  [swap(): return lax.ppermute(value, axis, [(i, i ^ step) for i in range(size)])]
    ppermute x0 -> x42, waiting for transfers between devices: none -> 42 us  [swap(): return lax.ppermute(value, axis, [(i, i ^ step) for i in range(size)])]
    psum x1 -> x0, blocking collectives: 41.4 us -> none  [on_device(): lax.psum((up_term, down_term, bias_term), ('crop', 'scene'))]
    dot_general x9 -> x0, matrix products: 37.9 us -> none  [the longest x1 8.09 us: local_grads(): jnp.einsum('brs,brc->bsc', chooser, feats, preferred_element_type=jnp.flo...]
    all_to_all x1 -> x0, blocking collectives: 32 us -> none  [on_device(): lax.all_to_all(pre_act[0, 0], 'scene', split_axis=0, concat_axis=0, tiled...]
    pallas_call x0 -> x9, Pallas kernels: none -> 25.8 us  [the longest x1 8.2 us: on_device(): pl.pallas_call(expand_kernel, grid=(steps,), in_specs=[place_spec, fine_s...]
    reshape x3 -> x0, local copies, waits for them, and re-layouts: 22 us -> none  [the longest x1 7.36 us: local_grads(): slot_grads = slot_grads.reshape(block_total, parents_block * 8, width)]
  transfers between devices with their start and end apart: 2 -> 42, of which waited for: 1 -> 14; matrix products, arithmetic and copies ran while one was open for 22% -> 1% of each run, Pallas kernels for 0% -> 15%
where the time goes in v1:
time: 121 us
  starting transfers between devices  44 us (36%)
  waiting for transfers between devices  42 us (35%)
  Pallas kernels  25.8 us (21%)
  local copies, waits for them, and re-layouts  7.01 us (6%)
    ppermute x42, starting transfers between devices, swap(): return lax.ppermute(value, axis, [(i, i ^ step) for i in range(size)])  44 us
    ppermute x42, waiting for transfers between devices, swap(): return lax.ppermute(value, axis, [(i, i ^ step) for i in range(size)])  42 us
    pallas_call x1, Pallas kernels, on_device(): pl.pallas_call(expand_kernel, grid=(steps,), in_specs=[place_spec, fine_s...  8.2 us
    pallas_call x4, Pallas kernels, on_device(): pl.pallas_call(fine_kernel, grid=(count,), in_specs=[at(column_spec), at(...  7.83 us
    squeeze x4, local copies, waits for them, and re-layouts, row_of(): return lax.dynamic_slice(array, start, (1,) + array.shape[1:])[0]  4.48 us
    pallas_call x1, Pallas kernels, on_device(): pl.pallas_call(lambda *refs: act_kernel(scene_count, *refs), in_specs=[sm...  3.83 us
    pallas_call x2, Pallas kernels, finish(): pl.pallas_call(lambda *refs: finish_kernel(scale, with_bias, *refs), grid...  3.22 us
    pallas_call x1, Pallas kernels, on_device(): pl.pallas_call(lambda *refs: pre_kernel(scene_count, *refs), in_specs=[sm...  2.76 us
  transfers between devices with their start and end apart: 42, of which 14 were waited for; matrix products, arithmetic and copies ran while one was open for 1% of the time, Pallas kernels for 15%

profile of v1, /device:TPU:0, one launch (start us, length us, event | category | flops | bytes accessed | tf_op | source)
XLA Modules:
  0.0 120.7 jit_solution(16347999775598217112)
XLA Ops:
  0.7 1.9 %dynamic-slice_bitcast_fusion.6 = (bf16[8,64,256]{2,1,0:T(8,128)(2,1)}, bf16[8,64,256]{2,1,0:T(8,128)(2,1)}) fusion(bf16[1,1,8,8,64,256]{5,4,3,2,1,0:T(8,128)(2,1)} %param.11, u32[]{:T(128)S(6)} %xor.46, u32[]{:T(128)S(6)} %xor.50), kind=kLoop, calls=%fused_computation.6 | loop fusion | bytes 1048584 | tf_op jit(solution)/shard_map/squeeze | solution.py:200
  2.6 2.4 %dynamic-slice_bitcast_fusion = (bf16[8,64,256]{2,1,0:T(8,128)(2,1)S(1)}, bf16[8,64,256]{2,1,0:T(8,128)(2,1)}, bf16[8,64,256]{2,1,0:T(8,128)(2,1)S(1)}, bf16[8,6...) fusion(bf16[8,8,64,256]{3,2,1,0:T(8,128)(2,1)} %bitcast.80, ...), kind=kLoop, calls=%fused_computation | loop fusion | bytes 3145752 | tf_op jit(solution)/shard_map/squeeze | solution.py:200
  5.0 3.0 %collective-permute-start.10 = (bf16[8,64,256]{2,1,0:T(8,128)(2,1)S(1)}, bf16[8,64,256]{2,1,0:T(8,128)(2,1)S(1)}, u32[]{:S(2)}, u32[]{:S(2)}) collective-permute-start(bf16[8,64,256]{2,1,0:T(8,128)(2,1)S(1)} %get-tuple-element.83), channel_id=1, source_target_pairs={{0,4},{1,5},{2,6},{3,7},{4,0},{5,1},{6,2},{7,3},{8,12},{9,13},{10,... | collective-permute-start | bytes 786440 | tf_op jit(solution)/shard_map/ppermute | solution.py:19
  8.0 2.7 %collective-permute-start.13 = (bf16[8,64,256]{2,1,0:T(8,128)(2,1)}, bf16[8,64,256]{2,1,0:T(8,128)(2,1)}, u32[]{:S(2)}, u32[]{:S(2)}) collective-permute-start(bf16[8,64,256]{2,1,0:T(8,128)(2,1)} %get-tuple-element.86), channel_id=1, source_target_pairs={{0,7},{1,6},{2,5},{3,4},{4,3},{5,2},{6,1},{7,0},{8,15},{9,14},{10,... | collective-permute-start | bytes 786440 | tf_op jit(solution)/shard_map/ppermute | solution.py:19
  11.7 9.1 %collective-permute-done.10.refs_6_ = bf16[8,64,256]{2,1,0:T(8,128)(2,1)S(1)} collective-permute-done((bf16[8,64,256]{2,1,0:T(8,128)(2,1)S(1)}, bf16[8,64,256]{2,1,0:T(8,128)(2,1)S(1)}, u32[]{:S(2)}, u32[]{:S(2)}) %collective-permute-start.10) | collective-permute-done | bytes 262176 | tf_op jit(solution)/shard_map/ppermute | solution.py:19
  20.8 3.0 %collective-permute-start.12 = (bf16[8,64,256]{2,1,0:T(8,128)(2,1)}, bf16[8,64,256]{2,1,0:T(8,128)(2,1)}, u32[]{:S(2)}, u32[]{:S(2)}) collective-permute-start(bf16[8,64,256]{2,1,0:T(8,128)(2,1)} %get-tuple-element.85), channel_id=1, source_target_pairs={{0,6},{1,7},{2,4},{3,5},{4,2},{5,3},{6,0},{7,1},{8,14},{9,15},{10,... | collective-permute-start | bytes 786440 | tf_op jit(solution)/shard_map/ppermute | solution.py:19
  23.7 6.7 %collective-permute-done.11.refs_7_ = bf16[8,64,256]{2,1,0:T(8,128)(2,1)S(1)} collective-permute-done((bf16[8,64,256]{2,1,0:T(8,128)(2,1)S(1)}, bf16[8,64,256]{2,1,0:T(8,128)(2,1)S(1)}, u32[]{:S(2)}, u32[]{:S(2)}) %collective-permute-start.11) | collective-permute-done | bytes 262176 | tf_op jit(solution)/shard_map/ppermute | solution.py:19
  34.7 8.2 %shard_map.120 = (bf16[1024,2048]{1,0:T(8,128)(2,1)S(1)}, bf16[2048,1024]{1,0:T(8,128)(2,1)S(1)}, f32[2048,256]{1,0:T(8,128)S(1)}) custom-call(s32[8,4,192]{2,1,0:T(4,128)S(1)} %add.87.places, bf16[6144,128]{1,0:T(8,128)(2,1)S(1)} %bitcast.77, bf16[6144,128]{1,0:T(8,128)(2,1)S(1)} %bitcast.78, bf16[8,256,128]{2,1,0:T(8,128)(2,1)S(1)} %copy-done.3), custom_call_target="tpu_custom_call" | custom-call | tf_op jit(solution)/shard_map/pallas_call | solution.py:307
  43.0 3.8 %shard_map.121 = (f32[2048,256]{1,0:T(8,128)S(1)}, f32[4,256,128]{2,1,0:T(8,128)S(1)}, bf16[4,256,128]{2,1,0:T(8,128)(2,1)S(1)}) custom-call(s32[72]{0:T(128)S(1)} %pad_add_fusion.1.refs_0_, s32[2]{0:T(128)S(1)} %pad_add_fusion.refs_1_.refs_0_, bf16[8,64,256]{2,1,0:T(8,128)(2,1)S(1)} %get-tuple-element.79.refs_2_, ...), custom_call_target="tpu_custom_call" | custom-call | tf_op jit(solution)/shard_map/pallas_call | solution.py:333
  53.7 2.0 %collective-permute-done.2.refs_5_ = bf16[8,64,256]{2,1,0:T(8,128)(2,1)S(1)} collective-permute-done((bf16[8,64,256]{2,1,0:T(8,128)(2,1)S(1)}, bf16[8,64,256]{2,1,0:T(8,128)(2,1)S(1)}, u32[]{:S(2)}, u32[]{:S(2)}) %collective-permute-start.2) | collective-permute-done | bytes 262176 | tf_op jit(solution)/shard_map/ppermute | solution.py:19
  55.7 2.5 %collective-permute-start.4 = (bf16[8,64,256]{2,1,0:T(8,128)(2,1)S(1)}, bf16[8,64,256]{2,1,0:T(8,128)(2,1)S(1)}, u32[]{:S(2)}, u32[]{:S(2)}) collective-permute-start(bf16[8,64,256]{2,1,0:T(8,128)(2,1)S(1)} %get-tuple-element.73), channel_id=1, source_target_pairs={{0,5},{1,4},{2,7},{3,6},{4,1},{5,0},{6,3},{7,2},{8,13},{9,12},{10,... | collective-permute-start | bytes 786440 | tf_op jit(solution)/shard_map/ppermute | solution.py:19
  61.3 6.7 %collective-permute-done.3.refs_6_ = bf16[8,64,256]{2,1,0:T(8,128)(2,1)S(1)} collective-permute-done((bf16[8,64,256]{2,1,0:T(8,128)(2,1)S(1)}, bf16[8,64,256]{2,1,0:T(8,128)(2,1)S(1)}, u32[]{:S(2)}, u32[]{:S(2)}) %collective-permute-start.3) | collective-permute-done | bytes 262176 | tf_op jit(solution)/shard_map/ppermute | solution.py:19
  68.1 4.3 %collective-permute-done.4.refs_7_ = bf16[8,64,256]{2,1,0:T(8,128)(2,1)S(1)} collective-permute-done((bf16[8,64,256]{2,1,0:T(8,128)(2,1)S(1)}, bf16[8,64,256]{2,1,0:T(8,128)(2,1)S(1)}, u32[]{:S(2)}, u32[]{:S(2)}) %collective-permute-start.4) | collective-permute-done | bytes 262176 | tf_op jit(solution)/shard_map/ppermute | solution.py:19
  72.4 5.1 %collective-permute-done.5.refs_8_ = bf16[8,64,256]{2,1,0:T(8,128)(2,1)S(1)} collective-permute-done((bf16[8,64,256]{2,1,0:T(8,128)(2,1)S(1)}, bf16[8,64,256]{2,1,0:T(8,128)(2,1)S(1)}, u32[]{:S(2)}, u32[]{:S(2)}) %collective-permute-start.5) | collective-permute-done | bytes 262176 | tf_op jit(solution)/shard_map/ppermute | solution.py:19
  77.5 2.8 %shard_map.122 = (bf16[2048,256]{1,0:T(8,128)(2,1)S(1)}, f32[4,144,256]{2,1,0:T(8,128)S(1)}, bf16[4,144,256]{2,1,0:T(8,128)(2,1)S(1)}) custom-call(s32[72]{0:T(128)S(1)} %pad_add_fusion.1.refs_0_, s32[2]{0:T(128)S(1)} %pad_add_fusion.refs_1_.refs_0_, bf16[8,64,256]{2,1,0:T(8,128)(2,1)S(1)} %get-tuple-element.68.refs_2_, ...), custom_call_target="tpu_custom_call" | custom-call | tf_op jit(solution)/shard_map/pallas_call | solution.py:348
  82.2 1.8 %collective-permute-start.19 = (bf16[144,256]{1,0:T(8,128)(2,1)S(1)}, bf16[144,256]{1,0:T(8,128)(2,1)S(1)}, u32[]{:S(2)}, u32[]{:S(2)}) collective-permute-start(bf16[144,256]{1,0:T(8,128)(2,1)S(1)} %get-tuple-element.120), channel_id=1, source_target_pairs={{0,2},{1,3},{2,0},{3,1},{4,6},{5,7},{6,4},{7,5},{8,10},{9,11},{10,... | collective-permute-start | bytes 221192 | tf_op jit(solution)/shard_map/ppermute | solution.py:19
  87.4 2.6 %collective-permute-start.33 = (bf16[256,128]{1,0:T(8,128)(2,1)S(1)}, bf16[256,128]{1,0:T(8,128)(2,1)S(1)}, u32[]{:S(2)}, u32[]{:S(2)}) collective-permute-start(bf16[256,128]{1,0:T(8,128)(2,1)S(1)} %fusion.3), channel_id=1, source_target_pairs={{0,16},{8,24},{16,0},{24,8},{1,17},{9,25},{17,1},{25,9},{2,18},{10... | collective-permute-start | bytes 196616 | tf_op jit(solution)/shard_map/ppermute | solution.py:19
  91.8 2.6 %collective-permute-start.23 = (bf16[144,256]{1,0:T(8,128)(2,1)S(1)}, bf16[144,256]{1,0:T(8,128)(2,1)S(1)}, u32[]{:S(2)}, u32[]{:S(2)}) collective-permute-start(bf16[144,256]{1,0:T(8,128)(2,1)S(1)} %fusion.1), channel_id=1, source_target_pairs={{0,16},{8,24},{16,0},{24,8},{1,17},{9,25},{17,1},{25,9},{2,18},{10... | collective-permute-start | bytes 221192 | tf_op jit(solution)/shard_map/ppermute | solution.py:19
  96.4 1.7 %collective-permute-start.36 = (bf16[256,128]{1,0:T(8,128)(2,1)S(1)}, bf16[256,128]{1,0:T(8,128)(2,1)S(1)}, u32[]{:S(2)}, u32[]{:S(2)}) collective-permute-start(bf16[256,128]{1,0:T(8,128)(2,1)S(1)} %add_convert_fusion.4.refs_1_), channel_id=1, source_target_pairs={{0,2},{1,3},{2,0},{3,1},{4,6},{5,7},{6,4},{7,5},{8,10},{9,11},{10,... | collective-permute-start | bytes 196616 | tf_op jit(solution)/shard_map/ppermute | solution.py:19
  106.7 2.3 %collective-permute-done.28.refs_5_ = bf16[144,256]{1,0:T(8,128)(2,1)S(1)} collective-permute-done((bf16[144,256]{1,0:T(8,128)(2,1)S(1)}, bf16[144,256]{1,0:T(8,128)(2,1)S(1)}, u32[]{:S(2)}, u32[]{:S(2)}) %collective-permute-start.28) | collective-permute-done | bytes 73760 | tf_op jit(solution)/shard_map/ppermute | solution.py:19
  109.6 2.0 %shard_map.123.refs_0_ = bf16[6144,128]{1,0:T(8,128)(2,1)} custom-call(s32[8,192,4]{2,1,0:T(8,128)S(1)} %bitcast.69, bf16[2048,256]{1,0:T(8,128)(2,1)S(1)} %get-tuple-element.96.pre_grad, bf16[1024,256]{1,0:T(8,128)(2,1)S(1)} %bitcast.73), custom_call_target="tpu_custom_call" | custom-call | tf_op jit(solution)/shard_map/pallas_call | solution.py:369
  111.6 2.0 %shard_map.124.refs_0_ = bf16[6144,128]{1,0:T(8,128)(2,1)} custom-call(s32[8,192,4]{2,1,0:T(8,128)S(1)} %bitcast.70, bf16[2048,256]{1,0:T(8,128)(2,1)S(1)} %get-tuple-element.96.pre_grad, bf16[1024,256]{1,0:T(8,128)(2,1)S(1)} %bitcast.74, bf16[6144,128]{1,0:T(8,128)(2,1)} %shard_map.123.refs_0_), custom_call_target="tpu_custom_call", output_to_operand_aliasing={{}: (3, {})} | custom-call | tf_op jit(solution)/shard_map/pallas_call | solution.py:369
  113.5 2.0 %shard_map.125.refs_0_ = bf16[6144,128]{1,0:T(8,128)(2,1)} custom-call(s32[8,192,4]{2,1,0:T(8,128)S(1)} %bitcast.71, bf16[2048,256]{1,0:T(8,128)(2,1)S(1)} %get-tuple-element.96.pre_grad, bf16[1024,256]{1,0:T(8,128)(2,1)S(1)} %bitcast.75, bf16[6144,128]{1,0:T(8,128)(2,1)} %shard_map.124.refs_0_), custom_call_target="tpu_custom_call", output_to_operand_aliasing={{}: (3, {})} | custom-call | tf_op jit(solution)/shard_map/pallas_call | solution.py:369
  115.5 2.0 %shard_map.126 = bf16[6144,128]{1,0:T(8,128)(2,1)} custom-call(s32[8,192,4]{2,1,0:T(8,128)S(1)} %bitcast.72, bf16[2048,256]{1,0:T(8,128)(2,1)S(1)} %get-tuple-element.96.pre_grad, bf16[1024,256]{1,0:T(8,128)(2,1)S(1)} %bitcast.76, bf16[6144,128]{1,0:T(8,128)(2,1)} %shard_map.125.refs_0_), custom_call_target="tpu_custom_call", output_to_operand_aliasing={{}: (3, {})} | custom-call | tf_op jit(solution)/shard_map/pallas_call | solution.py:369
  (108 shorter events, 36.8 us)
Async XLA Ops:
  5.0 15.8 %collective-permute-start.10 = (bf16[8,64,256]{2,1,0:T(8,128)(2,1)S(1)}, bf16[8,64,256]{2,1,0:T(8,128)(2,1)S(1)}, u32[]{:S(2)}, u32[]{:S(2)}) collective-permute-start(bf16[8,64,256]{2,1,0:T(8,128)(2,1)S(1)} %get-tuple-element.83), channel_id=1, source_target_pairs={{0,4},{1,5},{2,6},{3,7},{4,0},{5,1},{6,2},{7,3},{8,12},{9,13},{10,... | collective-permute-start | bytes 786440 | tf_op jit(solution)/shard_map/ppermute | solution.py:19
  8.0 22.4 %collective-permute-start.11 = (bf16[8,64,256]{2,1,0:T(8,128)(2,1)S(1)}, bf16[8,64,256]{2,1,0:T(8,128)(2,1)S(1)}, u32[]{:S(2)}, u32[]{:S(2)}) collective-permute-start(bf16[8,64,256]{2,1,0:T(8,128)(2,1)S(1)} %get-tuple-element.84), channel_id=1, source_target_pairs={{0,5},{1,4},{2,7},{3,6},{4,1},{5,0},{6,3},{7,2},{8,13},{9,12},{10,... | collective-permute-start | bytes 786440 | tf_op jit(solution)/shard_map/ppermute | solution.py:19
  8.0 34.9 %collective-permute-start.13 = (bf16[8,64,256]{2,1,0:T(8,128)(2,1)}, bf16[8,64,256]{2,1,0:T(8,128)(2,1)}, u32[]{:S(2)}, u32[]{:S(2)}) collective-permute-start(bf16[8,64,256]{2,1,0:T(8,128)(2,1)} %get-tuple-element.86), channel_id=1, source_target_pairs={{0,7},{1,6},{2,5},{3,4},{4,3},{5,2},{6,1},{7,0},{8,15},{9,14},{10,... | collective-permute-start | bytes 786440 | tf_op jit(solution)/shard_map/ppermute | solution.py:19
  10.7 32.2 %collective-permute-start.7 = (bf16[8,64,256]{2,1,0:T(8,128)(2,1)}, bf16[8,64,256]{2,1,0:T(8,128)(2,1)}, u32[]{:S(2)}, u32[]{:S(2)}) collective-permute-start(bf16[8,64,256]{2,1,0:T(8,128)(2,1)} %get-tuple-element.80), channel_id=1, source_target_pairs={{0,1},{1,0},{2,3},{3,2},{4,5},{5,4},{6,7},{7,6},{8,9},{9,8},{10,11... | collective-permute-start | bytes 786440 | tf_op jit(solution)/shard_map/ppermute | solution.py:19
  10.7 32.2 %collective-permute-start.9 = (bf16[8,64,256]{2,1,0:T(8,128)(2,1)}, bf16[8,64,256]{2,1,0:T(8,128)(2,1)}, u32[]{:S(2)}, u32[]{:S(2)}) collective-permute-start(bf16[8,64,256]{2,1,0:T(8,128)(2,1)} %get-tuple-element.82), channel_id=1, source_target_pairs={{0,3},{1,2},{2,1},{3,0},{4,7},{5,6},{6,5},{7,4},{8,11},{9,10},{10,... | collective-permute-start | bytes 786440 | tf_op jit(solution)/shard_map/ppermute | solution.py:19
  20.8 22.2 %collective-permute-start.12 = (bf16[8,64,256]{2,1,0:T(8,128)(2,1)}, bf16[8,64,256]{2,1,0:T(8,128)(2,1)}, u32[]{:S(2)}, u32[]{:S(2)}) collective-permute-start(bf16[8,64,256]{2,1,0:T(8,128)(2,1)} %get-tuple-element.85), channel_id=1, source_target_pairs={{0,6},{1,7},{2,4},{3,5},{4,2},{5,3},{6,0},{7,1},{8,14},{9,15},{10,... | collective-permute-start | bytes 786440 | tf_op jit(solution)/shard_map/ppermute | solution.py:19
  31.1 11.8 %collective-permute-start.8 = (bf16[8,64,256]{2,1,0:T(8,128)(2,1)}, bf16[8,64,256]{2,1,0:T(8,128)(2,1)}, u32[]{:S(2)}, u32[]{:S(2)}) collective-permute-start(bf16[8,64,256]{2,1,0:T(8,128)(2,1)} %get-tuple-element.81), channel_id=1, source_target_pairs={{0,2},{1,3},{2,0},{3,1},{4,6},{5,7},{6,4},{7,5},{8,10},{9,11},{10,... | collective-permute-start | bytes 786440 | tf_op jit(solution)/shard_map/ppermute | solution.py:19
  47.6 8.0 %collective-permute-start.2 = (bf16[8,64,256]{2,1,0:T(8,128)(2,1)S(1)}, bf16[8,64,256]{2,1,0:T(8,128)(2,1)S(1)}, u32[]{:S(2)}, u32[]{:S(2)}) collective-permute-start(bf16[8,64,256]{2,1,0:T(8,128)(2,1)S(1)} %get-tuple-element.71), channel_id=1, source_target_pairs={{0,3},{1,2},{2,1},{3,0},{4,7},{5,6},{6,5},{7,4},{8,11},{9,10},{10,... | collective-permute-start | bytes 786440 | tf_op jit(solution)/shard_map/ppermute | solution.py:19
  48.6 9.7 %collective-permute-start.15 = (bf16[256,128]{1,0:T(8,128)(2,1)S(1)}, bf16[256,128]{1,0:T(8,128)(2,1)S(1)}, u32[]{:S(2)}, u32[]{:S(2)}) collective-permute-start(bf16[256,128]{1,0:T(8,128)(2,1)S(1)} %get-tuple-element.123), channel_id=1, source_target_pairs={{0,2},{1,3},{2,0},{3,1},{4,6},{5,7},{6,4},{7,5},{8,10},{9,11},{10,... | collective-permute-start | bytes 196616 | tf_op jit(solution)/shard_map/ppermute | solution.py:19
  49.9 8.4 %collective-permute-start.16 = (bf16[256,128]{1,0:T(8,128)(2,1)S(1)}, bf16[256,128]{1,0:T(8,128)(2,1)S(1)}, u32[]{:S(2)}, u32[]{:S(2)}) collective-permute-start(bf16[256,128]{1,0:T(8,128)(2,1)S(1)} %get-tuple-element.125), channel_id=1, source_target_pairs={{0,4},{1,5},{2,6},{3,7},{4,0},{5,1},{6,2},{7,3},{8,12},{9,13},{10,... | collective-permute-start | bytes 196616 | tf_op jit(solution)/shard_map/ppermute | solution.py:19
  51.4 8.8 %collective-permute-start.17 = (bf16[256,128]{1,0:T(8,128)(2,1)S(1)}, bf16[256,128]{1,0:T(8,128)(2,1)S(1)}, u32[]{:S(2)}, u32[]{:S(2)}) collective-permute-start(bf16[256,128]{1,0:T(8,128)(2,1)S(1)} %get-tuple-element.124), channel_id=1, source_target_pairs={{0,6},{1,7},{2,4},{3,5},{4,2},{5,3},{6,0},{7,1},{8,14},{9,15},{10,... | collective-permute-start | bytes 196616 | tf_op jit(solution)/shard_map/ppermute | solution.py:19
  52.2 15.9 %collective-permute-start.3 = (bf16[8,64,256]{2,1,0:T(8,128)(2,1)S(1)}, bf16[8,64,256]{2,1,0:T(8,128)(2,1)S(1)}, u32[]{:S(2)}, u32[]{:S(2)}) collective-permute-start(bf16[8,64,256]{2,1,0:T(8,128)(2,1)S(1)} %get-tuple-element.72), channel_id=1, source_target_pairs={{0,4},{1,5},{2,6},{3,7},{4,0},{5,1},{6,2},{7,3},{8,12},{9,13},{10,... | collective-permute-start | bytes 786440 | tf_op jit(solution)/shard_map/ppermute | solution.py:19
  55.7 16.7 %collective-permute-start.4 = (bf16[8,64,256]{2,1,0:T(8,128)(2,1)S(1)}, bf16[8,64,256]{2,1,0:T(8,128)(2,1)S(1)}, u32[]{:S(2)}, u32[]{:S(2)}) collective-permute-start(bf16[8,64,256]{2,1,0:T(8,128)(2,1)S(1)} %get-tuple-element.73), channel_id=1, source_target_pairs={{0,5},{1,4},{2,7},{3,6},{4,1},{5,0},{6,3},{7,2},{8,13},{9,12},{10,... | collective-permute-start | bytes 786440 | tf_op jit(solution)/shard_map/ppermute | solution.py:19
  58.3 14.0 %collective-permute-start.6 = (bf16[8,64,256]{2,1,0:T(8,128)(2,1)S(1)}, bf16[8,64,256]{2,1,0:T(8,128)(2,1)S(1)}, u32[]{:S(2)}, u32[]{:S(2)}) collective-permute-start(bf16[8,64,256]{2,1,0:T(8,128)(2,1)S(1)} %get-tuple-element.75), channel_id=1, source_target_pairs={{0,7},{1,6},{2,5},{3,4},{4,3},{5,2},{6,1},{7,0},{8,15},{9,14},{10,... | collective-permute-start | bytes 786440 | tf_op jit(solution)/shard_map/ppermute | solution.py:19
  58.3 14.0 %collective-permute-start.1 = (bf16[8,64,256]{2,1,0:T(8,128)(2,1)S(1)}, bf16[8,64,256]{2,1,0:T(8,128)(2,1)S(1)}, u32[]{:S(2)}, u32[]{:S(2)}) collective-permute-start(bf16[8,64,256]{2,1,0:T(8,128)(2,1)S(1)} %get-tuple-element.70), channel_id=1, source_target_pairs={{0,2},{1,3},{2,0},{3,1},{4,6},{5,7},{6,4},{7,5},{8,10},{9,11},{10,... | collective-permute-start | bytes 786440 | tf_op jit(solution)/shard_map/ppermute | solution.py:19
  60.2 17.3 %collective-permute-start.5 = (bf16[8,64,256]{2,1,0:T(8,128)(2,1)S(1)}, bf16[8,64,256]{2,1,0:T(8,128)(2,1)S(1)}, u32[]{:S(2)}, u32[]{:S(2)}) collective-permute-start(bf16[8,64,256]{2,1,0:T(8,128)(2,1)S(1)} %get-tuple-element.74), channel_id=1, source_target_pairs={{0,6},{1,7},{2,4},{3,5},{4,2},{5,3},{6,0},{7,1},{8,14},{9,15},{10,... | collective-permute-start | bytes 786440 | tf_op jit(solution)/shard_map/ppermute | solution.py:19
  85.8 8.7 %collective-permute-start.32 = (bf16[256,128]{1,0:T(8,128)(2,1)S(1)}, bf16[256,128]{1,0:T(8,128)(2,1)S(1)}, u32[]{:S(2)}, u32[]{:S(2)}) collective-permute-start(bf16[256,128]{1,0:T(8,128)(2,1)S(1)} %fusion.3), channel_id=1, source_target_pairs={{0,8},{8,0},{16,24},{24,16},{1,9},{9,1},{17,25},{25,17},{2,10},{10... | collective-permute-start | bytes 196616 | tf_op jit(solution)/shard_map/ppermute | solution.py:19
  90.5 8.3 %collective-permute-start.22 = (bf16[144,256]{1,0:T(8,128)(2,1)S(1)}, bf16[144,256]{1,0:T(8,128)(2,1)S(1)}, u32[]{:S(2)}, u32[]{:S(2)}) collective-permute-start(bf16[144,256]{1,0:T(8,128)(2,1)S(1)} %fusion.1), channel_id=1, source_target_pairs={{0,8},{8,0},{16,24},{24,16},{1,9},{9,1},{17,25},{25,17},{2,10},{10... | collective-permute-start | bytes 221192 | tf_op jit(solution)/shard_map/ppermute | solution.py:19
  91.8 9.5 %collective-permute-start.23 = (bf16[144,256]{1,0:T(8,128)(2,1)S(1)}, bf16[144,256]{1,0:T(8,128)(2,1)S(1)}, u32[]{:S(2)}, u32[]{:S(2)}) collective-permute-start(bf16[144,256]{1,0:T(8,128)(2,1)S(1)} %fusion.1), channel_id=1, source_target_pairs={{0,16},{8,24},{16,0},{24,8},{1,17},{9,25},{17,1},{25,9},{2,18},{10... | collective-permute-start | bytes 221192 | tf_op jit(solution)/shard_map/ppermute | solution.py:19
  106.2 12.9 %collective-permute-start.25 = (bf16[144,256]{1,0:T(8,128)(2,1)S(1)}, bf16[144,256]{1,0:T(8,128)(2,1)S(1)}, u32[]{:S(2)}, u32[]{:S(2)}) collective-permute-start(bf16[144,256]{1,0:T(8,128)(2,1)S(1)} %add_convert_fusion.refs_1_), channel_id=1, source_target_pairs={{0,1},{1,0},{2,3},{3,2},{4,5},{5,4},{6,7},{7,6},{8,9},{9,8},{10,11... | collective-permute-start | bytes 221192 | tf_op jit(solution)/shard_map/ppermute | solution.py:19
  106.3 12.7 %collective-permute-start.27 = (bf16[144,256]{1,0:T(8,128)(2,1)S(1)}, bf16[144,256]{1,0:T(8,128)(2,1)S(1)}, u32[]{:S(2)}, u32[]{:S(2)}) collective-permute-start(bf16[144,256]{1,0:T(8,128)(2,1)S(1)} %collective-permute-done.26.refs_3_), channel_id=1, source_target_pairs={{0,1},{1,0},{2,3},{3,2},{4,5},{5,4},{6,7},{7,6},{8,9},{9,8},{10,11... | collective-permute-start | bytes 221192 | tf_op jit(solution)/shard_map/ppermute | solution.py:19
  109.0 10.0 %collective-permute-start.29 = (bf16[144,256]{1,0:T(8,128)(2,1)S(1)}, bf16[144,256]{1,0:T(8,128)(2,1)S(1)}, u32[]{:S(2)}, u32[]{:S(2)}) collective-permute-start(bf16[144,256]{1,0:T(8,128)(2,1)S(1)} %collective-permute-done.28.refs_5_), channel_id=1, source_target_pairs={{0,1},{1,0},{2,3},{3,2},{4,5},{5,4},{6,7},{7,6},{8,9},{9,8},{10,11... | collective-permute-start | bytes 221192 | tf_op jit(solution)/shard_map/ppermute | solution.py:19
  109.0 10.0 %collective-permute-start.31 = (bf16[144,256]{1,0:T(8,128)(2,1)S(1)}, bf16[144,256]{1,0:T(8,128)(2,1)S(1)}, u32[]{:S(2)}, u32[]{:S(2)}) collective-permute-start(bf16[144,256]{1,0:T(8,128)(2,1)S(1)} %collective-permute-done.30.refs_7_), channel_id=1, source_target_pairs={{0,1},{1,0},{2,3},{3,2},{4,5},{5,4},{6,7},{7,6},{8,9},{9,8},{10,11... | collective-permute-start | bytes 221192 | tf_op jit(solution)/shard_map/ppermute | solution.py:19
  109.5 7.9 %collective-permute-start.41 = (bf16[256,128]{1,0:T(8,128)(2,1)S(1)}, bf16[256,128]{1,0:T(8,128)(2,1)S(1)}, u32[]{:S(2)}, u32[]{:S(2)}) collective-permute-start(bf16[256,128]{1,0:T(8,128)(2,1)S(1)} %collective-permute-done.40.refs_7_), channel_id=1, source_target_pairs={{0,1},{1,0},{2,3},{3,2},{4,5},{5,4},{6,7},{7,6},{8,9},{9,8},{10,11... | collective-permute-start | bytes 196616 | tf_op jit(solution)/shard_map/ppermute | solution.py:19
  (28 other events, 231.2 us)

commit v2 on v1

--- a/solution.py
+++ b/solution.py
@@ -62,21 +62,16 @@
         lax.fori_loop(0, count, one, None)
 
 
-def deal(tiles, ids, mine, other, extra=None):
+def deal(tiles, ids, mine, other):
     for m, tile in enumerate(tiles):
-        rows = tile.shape[0]
 
         @pl.when(ids[1] == m % 2)
         def _():
-            mine[m // 2, :rows, :] = tile
-            if extra is not None:
-                mine[m // 2, rows:, :] = extra
+            mine[m // 2] = tile
 
         @pl.when(ids[1] != m % 2)
         def _():
-            other[m // 2, :rows, :] = tile.astype(BF16)
-            if extra is not None:
-                other[m // 2, rows:, :] = extra.astype(BF16)
+            other[m // 2] = tile.astype(BF16)
 
 
 def act_kernel(count, table, ids, *refs):
@@ -116,14 +111,27 @@
 
     each_block(table, received, one)
     total[...] = jnp.dot(feat_slots[...], pre_grad[...], preferred_element_type=F32)
-    pieces = 2 * mine.shape[0]
+    pieces, width = 2 * mine.shape[0], mine.shape[2]
     rows = total.shape[0] // pieces
-    tiles = [total[m * rows : (m + 1) * rows, :] for m in range(pieces)]
     line = jnp.sum(bias[...], axis=0, keepdims=True)
     row = lax.broadcasted_iota(jnp.int32, (BIAS_ROWS, line.shape[1]), 0)
     high = line.astype(BF16).astype(F32)
     extra = jnp.where(row == 0, high, jnp.where(row == 1, line - high, 0.0))
-    deal(tiles, ids, mine, other, extra)
+    tiles = [
+        jnp.concatenate(
+            [
+                part
+                for at in range(0, line.shape[1], width)
+                for part in (
+                    total[m * rows : (m + 1) * rows, at : at + width],
+                    extra[:, at : at + width],
+                )
+            ],
+            axis=0,
+        )
+        for m in range(pieces)
+    ]
+    deal(tiles, ids, mine, other)
 
 
 def fine_kernel(places, pre_grad, down_weight, *refs):
@@ -155,19 +163,23 @@
     return values[0]
 
 
-def finish_kernel(scale, with_bias, ids, *refs):
-    pieces = len(refs) - 1 - with_bias
-    out = refs[pieces]
-    for i in range(pieces):
+def finish_kernel(scale, ids, *refs):
+    *pieces, down_grad, up_grad, bias_grad = refs
+    rows, out_width = down_grad.shape[1:]
+    up_rows, width = up_grad.shape[1:]
+    for i, piece in enumerate(pieces):
         m = ids[0] ^ i
-        rows = out.shape[1]
-        out[m] = refs[i][:rows, :].astype(F32) * scale
-        if with_bias:
+        for at in range(0, out_width, width):
+            first = at // width * (rows + BIAS_ROWS)
+            down_grad[m, :, at : at + width] = piece[first : first + rows, :].astype(F32) * scale
 
             @pl.when(m == 0)
             def _():
-                pair = refs[i][rows : rows + 8, :].astype(F32)
-                refs[-1][...] = (pair[0:1] + pair[1:2]) * scale
+                pair = piece[first + rows : first + rows + 8, :].astype(F32)
+                bias_grad[:, at : at + width] = (pair[0:1] + pair[1:2]) * scale
+
+        first = out_width // width * (rows + BIAS_ROWS)
+        up_grad[m] = piece[first : first + up_rows, :].astype(F32) * scale
 
 
 def grant(mebibytes):
@@ -178,12 +190,12 @@
     return pl.BlockSpec(shape, lambda *_: (0,) * len(shape))
 
 
-def finish(scale, ids, pieces, shape, with_bias):
-    outputs = [jax.ShapeDtypeStruct(shape, F32)]
-    if with_bias:
-        outputs.append(jax.ShapeDtypeStruct((1, shape[2]), F32))
+def finish(scale, ids, pieces, down_shape, up_shape):
+    outputs = [
+        jax.ShapeDtypeStruct(shape, F32) for shape in (down_shape, up_shape, (1, down_shape[2]))
+    ]
     return pl.pallas_call(
-        lambda *refs: finish_kernel(scale, with_bias, *refs),
+        lambda *refs: finish_kernel(scale, *refs),
         grid_spec=pltpu.PrefetchScalarGridSpec(
             num_scalar_prefetch=1,
             grid=(1,),
@@ -230,20 +242,41 @@
     return [x for d in range(chips) for x in (even[d], odd[d])]
 
 
-def exchange(array, peers):
-    count = array.shape[0]
-    order = exchange_order(count)
+def cut(array, ids, distances):
+    def kernel(ids, array, *refs):
+        *parts, sems = refs
+        copies = [
+            pltpu.make_async_copy(array.at[ids[0] ^ k], part, sems.at[i])
+            for i, (k, part) in enumerate(zip(distances, parts))
+        ]
+        for copy in copies:
+            copy.start()
+        for copy in copies:
+            copy.wait()
+
+    return pl.pallas_call(
+        kernel,
+        in_specs=[
+            pl.BlockSpec(memory_space=pltpu.SMEM),
+            pl.BlockSpec(memory_space=pltpu.HBM),
+        ],
+        out_specs=[pl.BlockSpec(memory_space=pltpu.VMEM)] * len(distances),
+        out_shape=[pltpu.VMEM(array.shape[1:], array.dtype)] * len(distances),
+        scratch_shapes=[pltpu.SemaphoreType.DMA((len(distances),))],
+        compiler_params=grant(12),
+    )(ids, pltpu.with_memory_space_constraint(array, pltpu.HBM))
+
+
+def exchange(array, ids, groups):
     out = {}
-    for group in (order[:2], order[2:] + [0]):
-        sends = {k: row_of(array, peers[k]) for k in group}
-        array, *held = lax.optimization_barrier((array, *sends.values()))
-        for k, send in zip(group, held):
-            out[k] = send if k == 0 else swap(send, "scene", k)
-    return [out[k] for k in range(count)]
+    for group in groups:
+        for k, part in zip(group, cut(array, ids, group)):
+            out[k] = part if k == 0 else swap(part, "scene", k)
+    return [out[k] for k in range(array.shape[0])]
 
 
 def exchange_order(count):
-    return [6, 2, 4, 7, 3, 5, 1] if count == 8 else list(range(1, count))
+    return [2, 4, 6, 3, 5, 7, 1] if count == 8 else list(range(1, count))
 
 
 def on_device(
@@ -271,11 +304,11 @@
     steps = blocks // group
     slots = group * parents
     me = lax.axis_index("scene").astype(jnp.uint32)
-    peers = [me ^ jnp.uint32(k) for k in range(scene_count)]
     chip_peers = [(me >> 1) ^ jnp.uint32(k) for k in range(scene_count // 2)]
     whole_me = me.astype(jnp.int32)
     ids = jnp.stack([whole_me, whole_me & 1])
-    pre_received = exchange(pre_act[0, 0], peers)
+    order = exchange_order(scene_count)
+    pre_received = exchange(pre_act[0, 0], ids, [order[:2], order[2:] + [0]])
 
     earlier = jnp.arange(blocks)[None, :] < jnp.arange(blocks)[:, None]
     same_owner = owners[:, None] == owners[None, :]
@@ -298,8 +331,8 @@
     total_rows = blocks * parents
     coarse_f32 = pltpu.VMEM((total_rows, out_width), F32)
 
-    places, columns, ids, table, peers, chip_peers = lax.optimization_barrier(
-        (places, columns, ids, table, peers, chip_peers)
+    places, columns, ids, table, chip_peers = lax.optimization_barrier(
+        (places, columns, ids, table, chip_peers)
     )
     hbm = pl.BlockSpec(memory_space=pltpu.HBM)
     vmem = pl.BlockSpec(memory_space=pltpu.VMEM)
@@ -319,9 +352,14 @@
             pltpu.VMEM((slots, 8 * width), BF16),
         ],
         compiler_params=grant(12),
-    )(places, fine_feats[0], out_grad[0], up_weight)
+    )(
+        places,
+        pltpu.with_memory_space_constraint(fine_feats[0], pltpu.HBM),
+        pltpu.with_memory_space_constraint(out_grad[0], pltpu.HBM),
+        up_weight,
+    )
     deep_whole, conv = lax.optimization_barrier((deep_grad[0, 0], conv))
-    deep_received = exchange(deep_whole, peers)
+    deep_received = exchange(deep_whole, ids, [order + [0]])
 
     chips = scene_count // 2
 
@@ -350,14 +388,13 @@
         in_specs=[smem, smem] + [vmem] * (scene_count + 3),
         out_specs=[vmem] * 3,
         out_shape=[pltpu.VMEM((total_rows, out_width), BF16)]
-        + dealt(down_rows + BIAS_ROWS, out_width),
+        + dealt(out_width // width * (down_rows + BIAS_ROWS), width),
         scratch_shapes=[pltpu.VMEM((8 * width, out_width), F32), pltpu.VMEM((8, out_width), F32)],
         compiler_params=grant(12),
     )(table, ids, *deep_received, feat_slots, conv, slope)
     down_part = sum_plane(chip_peers, down_mine, down_other)
     down_done = sum_crops(down_part)
-    up_pieces = spread(up_done)
-    down_pieces = spread(down_done)
+    pieces = spread(jnp.concatenate([down_done, up_done]))
 
     fine = None
     flat_down = down_weight.reshape(8 * width, out_width)
@@ -378,8 +415,13 @@
         )(columns, pre_grad, flat_down, *([] if part == 0 else [fine]))
 
     scale = float(crop_count * scene_count * fine_rows) ** (-0.5)
-    (up_grad,) = finish(scale, ids, up_pieces, (scene_count, up_rows, width), 0)
-    down_grad, bias_grad = finish(scale, ids, down_pieces, (scene_count, down_rows, out_width), 1)
+    down_grad, up_grad, bias_grad = finish(
+        scale,
+        ids,
+        pieces,
+        (scene_count, down_rows, out_width),
+        (scene_count, up_rows, width),
+    )
     return (
         fine[None],
         down_grad.reshape(8, width, out_width),

time: 121 us -> 112 us (0.926)
  starting transfers between devices: 44 us -> 35.3 us
  local copies, waits for them, and re-layouts: 7.01 us -> 0.41 us
  Pallas kernels: 25.8 us -> 31.5 us
    ppermute x42 -> x35, starting transfers between devices: 44 us -> 35.3 us  [swap(): return lax.ppermute(value, axis, [(i, i ^ step) for i in range(size)])]
    pallas_call x2 -> x4, Pallas kernels: 3.22 us -> 8.77 us  [the longest x3 6.69 us: cut(): pl.pallas_call(kernel, in_specs=[pl.BlockSpec(memory_space=pltpu.SMEM), p...]
    squeeze x4 -> x0, local copies, waits for them, and re-layouts: 4.48 us -> none  [row_of(): return lax.dynamic_slice(array, start, (1,) + array.shape[1:])[0]]
    unnamed x20 -> x10, local copies, waits for them, and re-layouts: 2.15 us -> 0.02 us
    ppermute x42 -> x35, waiting for transfers between devices: 42 us -> 43.1 us  [swap(): return lax.ppermute(value, axis, [(i, i ^ step) for i in range(size)])]
  transfers between devices with their start and end apart: 42 -> 35, of which waited for: 14 -> 15; matrix products, arithmetic and copies ran while one was open for 1% -> 1% of each run, Pallas kernels for 15% -> 20%
where the time goes in v2:
time: 112 us
  waiting for transfers between devices  43.1 us (38%)
  starting transfers between devices  35.3 us (32%)
  Pallas kernels  31.5 us (28%)
    ppermute x35, waiting for transfers between devices, swap(): return lax.ppermute(value, axis, [(i, i ^ step) for i in range(size)])  43.1 us
    ppermute x35, starting transfers between devices, swap(): return lax.ppermute(value, axis, [(i, i ^ step) for i in range(size)])  35.3 us
    pallas_call x1, Pallas kernels, on_device(): pl.pallas_call(expand_kernel, grid=(steps,), in_specs=[place_spec, fine_s...  9.3 us
    pallas_call x4, Pallas kernels, on_device(): pl.pallas_call(fine_kernel, grid=(count,), in_specs=[at(column_spec), at(...  7.83 us
    pallas_call x3, Pallas kernels, cut(): pl.pallas_call(kernel, in_specs=[pl.BlockSpec(memory_space=pltpu.SMEM), p...  6.69 us
    pallas_call x1, Pallas kernels, on_device(): pl.pallas_call(lambda *refs: act_kernel(scene_count, *refs), in_specs=[sm...  2.96 us
    pallas_call x1, Pallas kernels, on_device(): pl.pallas_call(lambda *refs: pre_kernel(scene_count, *refs), in_specs=[sm...  2.7 us
  transfers between devices with their start and end apart: 35, of which 15 were waited for; matrix products, arithmetic and copies ran while one was open for 1% of the time, Pallas kernels for 20%

profile of v2, /device:TPU:0, one launch (start us, length us, event | category | flops | bytes accessed | tf_op | source)
XLA Modules:
  0.0 112.1 jit_solution(3161225421070732429)
XLA Ops:
  2.3 3.0 %collective-permute-start.8 = (bf16[8,64,256]{2,1,0:T(8,128)(2,1)S(1)}, bf16[8,64,256]{2,1,0:T(8,128)(2,1)S(1)}, u32[]{:S(2)}, u32[]{:S(2)}) collective-permute-start(bf16[8,64,256]{2,1,0:T(8,128)(2,1)S(1)} %get-tuple-element.62), channel_id=1, source_target_pairs={{0,2},{1,3},{2,0},{3,1},{4,6},{5,7},{6,4},{7,5},{8,10},{9,11},{10,... | collective-permute-start | bytes 786440 | tf_op jit(solution)/shard_map/ppermute | solution.py:19
  6.9 3.0 %shard_map.122 = (bf16[8,64,256]{2,1,0:T(8,128)(2,1)}, bf16[8,64,256]{2,1,0:T(8,128)(2,1)}, bf16[8,64,256]{2,1,0:T(8,128)(2,1)}, bf16[8,64,256]{2,1,0:T(8,128)(2...) custom-call(s32[2]{0:T(128)S(1)} %pad_add_fusion.ids.refs_1_.refs_0_, bf16[8,8,64,256]{3,2,1,0:T(8,128)(2,1)} %bitcast.47), custom_call_target="tpu_custom_call" | custom-call | tf_op jit(solution)/shard_map/pallas_call | solution.py:257
  11.7 3.6 %collective-permute-start.12 = (bf16[8,64,256]{2,1,0:T(8,128)(2,1)}, bf16[8,64,256]{2,1,0:T(8,128)(2,1)S(1)}, u32[]{:S(2)}, u32[]{:S(2)}) collective-permute-start(bf16[8,64,256]{2,1,0:T(8,128)(2,1)} %get-tuple-element.66), channel_id=1, source_target_pairs={{0,6},{1,7},{2,4},{3,5},{4,2},{5,3},{6,0},{7,1},{8,14},{9,15},{10,... | collective-permute-start | bytes 786440 | tf_op jit(solution)/shard_map/ppermute | solution.py:19
  15.9 9.3 %shard_map.120 = (bf16[1024,2048]{1,0:T(8,128)(2,1)S(1)}, bf16[2048,1024]{1,0:T(8,128)(2,1)S(1)}, f32[2048,256]{1,0:T(8,128)S(1)}) custom-call(s32[8,4,192]{2,1,0:T(4,128)S(1)} %add.87.places, bf16[6144,128]{1,0:T(8,128)(2,1)} %bitcast.49, bf16[6144,128]{1,0:T(8,128)(2,1)} %bitcast.50, bf16[8,256,128]{2,1,0:T(8,128)(2,1)S(1)} %copy-done.1), custom_call_target="tpu_custom_call" | custom-call | tf_op jit(solution)/shard_map/pallas_call | solution.py:340
  25.3 5.1 %collective-permute-done.11.refs_7_ = bf16[8,64,256]{2,1,0:T(8,128)(2,1)S(1)} collective-permute-done((bf16[8,64,256]{2,1,0:T(8,128)(2,1)}, bf16[8,64,256]{2,1,0:T(8,128)(2,1)S(1)}, u32[]{:S(2)}, u32[]{:S(2)}) %collective-permute-start.11) | collective-permute-done | bytes 262176 | tf_op jit(solution)/shard_map/ppermute | solution.py:19
  30.4 3.0 %shard_map.124 = (f32[2048,256]{1,0:T(8,128)S(1)}, f32[4,256,128]{2,1,0:T(8,128)S(1)}, bf16[4,256,128]{2,1,0:T(8,128)(2,1)S(1)}) custom-call(s32[72]{0:T(128)S(1)} %pad_add_fusion.1.refs_0_, s32[2]{0:T(128)S(1)} %pad_add_fusion.ids.refs_1_.refs_0_, bf16[8,64,256]{2,1,0:T(8,128)(2,1)S(1)} %get-tuple-element.60.refs_2_, ...), custom_call_target="tpu_custom_call" | custom-call | tf_op jit(solution)/shard_map/pallas_call | solution.py:371
  33.5 2.1 %shard_map.121 = (bf16[8,64,256]{2,1,0:T(8,128)(2,1)S(1)}, bf16[8,64,256]{2,1,0:T(8,128)(2,1)S(1)}, bf16[8,64,256]{2,1,0:T(8,128)(2,1)S(1)}, bf16[8,64,256]{2,1,...) custom-call(s32[2]{0:T(128)S(1)} %pad_add_fusion.ids.refs_1_.refs_0_, ...), custom_call_target="tpu_custom_call" | custom-call | tf_op jit(solution)/shard_map/pallas_call | solution.py:257
  41.2 4.1 %collective-permute-done.1.refs_4_ = bf16[8,64,256]{2,1,0:T(8,128)(2,1)S(1)} collective-permute-done((bf16[8,64,256]{2,1,0:T(8,128)(2,1)S(1)}, bf16[8,64,256]{2,1,0:T(8,128)(2,1)S(1)}, u32[]{:S(2)}, u32[]{:S(2)}) %collective-permute-start.1) | collective-permute-done | bytes 262176 | tf_op jit(solution)/shard_map/ppermute | solution.py:19
  48.1 2.4 %collective-permute-start.5 = (bf16[8,64,256]{2,1,0:T(8,128)(2,1)S(1)}, bf16[8,64,256]{2,1,0:T(8,128)(2,1)S(1)}, u32[]{:S(2)}, u32[]{:S(2)}) collective-permute-start(bf16[8,64,256]{2,1,0:T(8,128)(2,1)S(1)} %get-tuple-element.56), channel_id=1, source_target_pairs={{0,6},{1,7},{2,4},{3,5},{4,2},{5,3},{6,0},{7,1},{8,14},{9,15},{10,... | collective-permute-start | bytes 786440 | tf_op jit(solution)/shard_map/ppermute | solution.py:19
  50.5 2.2 %collective-permute-done.2.refs_5_ = bf16[8,64,256]{2,1,0:T(8,128)(2,1)S(1)} collective-permute-done((bf16[8,64,256]{2,1,0:T(8,128)(2,1)S(1)}, bf16[8,64,256]{2,1,0:T(8,128)(2,1)S(1)}, u32[]{:S(2)}, u32[]{:S(2)}) %collective-permute-start.2) | collective-permute-done | bytes 262176 | tf_op jit(solution)/shard_map/ppermute | solution.py:19
  52.7 13.0 %collective-permute-done.3.refs_6_ = bf16[8,64,256]{2,1,0:T(8,128)(2,1)S(1)} collective-permute-done((bf16[8,64,256]{2,1,0:T(8,128)(2,1)S(1)}, bf16[8,64,256]{2,1,0:T(8,128)(2,1)S(1)}, u32[]{:S(2)}, u32[]{:S(2)}) %collective-permute-start.3) | collective-permute-done | bytes 262176 | tf_op jit(solution)/shard_map/ppermute | solution.py:19
  65.7 2.6 %collective-permute-done.4.refs_7_ = bf16[8,64,256]{2,1,0:T(8,128)(2,1)S(1)} collective-permute-done((bf16[8,64,256]{2,1,0:T(8,128)(2,1)S(1)}, bf16[8,64,256]{2,1,0:T(8,128)(2,1)S(1)}, u32[]{:S(2)}, u32[]{:S(2)}) %collective-permute-start.4) | collective-permute-done | bytes 262176 | tf_op jit(solution)/shard_map/ppermute | solution.py:19
  68.3 2.7 %shard_map.125 = (bf16[2048,256]{1,0:T(8,128)(2,1)S(1)}, f32[4,288,128]{2,1,0:T(8,128)S(1)}, bf16[4,288,128]{2,1,0:T(8,128)(2,1)S(1)}) custom-call(s32[72]{0:T(128)S(1)} %pad_add_fusion.1.refs_0_, s32[2]{0:T(128)S(1)} %pad_add_fusion.ids.refs_1_.refs_0_, bf16[8,64,256]{2,1,0:T(8,128)(2,1)S(1)} %get-tuple-element.50.refs_2_, ...), custom_call_target="tpu_custom_call" | custom-call | tf_op jit(solution)/shard_map/pallas_call | solution.py:386
  77.2 3.6 %collective-permute-start.27 = (bf16[256,128]{1,0:T(8,128)(2,1)S(1)}, bf16[256,128]{1,0:T(8,128)(2,1)S(1)}, u32[]{:S(2)}, u32[]{:S(2)}) collective-permute-start(bf16[256,128]{1,0:T(8,128)(2,1)S(1)} %fusion.3), channel_id=1, source_target_pairs={{0,24},{8,16},{16,8},{24,0},{1,25},{9,17},{17,9},{25,1},{2,26},{10... | collective-permute-start | bytes 196616 | tf_op jit(solution)/shard_map/ppermute | solution.py:19
  81.8 3.7 %collective-permute-start.24 = (bf16[288,128]{1,0:T(8,128)(2,1)S(1)}, bf16[288,128]{1,0:T(8,128)(2,1)S(1)}, u32[]{:S(2)}, u32[]{:S(2)}) collective-permute-start(bf16[288,128]{1,0:T(8,128)(2,1)S(1)} %fusion.1), channel_id=1, source_target_pairs={{0,24},{8,16},{16,8},{24,0},{1,25},{9,17},{17,9},{25,1},{2,26},{10... | collective-permute-start | bytes 221192 | tf_op jit(solution)/shard_map/ppermute | solution.py:19
  87.5 1.7 %collective-permute-done.24 = bf16[288,128]{1,0:T(8,128)(2,1)S(1)} collective-permute-done((bf16[288,128]{1,0:T(8,128)(2,1)S(1)}, bf16[288,128]{1,0:T(8,128)(2,1)S(1)}, u32[]{:S(2)}, u32[]{:S(2)}) %collective-permute-start.24) | collective-permute-done | bytes 73760 | tf_op jit(solution)/shard_map/ppermute | solution.py:19
  89.2 3.2 %collective-permute-done.23 = bf16[288,128]{1,0:T(8,128)(2,1)S(1)} collective-permute-done((bf16[288,128]{1,0:T(8,128)(2,1)S(1)}, bf16[288,128]{1,0:T(8,128)(2,1)S(1)}, u32[]{:S(2)}, u32[]{:S(2)}) %collective-permute-start.23) | collective-permute-done | bytes 73760 | tf_op jit(solution)/shard_map/ppermute | solution.py:19
  92.5 1.7 %collective-permute-start.33 = (bf16[544,128]{1,0:T(8,128)(2,1)S(1)}, bf16[544,128]{1,0:T(8,128)(2,1)S(1)}, u32[]{:S(2)}, u32[]{:S(2)}) collective-permute-start(bf16[544,128]{1,0:T(8,128)(2,1)S(1)} %pad_maximum_fusion.refs_1_), channel_id=1, source_target_pairs={{0,6},{1,7},{2,4},{3,5},{4,2},{5,3},{6,0},{7,1},{8,14},{9,15},{10,... | collective-permute-start | bytes 417800 | tf_op jit(solution)/shard_map/ppermute | solution.py:19
  96.1 3.9 %collective-permute-done.33.refs_7_ = bf16[544,128]{1,0:T(8,128)(2,1)S(1)} collective-permute-done((bf16[544,128]{1,0:T(8,128)(2,1)S(1)}, bf16[544,128]{1,0:T(8,128)(2,1)S(1)}, u32[]{:S(2)}, u32[]{:S(2)}) %collective-permute-start.33) | collective-permute-done | bytes 139296 | tf_op jit(solution)/shard_map/ppermute | solution.py:19
  102.1 2.0 %shard_map.126.refs_0_ = bf16[6144,128]{1,0:T(8,128)(2,1)} custom-call(s32[8,192,4]{2,1,0:T(8,128)S(1)} %bitcast.37, bf16[2048,256]{1,0:T(8,128)(2,1)S(1)} %get-tuple-element.77.pre_grad, bf16[1024,256]{1,0:T(8,128)(2,1)S(1)} %bitcast.41), custom_call_target="tpu_custom_call" | custom-call | tf_op jit(solution)/shard_map/pallas_call | solution.py:406
  104.1 2.0 %shard_map.127.refs_0_ = bf16[6144,128]{1,0:T(8,128)(2,1)} custom-call(s32[8,192,4]{2,1,0:T(8,128)S(1)} %bitcast.38, bf16[2048,256]{1,0:T(8,128)(2,1)S(1)} %get-tuple-element.77.pre_grad, bf16[1024,256]{1,0:T(8,128)(2,1)S(1)} %bitcast.42, bf16[6144,128]{1,0:T(8,128)(2,1)} %shard_map.126.refs_0_), custom_call_target="tpu_custom_call", output_to_operand_aliasing={{}: (3, {})} | custom-call | tf_op jit(solution)/shard_map/pallas_call | solution.py:406
  106.0 2.0 %shard_map.128.refs_0_ = bf16[6144,128]{1,0:T(8,128)(2,1)} custom-call(s32[8,192,4]{2,1,0:T(8,128)S(1)} %bitcast.39, bf16[2048,256]{1,0:T(8,128)(2,1)S(1)} %get-tuple-element.77.pre_grad, bf16[1024,256]{1,0:T(8,128)(2,1)S(1)} %bitcast.43, bf16[6144,128]{1,0:T(8,128)(2,1)} %shard_map.127.refs_0_), custom_call_target="tpu_custom_call", output_to_operand_aliasing={{}: (3, {})} | custom-call | tf_op jit(solution)/shard_map/pallas_call | solution.py:406
  108.0 2.0 %shard_map.129 = bf16[6144,128]{1,0:T(8,128)(2,1)} custom-call(s32[8,192,4]{2,1,0:T(8,128)S(1)} %bitcast.40, bf16[2048,256]{1,0:T(8,128)(2,1)S(1)} %get-tuple-element.77.pre_grad, bf16[1024,256]{1,0:T(8,128)(2,1)S(1)} %bitcast.44, bf16[6144,128]{1,0:T(8,128)(2,1)} %shard_map.128.refs_0_), custom_call_target="tpu_custom_call", output_to_operand_aliasing={{}: (3, {})} | custom-call | tf_op jit(solution)/shard_map/pallas_call | solution.py:406
  110.0 2.1 %shard_map.130 = (f32[8,128,256]{2,1,0:T(8,128)}, f32[8,256,128]{2,1,0:T(8,128)}, f32[1,256]{1,0:T(1,128)}) custom-call(s32[2]{0:T(128)S(1)} %pad_add_fusion.ids.refs_1_.refs_0_, bf16[544,128]{1,0:T(8,128)(2,1)S(1)} %pad_maximum_fusion.refs_1_, bf16[544,128]{1,0:T(8,128)(2,1)S(1)} %collective-permute-done.28.refs_2_, ...), custom_call_target="tpu_custom_call" | custom-call | tf_op jit(solution)/shard_map/pallas_call | solution.py:197
  (83 shorter events, 27.5 us)
Async XLA Ops:
  2.3 9.3 %collective-permute-start.8 = (bf16[8,64,256]{2,1,0:T(8,128)(2,1)S(1)}, bf16[8,64,256]{2,1,0:T(8,128)(2,1)S(1)}, u32[]{:S(2)}, u32[]{:S(2)}) collective-permute-start(bf16[8,64,256]{2,1,0:T(8,128)(2,1)S(1)} %get-tuple-element.62), channel_id=1, source_target_pairs={{0,2},{1,3},{2,0},{3,1},{4,6},{5,7},{6,4},{7,5},{8,10},{9,11},{10,... | collective-permute-start | bytes 786440 | tf_op jit(solution)/shard_map/ppermute | solution.py:19
  5.4 9.9 %collective-permute-start.10 = (bf16[8,64,256]{2,1,0:T(8,128)(2,1)S(1)}, bf16[8,64,256]{2,1,0:T(8,128)(2,1)S(1)}, u32[]{:S(2)}, u32[]{:S(2)}) collective-permute-start(bf16[8,64,256]{2,1,0:T(8,128)(2,1)S(1)} %get-tuple-element.64), channel_id=1, source_target_pairs={{0,4},{1,5},{2,6},{3,7},{4,0},{5,1},{6,2},{7,3},{8,12},{9,13},{10,... | collective-permute-start | bytes 786440 | tf_op jit(solution)/shard_map/ppermute | solution.py:19
  9.9 15.4 %collective-permute-start.7 = (bf16[8,64,256]{2,1,0:T(8,128)(2,1)}, bf16[8,64,256]{2,1,0:T(8,128)(2,1)S(1)}, u32[]{:S(2)}, u32[]{:S(2)}) collective-permute-start(bf16[8,64,256]{2,1,0:T(8,128)(2,1)} %get-tuple-element.61), channel_id=1, source_target_pairs={{0,1},{1,0},{2,3},{3,2},{4,5},{5,4},{6,7},{7,6},{8,9},{9,8},{10,11... | collective-permute-start | bytes 786440 | tf_op jit(solution)/shard_map/ppermute | solution.py:19
  9.9 15.3 %collective-permute-start.9 = (bf16[8,64,256]{2,1,0:T(8,128)(2,1)}, bf16[8,64,256]{2,1,0:T(8,128)(2,1)S(1)}, u32[]{:S(2)}, u32[]{:S(2)}) collective-permute-start(bf16[8,64,256]{2,1,0:T(8,128)(2,1)} %get-tuple-element.63), channel_id=1, source_target_pairs={{0,3},{1,2},{2,1},{3,0},{4,7},{5,6},{6,5},{7,4},{8,11},{9,10},{10,... | collective-permute-start | bytes 786440 | tf_op jit(solution)/shard_map/ppermute | solution.py:19
  10.6 19.8 %collective-permute-start.11 = (bf16[8,64,256]{2,1,0:T(8,128)(2,1)}, bf16[8,64,256]{2,1,0:T(8,128)(2,1)S(1)}, u32[]{:S(2)}, u32[]{:S(2)}) collective-permute-start(bf16[8,64,256]{2,1,0:T(8,128)(2,1)} %get-tuple-element.65), channel_id=1, source_target_pairs={{0,5},{1,4},{2,7},{3,6},{4,1},{5,0},{6,3},{7,2},{8,13},{9,12},{10,... | collective-permute-start | bytes 786440 | tf_op jit(solution)/shard_map/ppermute | solution.py:19
  11.7 18.7 %collective-permute-start.12 = (bf16[8,64,256]{2,1,0:T(8,128)(2,1)}, bf16[8,64,256]{2,1,0:T(8,128)(2,1)S(1)}, u32[]{:S(2)}, u32[]{:S(2)}) collective-permute-start(bf16[8,64,256]{2,1,0:T(8,128)(2,1)} %get-tuple-element.66), channel_id=1, source_target_pairs={{0,6},{1,7},{2,4},{3,5},{4,2},{5,3},{6,0},{7,1},{8,14},{9,15},{10,... | collective-permute-start | bytes 786440 | tf_op jit(solution)/shard_map/ppermute | solution.py:19
  15.2 15.1 %collective-permute-start.13 = (bf16[8,64,256]{2,1,0:T(8,128)(2,1)}, bf16[8,64,256]{2,1,0:T(8,128)(2,1)S(1)}, u32[]{:S(2)}, u32[]{:S(2)}) collective-permute-start(bf16[8,64,256]{2,1,0:T(8,128)(2,1)} %get-tuple-element.67), channel_id=1, source_target_pairs={{0,7},{1,6},{2,5},{3,4},{4,3},{5,2},{6,1},{7,0},{8,15},{9,14},{10,... | collective-permute-start | bytes 786440 | tf_op jit(solution)/shard_map/ppermute | solution.py:19
  36.1 9.2 %collective-permute-start.1 = (bf16[8,64,256]{2,1,0:T(8,128)(2,1)S(1)}, bf16[8,64,256]{2,1,0:T(8,128)(2,1)S(1)}, u32[]{:S(2)}, u32[]{:S(2)}) collective-permute-start(bf16[8,64,256]{2,1,0:T(8,128)(2,1)S(1)} %get-tuple-element.52), channel_id=1, source_target_pairs={{0,2},{1,3},{2,0},{3,1},{4,6},{5,7},{6,4},{7,5},{8,10},{9,11},{10,... | collective-permute-start | bytes 786440 | tf_op jit(solution)/shard_map/ppermute | solution.py:19
  37.6 9.0 %collective-permute-start.15 = (bf16[256,128]{1,0:T(8,128)(2,1)S(1)}, bf16[256,128]{1,0:T(8,128)(2,1)S(1)}, u32[]{:S(2)}, u32[]{:S(2)}) collective-permute-start(bf16[256,128]{1,0:T(8,128)(2,1)S(1)} %get-tuple-element.89), channel_id=1, source_target_pairs={{0,2},{1,3},{2,0},{3,1},{4,6},{5,7},{6,4},{7,5},{8,10},{9,11},{10,... | collective-permute-start | bytes 196616 | tf_op jit(solution)/shard_map/ppermute | solution.py:19
  38.2 9.8 %collective-permute-start.17 = (bf16[256,128]{1,0:T(8,128)(2,1)S(1)}, bf16[256,128]{1,0:T(8,128)(2,1)S(1)}, u32[]{:S(2)}, u32[]{:S(2)}) collective-permute-start(bf16[256,128]{1,0:T(8,128)(2,1)S(1)} %get-tuple-element.90), channel_id=1, source_target_pairs={{0,6},{1,7},{2,4},{3,5},{4,2},{5,3},{6,0},{7,1},{8,14},{9,15},{10,... | collective-permute-start | bytes 196616 | tf_op jit(solution)/shard_map/ppermute | solution.py:19
  39.7 10.8 %collective-permute-start.16 = (bf16[256,128]{1,0:T(8,128)(2,1)S(1)}, bf16[256,128]{1,0:T(8,128)(2,1)S(1)}, u32[]{:S(2)}, u32[]{:S(2)}) collective-permute-start(bf16[256,128]{1,0:T(8,128)(2,1)S(1)} %get-tuple-element.91), channel_id=1, source_target_pairs={{0,4},{1,5},{2,6},{3,7},{4,0},{5,1},{6,2},{7,3},{8,12},{9,13},{10,... | collective-permute-start | bytes 196616 | tf_op jit(solution)/shard_map/ppermute | solution.py:19
  41.2 11.5 %collective-permute-start.2 = (bf16[8,64,256]{2,1,0:T(8,128)(2,1)S(1)}, bf16[8,64,256]{2,1,0:T(8,128)(2,1)S(1)}, u32[]{:S(2)}, u32[]{:S(2)}) collective-permute-start(bf16[8,64,256]{2,1,0:T(8,128)(2,1)S(1)} %get-tuple-element.53), channel_id=1, source_target_pairs={{0,3},{1,2},{2,1},{3,0},{4,7},{5,6},{6,5},{7,4},{8,11},{9,10},{10,... | collective-permute-start | bytes 786440 | tf_op jit(solution)/shard_map/ppermute | solution.py:19
  45.3 20.4 %collective-permute-start.3 = (bf16[8,64,256]{2,1,0:T(8,128)(2,1)S(1)}, bf16[8,64,256]{2,1,0:T(8,128)(2,1)S(1)}, u32[]{:S(2)}, u32[]{:S(2)}) collective-permute-start(bf16[8,64,256]{2,1,0:T(8,128)(2,1)S(1)} %get-tuple-element.54), channel_id=1, source_target_pairs={{0,4},{1,5},{2,6},{3,7},{4,0},{5,1},{6,2},{7,3},{8,12},{9,13},{10,... | collective-permute-start | bytes 786440 | tf_op jit(solution)/shard_map/ppermute | solution.py:19
  46.7 21.6 %collective-permute-start.4 = (bf16[8,64,256]{2,1,0:T(8,128)(2,1)S(1)}, bf16[8,64,256]{2,1,0:T(8,128)(2,1)S(1)}, u32[]{:S(2)}, u32[]{:S(2)}) collective-permute-start(bf16[8,64,256]{2,1,0:T(8,128)(2,1)S(1)} %get-tuple-element.55), channel_id=1, source_target_pairs={{0,5},{1,4},{2,7},{3,6},{4,1},{5,0},{6,3},{7,2},{8,13},{9,12},{10,... | collective-permute-start | bytes 786440 | tf_op jit(solution)/shard_map/ppermute | solution.py:19
  48.1 20.3 %collective-permute-start.5 = (bf16[8,64,256]{2,1,0:T(8,128)(2,1)S(1)}, bf16[8,64,256]{2,1,0:T(8,128)(2,1)S(1)}, u32[]{:S(2)}, u32[]{:S(2)}) collective-permute-start(bf16[8,64,256]{2,1,0:T(8,128)(2,1)S(1)} %get-tuple-element.56), channel_id=1, source_target_pairs={{0,6},{1,7},{2,4},{3,5},{4,2},{5,3},{6,0},{7,1},{8,14},{9,15},{10,... | collective-permute-start | bytes 786440 | tf_op jit(solution)/shard_map/ppermute | solution.py:19
  50.5 17.9 %collective-permute-start.6 = (bf16[8,64,256]{2,1,0:T(8,128)(2,1)S(1)}, bf16[8,64,256]{2,1,0:T(8,128)(2,1)S(1)}, u32[]{:S(2)}, u32[]{:S(2)}) collective-permute-start(bf16[8,64,256]{2,1,0:T(8,128)(2,1)S(1)} %get-tuple-element.57), channel_id=1, source_target_pairs={{0,7},{1,6},{2,5},{3,4},{4,3},{5,2},{6,1},{7,0},{8,15},{9,14},{10,... | collective-permute-start | bytes 786440 | tf_op jit(solution)/shard_map/ppermute | solution.py:19
  77.2 8.2 %collective-permute-start.27 = (bf16[256,128]{1,0:T(8,128)(2,1)S(1)}, bf16[256,128]{1,0:T(8,128)(2,1)S(1)}, u32[]{:S(2)}, u32[]{:S(2)}) collective-permute-start(bf16[256,128]{1,0:T(8,128)(2,1)S(1)} %fusion.3), channel_id=1, source_target_pairs={{0,24},{8,16},{16,8},{24,0},{1,25},{9,17},{17,9},{25,1},{2,26},{10... | collective-permute-start | bytes 196616 | tf_op jit(solution)/shard_map/ppermute | solution.py:19
  81.8 7.4 %collective-permute-start.24 = (bf16[288,128]{1,0:T(8,128)(2,1)S(1)}, bf16[288,128]{1,0:T(8,128)(2,1)S(1)}, u32[]{:S(2)}, u32[]{:S(2)}) collective-permute-start(bf16[288,128]{1,0:T(8,128)(2,1)S(1)} %fusion.1), channel_id=1, source_target_pairs={{0,24},{8,16},{16,8},{24,0},{1,25},{9,17},{17,9},{25,1},{2,26},{10... | collective-permute-start | bytes 221192 | tf_op jit(solution)/shard_map/ppermute | solution.py:19
  92.5 7.4 %collective-permute-start.33 = (bf16[544,128]{1,0:T(8,128)(2,1)S(1)}, bf16[544,128]{1,0:T(8,128)(2,1)S(1)}, u32[]{:S(2)}, u32[]{:S(2)}) collective-permute-start(bf16[544,128]{1,0:T(8,128)(2,1)S(1)} %pad_maximum_fusion.refs_1_), channel_id=1, source_target_pairs={{0,6},{1,7},{2,4},{3,5},{4,2},{5,3},{6,0},{7,1},{8,14},{9,15},{10,... | collective-permute-start | bytes 417800 | tf_op jit(solution)/shard_map/ppermute | solution.py:19
  94.2 7.4 %collective-permute-start.31 = (bf16[544,128]{1,0:T(8,128)(2,1)S(1)}, bf16[544,128]{1,0:T(8,128)(2,1)S(1)}, u32[]{:S(2)}, u32[]{:S(2)}) collective-permute-start(bf16[544,128]{1,0:T(8,128)(2,1)S(1)} %pad_maximum_fusion.refs_1_), channel_id=1, source_target_pairs={{0,4},{1,5},{2,6},{3,7},{4,0},{5,1},{6,2},{7,3},{8,12},{9,13},{10,... | collective-permute-start | bytes 417800 | tf_op jit(solution)/shard_map/ppermute | solution.py:19
  96.1 13.9 %collective-permute-start.28 = (bf16[544,128]{1,0:T(8,128)(2,1)S(1)}, bf16[544,128]{1,0:T(8,128)(2,1)S(1)}, u32[]{:S(2)}, u32[]{:S(2)}) collective-permute-start(bf16[544,128]{1,0:T(8,128)(2,1)S(1)} %pad_maximum_fusion.refs_1_), channel_id=1, source_target_pairs={{0,1},{1,0},{2,3},{3,2},{4,5},{5,4},{6,7},{7,6},{8,9},{9,8},{10,11... | collective-permute-start | bytes 417800 | tf_op jit(solution)/shard_map/ppermute | solution.py:19
  100.0 10.0 %collective-permute-start.34 = (bf16[544,128]{1,0:T(8,128)(2,1)S(1)}, bf16[544,128]{1,0:T(8,128)(2,1)S(1)}, u32[]{:S(2)}, u32[]{:S(2)}) collective-permute-start(bf16[544,128]{1,0:T(8,128)(2,1)S(1)} %collective-permute-done.33.refs_7_), channel_id=1, source_target_pairs={{0,1},{1,0},{2,3},{3,2},{4,5},{5,4},{6,7},{7,6},{8,9},{9,8},{10,11... | collective-permute-start | bytes 417800 | tf_op jit(solution)/shard_map/ppermute | solution.py:19
  101.6 8.4 %collective-permute-start.32 = (bf16[544,128]{1,0:T(8,128)(2,1)S(1)}, bf16[544,128]{1,0:T(8,128)(2,1)S(1)}, u32[]{:S(2)}, u32[]{:S(2)}) collective-permute-start(bf16[544,128]{1,0:T(8,128)(2,1)S(1)} %collective-permute-done.31.refs_5_), channel_id=1, source_target_pairs={{0,1},{1,0},{2,3},{3,2},{4,5},{5,4},{6,7},{7,6},{8,9},{9,8},{10,11... | collective-permute-start | bytes 417800 | tf_op jit(solution)/shard_map/ppermute | solution.py:19
  101.6 8.4 %collective-permute-start.30 = (bf16[544,128]{1,0:T(8,128)(2,1)S(1)}, bf16[544,128]{1,0:T(8,128)(2,1)S(1)}, u32[]{:S(2)}, u32[]{:S(2)}) collective-permute-start(bf16[544,128]{1,0:T(8,128)(2,1)S(1)} %collective-permute-done.29.refs_3_), channel_id=1, source_target_pairs={{0,1},{1,0},{2,3},{3,2},{4,5},{5,4},{6,7},{7,6},{8,9},{9,8},{10,11... | collective-permute-start | bytes 417800 | tf_op jit(solution)/shard_map/ppermute | solution.py:19
  (16 other events, 141.5 us)

commit v3 on v2

--- a/solution.py
+++ b/solution.py
@@ -11,7 +11,7 @@
 NT = (((1,), (1,)), ((), ()))
 TN = (((0,), (0,)), ((), ()))
 BIAS_ROWS = 16
-FINE_PARTS = 4
+FINE_SHARES = (8, 8, 8, 8)
 
 
 def swap(value, axis, step):
@@ -98,7 +98,7 @@
 
 def pre_kernel(count, table, ids, *refs):
     received, rest = refs[:count], refs[count:]
-    feat_slots, conv, slope, pre_grad, mine, other, total, bias = rest
+    feat_slots, conv, slope, pre_grad, other, extra, bias = rest
     bias[...] = jnp.zeros_like(bias)
     parents = received[0].shape[1]
 
@@ -110,41 +110,61 @@
         bias[...] += jnp.sum(wide.reshape(-1, 8, wide.shape[1]), axis=0)
 
     each_block(table, received, one)
-    total[...] = jnp.dot(feat_slots[...], pre_grad[...], preferred_element_type=F32)
-    pieces, width = 2 * mine.shape[0], mine.shape[2]
-    rows = total.shape[0] // pieces
     line = jnp.sum(bias[...], axis=0, keepdims=True)
-    row = lax.broadcasted_iota(jnp.int32, (BIAS_ROWS, line.shape[1]), 0)
     high = line.astype(BF16).astype(F32)
-    extra = jnp.where(row == 0, high, jnp.where(row == 1, line - high, 0.0))
-    tiles = [
-        jnp.concatenate(
-            [
-                part
-                for at in range(0, line.shape[1], width)
-                for part in (
-                    total[m * rows : (m + 1) * rows, at : at + width],
-                    extra[:, at : at + width],
-                )
-            ],
-            axis=0,
-        )
-        for m in range(pieces)
+    width = extra.shape[1]
+    extra[...] = jnp.zeros_like(extra)
+    for i, part in enumerate((high, line - high)):
+        for j in range(line.shape[1] // width):
+            at = i * (line.shape[1] // width) + j
+            extra[at : at + 1, :] = part[:, j * width : (j + 1) * width]
+    down_pieces(1 - ids[1], feat_slots, pre_grad, extra, other)
+
+
+def own_kernel(ids, feat_slots, pre_grad, extra, mine):
+    down_pieces(ids[1], feat_slots, pre_grad, extra, mine)
+
+
+def down_pieces(core, feat_slots, pre_grad, extra, out):
+    chips, _, width = out.shape
+    rows = feat_slots.shape[0] // (2 * chips)
+    lines = [
+        feat_slots[pl.ds(pl.multiple_of((2 * i + core) * rows, rows), rows), :]
+        for i in range(chips)
     ]
-    deal(tiles, ids, mine, other)
-
-
-def fine_kernel(places, pre_grad, down_weight, *refs):
+    total = jnp.dot(jnp.concatenate(lines, axis=0), pre_grad[...], preferred_element_type=F32)
+    for i in range(chips):
+        for j in range(total.shape[1] // width):
+            tile = total[i * rows : (i + 1) * rows, j * width : (j + 1) * width]
+            out[i, j * rows : (j + 1) * rows, :] = tile.astype(out.dtype)
+        out[i, out.shape[1] - BIAS_ROWS :, :] = extra[...].astype(out.dtype)
+
+
+def prepare_kernel(
+    parents, parent_slot, child_offset, down_weight, places, columns, down_wide, flat
+):
+    steps, group, rows = places.shape
+    flat[...] = jnp.zeros_like(flat)
+    for block in range(steps * group):
+        at = slice(block * rows, (block + 1) * rows)
+        place = child_offset[0:1, at] * parents + parent_slot[0:1, at]
+        places[block // group, block % group : block % group + 1, :] = place
+        flat[block : block + 1, :rows] = place
+    columns[...] = jnp.transpose(flat[...])
+    width = down_weight.shape[1]
+    for k in range(8):
+        down_wide[:, k * width : (k + 1) * width] = jnp.transpose(down_weight[k])
+
+
+def fine_kernel(first, group, parents, columns, pre_grad, down_wide, *refs):
     fine = refs[-1]
-    group = places.shape[2]
-    rows, width = fine.shape[0] // group, fine.shape[1]
-    parents = pre_grad.shape[0] // group
-    slot_grads = lax.dot_general(
-        pre_grad[...], down_weight[...], NT, preferred_element_type=F32
-    ).astype(BF16)
+    rows, width = fine.shape[0] * parents // pre_grad.shape[0], fine.shape[1]
+    grads = pre_grad[first * parents : (first + group) * parents, :]
+    slot_grads = jnp.dot(grads, down_wide[...], preferred_element_type=F32).astype(BF16)
     for i in range(group):
         slots = lax.broadcasted_iota(jnp.int32, (rows, parents * 8), 1)
-        chooser = jnp.where(slots == places[0, :, i : i + 1], 1.0, 0.0).astype(BF16)
+        place = columns[:rows, first + i : first + i + 1]
+        chooser = jnp.where(slots == place, 1.0, 0.0).astype(BF16)
         tall = jnp.concatenate(
             [
                 slot_grads[i * parents : (i + 1) * parents, k * width : (k + 1) * width]
@@ -152,7 +172,7 @@
             ],
             axis=0,
         )
-        fine[i * rows : (i + 1) * rows, :] = jnp.dot(
+        fine[(first + i) * rows : (first + i + 1) * rows, :] = jnp.dot(
             chooser, tall, preferred_element_type=F32
         ).astype(BF16)
 
@@ -163,48 +183,52 @@
     return values[0]
 
 
-def finish_kernel(scale, ids, *refs):
-    *pieces, down_grad, up_grad, bias_grad = refs
+def up_end_kernel(scale, ids, *refs):
+    *pieces, up_grad = refs
+    for i, piece in enumerate(pieces):
+        up_grad[ids[0] ^ i] = piece[...].astype(F32) * scale
+
+
+def down_end_kernel(scale, ids, *refs):
+    *pieces, down_grad, bias_grad = refs
     rows, out_width = down_grad.shape[1:]
-    up_rows, width = up_grad.shape[1:]
+    width = pieces[0].shape[1]
     for i, piece in enumerate(pieces):
         m = ids[0] ^ i
-        for at in range(0, out_width, width):
-            first = at // width * (rows + BIAS_ROWS)
-            down_grad[m, :, at : at + width] = piece[first : first + rows, :].astype(F32) * scale
-
-            @pl.when(m == 0)
-            def _():
-                pair = piece[first + rows : first + rows + 8, :].astype(F32)
-                bias_grad[:, at : at + width] = (pair[0:1] + pair[1:2]) * scale
-
-        first = out_width // width * (rows + BIAS_ROWS)
-        up_grad[m] = piece[first : first + up_rows, :].astype(F32) * scale
-
-
-def grant(mebibytes):
-    return pltpu.CompilerParams(vmem_limit_bytes=mebibytes << 20)
-
-
-def whole_spec(shape):
-    return pl.BlockSpec(shape, lambda *_: (0,) * len(shape))
-
-
-def finish(scale, ids, pieces, down_shape, up_shape):
-    outputs = [
-        jax.ShapeDtypeStruct(shape, F32) for shape in (down_shape, up_shape, (1, down_shape[2]))
-    ]
+        parts = out_width // width
+        for j in range(parts):
+            tile = piece[j * rows : (j + 1) * rows, :].astype(F32)
+            down_grad[m, :, j * width : (j + 1) * width] = tile * scale
+
+        @pl.when(m == 0)
+        def _():
+            lines = piece[parts * rows :, :].astype(F32)
+            for j in range(parts):
+                pair = lines[j : j + 1] + lines[parts + j : parts + j + 1]
+                bias_grad[:, j * width : (j + 1) * width] = pair * scale
+
+
+def finish(kernel, ids, pieces, shapes):
+    vmem = pl.BlockSpec(memory_space=pltpu.VMEM)
     return pl.pallas_call(
-        lambda *refs: finish_kernel(scale, *refs),
+        kernel,
         grid_spec=pltpu.PrefetchScalarGridSpec(
             num_scalar_prefetch=1,
             grid=(1,),
-            in_specs=[whole_spec(x.shape) for x in pieces],
-            out_specs=[whole_spec(x.shape) for x in outputs],
+            in_specs=[vmem] * len(pieces),
+            out_specs=[whole_spec(shape) for shape in shapes],
         ),
-        out_shape=outputs,
+        out_shape=[jax.ShapeDtypeStruct(shape, F32) for shape in shapes],
         compiler_params=grant(12),
     )(ids, *pieces)
+
+
+def grant(mebibytes):
+    return pltpu.CompilerParams(vmem_limit_bytes=mebibytes << 20)
+
+
+def whole_spec(shape):
+    return pl.BlockSpec(shape, lambda *_: (0,) * len(shape))
 
 
 def row_of(array, index):
@@ -228,9 +252,13 @@
     return sorted(range(1, count), key=lambda d: -bin(d).count("1"))
 
 
+def crop_order(count):
+    return [2, 3, 1] if count == 4 else far_first(count)
+
+
 def sum_crops(part):
     crops = lax.axis_size("crop")
-    parts = {d: swap(part, "crop", d) for d in far_first(crops)}
+    parts = {d: swap(part, "crop", d) for d in crop_order(crops)}
     return tree([part.astype(F32)] + [parts[d].astype(F32) for d in range(1, crops)]).astype(BF16)
 
 
@@ -307,6 +335,7 @@
     chip_peers = [(me >> 1) ^ jnp.uint32(k) for k in range(scene_count // 2)]
     whole_me = me.astype(jnp.int32)
     ids = jnp.stack([whole_me, whole_me & 1])
+    ids, chip_peers = lax.optimization_barrier((ids, chip_peers))
     order = exchange_order(scene_count)
     pre_received = exchange(pre_act[0, 0], ids, [order[:2], order[2:] + [0]])
 
@@ -322,20 +351,28 @@
     ).astype(jnp.int32)
     table = jnp.concatenate([table, counts])
 
-    places = (child_offset[0] * parents + parent_slot[0]).reshape(steps, group, rows)
-    columns = places.transpose(0, 2, 1)
-    column_spec = pl.BlockSpec((1, rows, group), lambda g, *_: (g, 0, 0))
+    ids, table, chip_peers = lax.optimization_barrier((ids, table, chip_peers))
+    lanes = -(-rows // 128) * 128
+    vmem = pl.BlockSpec(memory_space=pltpu.VMEM)
+    places, columns, down_wide = pl.pallas_call(
+        lambda *refs: prepare_kernel(parents, *refs),
+        in_specs=[vmem] * 3,
+        out_specs=[vmem] * 3,
+        out_shape=[
+            jax.ShapeDtypeStruct((steps, group, rows), jnp.int32),
+            pltpu.VMEM((lanes, blocks), jnp.int32),
+            pltpu.VMEM((out_width, 8 * width), BF16),
+        ],
+        scratch_shapes=[pltpu.VMEM((blocks, lanes), jnp.int32)],
+        compiler_params=grant(12),
+    )(parent_slot, child_offset, down_weight)
     place_spec = pl.BlockSpec((1, group, rows), lambda g, *_: (g, 0, 0))
     fine_spec = pl.BlockSpec((group * rows, width), lambda g, *_: (g, 0))
     coarse_spec = pl.BlockSpec((slots, out_width), lambda g, *_: (g, 0))
     total_rows = blocks * parents
     coarse_f32 = pltpu.VMEM((total_rows, out_width), F32)
 
-    places, columns, ids, table, chip_peers = lax.optimization_barrier(
-        (places, columns, ids, table, chip_peers)
-    )
     hbm = pl.BlockSpec(memory_space=pltpu.HBM)
-    vmem = pl.BlockSpec(memory_space=pltpu.VMEM)
     smem = pl.BlockSpec(memory_space=pltpu.SMEM)
     feat_slots, cot_slots, conv = pl.pallas_call(
         expand_kernel,
@@ -383,44 +420,60 @@
     slope, up_part = lax.optimization_barrier((slope, up_part))
     up_done = sum_crops(up_part)
 
-    pre_grad, down_mine, down_other = pl.pallas_call(
+    mine_shape, other_shape = dealt(
+        out_width // width * down_rows + BIAS_ROWS, width
+    )
+    pre_grad, down_other, extra = pl.pallas_call(
         lambda *refs: pre_kernel(scene_count, *refs),
         in_specs=[smem, smem] + [vmem] * (scene_count + 3),
         out_specs=[vmem] * 3,
-        out_shape=[pltpu.VMEM((total_rows, out_width), BF16)]
-        + dealt(out_width // width * (down_rows + BIAS_ROWS), width),
-        scratch_shapes=[pltpu.VMEM((8 * width, out_width), F32), pltpu.VMEM((8, out_width), F32)],
+        out_shape=[
+            pltpu.VMEM((total_rows, out_width), BF16),
+            other_shape,
+            pltpu.VMEM((BIAS_ROWS, width), F32),
+        ],
+        scratch_shapes=[pltpu.VMEM((8, out_width), F32)],
         compiler_params=grant(12),
     )(table, ids, *deep_received, feat_slots, conv, slope)
+    down_mine = pl.pallas_call(
+        own_kernel,
+        in_specs=[smem] + [vmem] * 3,
+        out_specs=vmem,
+        out_shape=mine_shape,
+        compiler_params=grant(12),
+    )(ids, feat_slots, pre_grad, extra)
     down_part = sum_plane(chip_peers, down_mine, down_other)
     down_done = sum_crops(down_part)
-    pieces = spread(jnp.concatenate([down_done, up_done]))
+    down_pieces = spread(down_done)
+    up_pieces = spread(up_done)
 
     fine = None
-    flat_down = down_weight.reshape(8 * width, out_width)
-    for part in range(FINE_PARTS):
-        first, count = part * steps // FINE_PARTS, steps // FINE_PARTS
-        at = lambda spec: pl.BlockSpec(
-            spec.block_shape, lambda g, first=first: (g + first,) + (0,) * (len(spec.block_shape) - 1)
-        )
+    first = 0
+    for part, share in enumerate(FINE_SHARES):
+        group = blocks * share // sum(FINE_SHARES)
+        held = [] if part == 0 else [fine]
         fine = pl.pallas_call(
-            fine_kernel,
-            grid=(count,),
-            in_specs=[at(column_spec), at(coarse_spec), whole_spec(flat_down.shape)]
-            + ([] if part == 0 else [hbm]),
-            out_specs=at(fine_spec),
-            out_shape=jax.ShapeDtypeStruct((fine_rows, width), BF16),
-            input_output_aliases={} if part == 0 else {3: 0},
+            lambda *refs, first=first, group=group: fine_kernel(first, group, parents, *refs),
+            in_specs=[vmem] * (3 + len(held)),
+            out_specs=vmem,
+            out_shape=pltpu.VMEM((fine_rows, width), BF16),
+            input_output_aliases={3: 0} if held else {},
             compiler_params=grant(12),
-        )(columns, pre_grad, flat_down, *([] if part == 0 else [fine]))
+        )(columns, pre_grad, down_wide, *held)
+        first += group
 
     scale = float(crop_count * scene_count * fine_rows) ** (-0.5)
-    down_grad, up_grad, bias_grad = finish(
-        scale,
+    (up_grad,) = finish(
+        lambda *refs: up_end_kernel(scale, *refs),
         ids,
-        pieces,
-        (scene_count, down_rows, out_width),
-        (scene_count, up_rows, width),
+        up_pieces,
+        [(scene_count, up_rows, width)],
+    )
+    down_grad, bias_grad = finish(
+        lambda *refs: down_end_kernel(scale, *refs),
+        ids,
+        down_pieces,
+        [(scene_count, down_rows, out_width), (1, out_width)],
     )
     return (
         fine[None],

time: 112 us -> 107 us (0.955)
  waiting for transfers between devices: 43.1 us -> 36.5 us
  starting transfers between devices: 35.3 us -> 39.2 us
  Pallas kernels: 31.5 us -> 28.2 us
    ppermute x35 -> x42, waiting for transfers between devices: 43.1 us -> 36.5 us  [swap(): return lax.ppermute(value, axis, [(i, i ^ step) for i in range(size)])]
    ppermute x35 -> x42, starting transfers between devices: 35.3 us -> 39.2 us  [swap(): return lax.ppermute(value, axis, [(i, i ^ step) for i in range(size)])]
    pallas_call x5 -> x8, Pallas kernels: 9.91 us -> 8.29 us  [the longest x4 3.48 us: on_device(): pl.pallas_call(lambda *refs, first=first, group=group: fine_kernel(first,...]
    unnamed x10 -> x11, local copies, waits for them, and re-layouts: 0.02 us -> 1.18 us
  transfers between devices with their start and end apart: 35 -> 42, of which waited for: 15 -> 12; matrix products, arithmetic and copies ran while one was open for 1% -> 2% of each run, Pallas kernels for 20% -> 19%
where the time goes in v3:
time: 107 us
  starting transfers between devices  39.2 us (37%)
  waiting for transfers between devices  36.5 us (34%)
  Pallas kernels  28.2 us (26%)
  local copies, waits for them, and re-layouts  1.18 us (1%)
    ppermute x42, starting transfers between devices, swap(): return lax.ppermute(value, axis, [(i, i ^ step) for i in range(size)])  39.2 us
    ppermute x42, waiting for transfers between devices, swap(): return lax.ppermute(value, axis, [(i, i ^ step) for i in range(size)])  36.5 us
    pallas_call x1, Pallas kernels, on_device(): pl.pallas_call(expand_kernel, grid=(steps,), in_specs=[place_spec, fine_s...  9.32 us
    pallas_call x3, Pallas kernels, cut(): pl.pallas_call(kernel, in_specs=[pl.BlockSpec(memory_space=pltpu.SMEM), p...  5.64 us
    pallas_call x4, Pallas kernels, on_device(): pl.pallas_call(lambda *refs, first=first, group=group: fine_kernel(first,...  3.48 us
    pallas_call x2, Pallas kernels, finish(): pl.pallas_call(kernel, grid_spec=pltpu.PrefetchScalarGridSpec(num_scalar_...  3.22 us
    pallas_call x1, Pallas kernels, on_device(): pl.pallas_call(lambda *refs: act_kernel(scene_count, *refs), in_specs=[sm...  2.94 us
  transfers between devices with their start and end apart: 42, of which 12 were waited for; matrix products, arithmetic and copies ran while one was open for 2% of the time, Pallas kernels for 19%

profile of v3, /device:TPU:0, one launch (start us, length us, event | category | flops | bytes accessed | tf_op | source)
XLA Modules:
  0.0 106.8 jit_solution(2860422827064342124)
XLA Ops:
  0.7 1.6 %shard_map.124 = (bf16[8,64,256]{2,1,0:T(8,128)(2,1)S(1)}, bf16[8,64,256]{2,1,0:T(8,128)(2,1)S(1)}) custom-call(s32[2]{0:T(128)S(1)} %pad_add_fusion.ids.refs_1_.refs_0_, bf16[8,8,64,256]{3,2,1,0:T(8,128)(2,1)} %bitcast.36), custom_call_target="tpu_custom_call" | custom-call | tf_op jit(solution)/shard_map/pallas_call | solution.py:285
  2.4 3.0 %collective-permute-start.8 = (bf16[8,64,256]{2,1,0:T(8,128)(2,1)S(1)}, bf16[8,64,256]{2,1,0:T(8,128)(2,1)S(1)}, u32[]{:S(2)}, u32[]{:S(2)}) collective-permute-start(bf16[8,64,256]{2,1,0:T(8,128)(2,1)S(1)} %get-tuple-element.72), channel_id=1, source_target_pairs={{0,2},{1,3},{2,0},{3,1},{4,6},{5,7},{6,4},{7,5},{8,10},{9,11},{10,... | collective-permute-start | bytes 786440 | tf_op jit(solution)/shard_map/ppermute | solution.py:19
  5.4 1.5 %collective-permute-start.10 = (bf16[8,64,256]{2,1,0:T(8,128)(2,1)S(1)}, bf16[8,64,256]{2,1,0:T(8,128)(2,1)S(1)}, u32[]{:S(2)}, u32[]{:S(2)}) collective-permute-start(bf16[8,64,256]{2,1,0:T(8,128)(2,1)S(1)} %get-tuple-element.74), channel_id=1, source_target_pairs={{0,4},{1,5},{2,6},{3,7},{4,0},{5,1},{6,2},{7,3},{8,12},{9,13},{10,... | collective-permute-start | bytes 786440 | tf_op jit(solution)/shard_map/ppermute | solution.py:19
  6.9 1.9 %shard_map.123 = (bf16[8,64,256]{2,1,0:T(8,128)(2,1)S(1)}, bf16[8,64,256]{2,1,0:T(8,128)(2,1)S(1)}, bf16[8,64,256]{2,1,0:T(8,128)(2,1)S(1)}, bf16[8,64,256]{2,1,...) custom-call(s32[2]{0:T(128)S(1)} %pad_add_fusion.ids.refs_1_.refs_0_, ...), custom_call_target="tpu_custom_call" | custom-call | tf_op jit(solution)/shard_map/pallas_call | solution.py:285
  9.8 2.1 %collective-permute-done.8.refs_4_ = bf16[8,64,256]{2,1,0:T(8,128)(2,1)S(1)} collective-permute-done((bf16[8,64,256]{2,1,0:T(8,128)(2,1)S(1)}, bf16[8,64,256]{2,1,0:T(8,128)(2,1)S(1)}, u32[]{:S(2)}, u32[]{:S(2)}) %collective-permute-start.8) | collective-permute-done | bytes 262176 | tf_op jit(solution)/shard_map/ppermute | solution.py:19
  11.9 3.7 %collective-permute-start.12 = (bf16[8,64,256]{2,1,0:T(8,128)(2,1)S(1)}, bf16[8,64,256]{2,1,0:T(8,128)(2,1)S(1)}, u32[]{:S(2)}, u32[]{:S(2)}) collective-permute-start(bf16[8,64,256]{2,1,0:T(8,128)(2,1)S(1)} %get-tuple-element.76), channel_id=1, source_target_pairs={{0,6},{1,7},{2,4},{3,5},{4,2},{5,3},{6,0},{7,1},{8,14},{9,15},{10,... | collective-permute-start | bytes 786440 | tf_op jit(solution)/shard_map/ppermute | solution.py:19
  16.2 9.3 %shard_map.121 = (bf16[1024,2048]{1,0:T(8,128)(2,1)S(1)}, bf16[2048,1024]{1,0:T(8,128)(2,1)S(1)}, f32[2048,256]{1,0:T(8,128)S(1)}) custom-call(s32[8,4,192]{2,1,0:T(4,128)S(1)} %get-tuple-element.57.places, bf16[6144,128]{1,0:T(8,128)(2,1)} %bitcast.39, bf16[6144,128]{1,0:T(8,128)(2,1)} %bitcast.40, bf16[8,256,128]{2,1,0:T(8,128)(2,1)S(1)} %copy-done), custom_call_target="tpu_custom_call" | custom-call | tf_op jit(solution)/shard_map/pallas_call | solution.py:377
  25.5 3.5 %collective-permute-done.11.refs_7_ = bf16[8,64,256]{2,1,0:T(8,128)(2,1)S(1)} collective-permute-done((bf16[8,64,256]{2,1,0:T(8,128)(2,1)S(1)}, bf16[8,64,256]{2,1,0:T(8,128)(2,1)S(1)}, u32[]{:S(2)}, u32[]{:S(2)}) %collective-permute-start.11) | collective-permute-done | bytes 262176 | tf_op jit(solution)/shard_map/ppermute | solution.py:19
  29.1 2.9 %shard_map.125 = (f32[2048,256]{1,0:T(8,128)S(1)}, f32[4,256,128]{2,1,0:T(8,128)S(1)}, bf16[4,256,128]{2,1,0:T(8,128)(2,1)S(1)}) custom-call(s32[72]{0:T(128)S(1)} %pad_add_fusion.1.refs_0_, s32[2]{0:T(128)S(1)} %pad_add_fusion.ids.refs_1_.refs_0_, bf16[8,64,256]{2,1,0:T(8,128)(2,1)S(1)} %get-tuple-element.70.refs_2_, ...), custom_call_target="tpu_custom_call" | custom-call | tf_op jit(solution)/shard_map/pallas_call | solution.py:408
  32.9 2.1 %shard_map.122 = (bf16[8,64,256]{2,1,0:T(8,128)(2,1)S(1)}, bf16[8,64,256]{2,1,0:T(8,128)(2,1)S(1)}, bf16[8,64,256]{2,1,0:T(8,128)(2,1)S(1)}, bf16[8,64,256]{2,1,...) custom-call(s32[2]{0:T(128)S(1)} %pad_add_fusion.ids.refs_1_.refs_0_, ...), custom_call_target="tpu_custom_call" | custom-call | tf_op jit(solution)/shard_map/pallas_call | solution.py:285
  37.3 1.5 %collective-permute-start.17 = (bf16[256,128]{1,0:T(8,128)(2,1)S(1)}, bf16[256,128]{1,0:T(8,128)(2,1)S(1)}, u32[]{:S(2)}, u32[]{:S(2)}) collective-permute-start(bf16[256,128]{1,0:T(8,128)(2,1)S(1)} %get-tuple-element.100), channel_id=1, source_target_pairs={{0,6},{1,7},{2,4},{3,5},{4,2},{5,3},{6,0},{7,1},{8,14},{9,15},{10,... | collective-permute-start | bytes 196616 | tf_op jit(solution)/shard_map/ppermute | solution.py:19
  40.0 4.3 %collective-permute-done.1.refs_4_ = bf16[8,64,256]{2,1,0:T(8,128)(2,1)S(1)} collective-permute-done((bf16[8,64,256]{2,1,0:T(8,128)(2,1)S(1)}, bf16[8,64,256]{2,1,0:T(8,128)(2,1)S(1)}, u32[]{:S(2)}, u32[]{:S(2)}) %collective-permute-start.1) | collective-permute-done | bytes 262176 | tf_op jit(solution)/shard_map/ppermute | solution.py:19
  44.3 1.5 %collective-permute-start.3 = (bf16[8,64,256]{2,1,0:T(8,128)(2,1)S(1)}, bf16[8,64,256]{2,1,0:T(8,128)(2,1)S(1)}, u32[]{:S(2)}, u32[]{:S(2)}) collective-permute-start(bf16[8,64,256]{2,1,0:T(8,128)(2,1)S(1)} %get-tuple-element.64), channel_id=1, source_target_pairs={{0,4},{1,5},{2,6},{3,7},{4,0},{5,1},{6,2},{7,3},{8,12},{9,13},{10,... | collective-permute-start | bytes 786440 | tf_op jit(solution)/shard_map/ppermute | solution.py:19
  45.9 2.2 %collective-permute-done.17 = bf16[256,128]{1,0:T(8,128)(2,1)S(1)} collective-permute-done((bf16[256,128]{1,0:T(8,128)(2,1)S(1)}, bf16[256,128]{1,0:T(8,128)(2,1)S(1)}, u32[]{:S(2)}, u32[]{:S(2)}) %collective-permute-start.17) | collective-permute-done | bytes 65568 | tf_op jit(solution)/shard_map/ppermute | solution.py:19
  49.7 2.0 %collective-permute-done.2.refs_5_ = bf16[8,64,256]{2,1,0:T(8,128)(2,1)S(1)} collective-permute-done((bf16[8,64,256]{2,1,0:T(8,128)(2,1)S(1)}, bf16[8,64,256]{2,1,0:T(8,128)(2,1)S(1)}, u32[]{:S(2)}, u32[]{:S(2)}) %collective-permute-start.2) | collective-permute-done | bytes 262176 | tf_op jit(solution)/shard_map/ppermute | solution.py:19
  51.7 13.2 %collective-permute-done.3.refs_6_ = bf16[8,64,256]{2,1,0:T(8,128)(2,1)S(1)} collective-permute-done((bf16[8,64,256]{2,1,0:T(8,128)(2,1)S(1)}, bf16[8,64,256]{2,1,0:T(8,128)(2,1)S(1)}, u32[]{:S(2)}, u32[]{:S(2)}) %collective-permute-start.3) | collective-permute-done | bytes 262176 | tf_op jit(solution)/shard_map/ppermute | solution.py:19
  64.8 4.0 %collective-permute-done.4.refs_7_ = bf16[8,64,256]{2,1,0:T(8,128)(2,1)S(1)} collective-permute-done((bf16[8,64,256]{2,1,0:T(8,128)(2,1)S(1)}, bf16[8,64,256]{2,1,0:T(8,128)(2,1)S(1)}, u32[]{:S(2)}, u32[]{:S(2)}) %collective-permute-start.4) | collective-permute-done | bytes 262176 | tf_op jit(solution)/shard_map/ppermute | solution.py:19
  68.8 2.0 %shard_map.126 = (bf16[2048,256]{1,0:T(8,128)(2,1)S(1)}, bf16[4,272,128]{2,1,0:T(8,128)(2,1)S(1)}, f32[16,128]{1,0:T(8,128)S(1)}) custom-call(s32[72]{0:T(128)S(1)} %pad_add_fusion.1.refs_0_, s32[2]{0:T(128)S(1)} %pad_add_fusion.ids.refs_1_.refs_0_, bf16[8,64,256]{2,1,0:T(8,128)(2,1)S(1)} %get-tuple-element.60.refs_2_, ...), custom_call_target="tpu_custom_call" | custom-call | tf_op jit(solution)/shard_map/pallas_call | solution.py:426
  73.9 1.4 %collective-permute-start.21 = (bf16[272,128]{1,0:T(8,128)(2,1)S(1)}, bf16[272,128]{1,0:T(8,128)(2,1)S(1)}, u32[]{:S(2)}, u32[]{:S(2)}) collective-permute-start(bf16[272,128]{1,0:T(8,128)(2,1)S(1)} %get-tuple-element.97), channel_id=1, source_target_pairs={{0,6},{1,7},{2,4},{3,5},{4,2},{5,3},{6,0},{7,1},{8,14},{9,15},{10,... | collective-permute-start | bytes 208904 | tf_op jit(solution)/shard_map/ppermute | solution.py:19
  76.5 3.6 %collective-permute-start.34 = (bf16[256,128]{1,0:T(8,128)(2,1)S(1)}, bf16[256,128]{1,0:T(8,128)(2,1)S(1)}, u32[]{:S(2)}, u32[]{:S(2)}) collective-permute-start(bf16[256,128]{1,0:T(8,128)(2,1)S(1)} %fusion.3), channel_id=1, source_target_pairs={{0,24},{8,16},{16,8},{24,0},{1,25},{9,17},{17,9},{25,1},{2,26},{10... | collective-permute-start | bytes 196616 | tf_op jit(solution)/shard_map/ppermute | solution.py:19
  80.9 3.7 %collective-permute-start.24 = (bf16[272,128]{1,0:T(8,128)(2,1)S(1)}, bf16[272,128]{1,0:T(8,128)(2,1)S(1)}, u32[]{:S(2)}, u32[]{:S(2)}) collective-permute-start(bf16[272,128]{1,0:T(8,128)(2,1)S(1)} %fusion.1), channel_id=1, source_target_pairs={{0,24},{8,16},{16,8},{24,0},{1,25},{9,17},{17,9},{25,1},{2,26},{10... | collective-permute-start | bytes 208904 | tf_op jit(solution)/shard_map/ppermute | solution.py:19
  85.4 1.8 %collective-permute-done.33 = bf16[256,128]{1,0:T(8,128)(2,1)S(1)} collective-permute-done((bf16[256,128]{1,0:T(8,128)(2,1)S(1)}, bf16[256,128]{1,0:T(8,128)(2,1)S(1)}, u32[]{:S(2)}, u32[]{:S(2)}) %collective-permute-start.33) | collective-permute-done | bytes 65568 | tf_op jit(solution)/shard_map/ppermute | solution.py:19
  103.6 1.6 %shard_map.133 = f32[8,256,128]{2,1,0:T(8,128)} custom-call(s32[2]{0:T(128)S(1)} %pad_add_fusion.ids.refs_1_.refs_0_, bf16[256,128]{1,0:T(8,128)(2,1)S(1)} %add_convert_fusion.4.refs_1_, bf16[256,128]{1,0:T(8,128)(2,1)S(1)} %collective-permute-done.35.refs_2_, bf16[256,128]{1,0:T(8,128)(2,1)S(1)} %collective-permute-done.36.refs_3_, ...), custom_call_target="tpu_custom_call" | custom-call | tf_op jit(solution)/shard_map/pallas_call | solution.py:213
  105.2 1.6 %shard_map.132 = (f32[8,128,256]{2,1,0:T(8,128)}, f32[1,256]{1,0:T(1,128)}) custom-call(s32[2]{0:T(128)S(1)} %pad_add_fusion.ids.refs_1_.refs_0_, bf16[272,128]{1,0:T(8,128)(2,1)S(1)} %add_convert_fusion.refs_1_, bf16[272,128]{1,0:T(8,128)(2,1)S(1)} %collective-permute-done.25.refs_2_, bf16[272,128]{1,0:T(8,128)(2,1)S(1)} %collective-permute-done.26.refs_3_, ...), custom_call_target="tpu_custom_call" | custom-call | tf_op jit(solution)/shard_map/pallas_call | solution.py:213
  (97 shorter events, 29.7 us)
Async XLA Ops:
  2.4 9.5 %collective-permute-start.8 = (bf16[8,64,256]{2,1,0:T(8,128)(2,1)S(1)}, bf16[8,64,256]{2,1,0:T(8,128)(2,1)S(1)}, u32[]{:S(2)}, u32[]{:S(2)}) collective-permute-start(bf16[8,64,256]{2,1,0:T(8,128)(2,1)S(1)} %get-tuple-element.72), channel_id=1, source_target_pairs={{0,2},{1,3},{2,0},{3,1},{4,6},{5,7},{6,4},{7,5},{8,10},{9,11},{10,... | collective-permute-start | bytes 786440 | tf_op jit(solution)/shard_map/ppermute | solution.py:19
  5.4 10.1 %collective-permute-start.10 = (bf16[8,64,256]{2,1,0:T(8,128)(2,1)S(1)}, bf16[8,64,256]{2,1,0:T(8,128)(2,1)S(1)}, u32[]{:S(2)}, u32[]{:S(2)}) collective-permute-start(bf16[8,64,256]{2,1,0:T(8,128)(2,1)S(1)} %get-tuple-element.74), channel_id=1, source_target_pairs={{0,4},{1,5},{2,6},{3,7},{4,0},{5,1},{6,2},{7,3},{8,12},{9,13},{10,... | collective-permute-start | bytes 786440 | tf_op jit(solution)/shard_map/ppermute | solution.py:19
  8.9 16.6 %collective-permute-start.7 = (bf16[8,64,256]{2,1,0:T(8,128)(2,1)S(1)}, bf16[8,64,256]{2,1,0:T(8,128)(2,1)S(1)}, u32[]{:S(2)}, u32[]{:S(2)}) collective-permute-start(bf16[8,64,256]{2,1,0:T(8,128)(2,1)S(1)} %get-tuple-element.71), channel_id=1, source_target_pairs={{0,1},{1,0},{2,3},{3,2},{4,5},{5,4},{6,7},{7,6},{8,9},{9,8},{10,11... | collective-permute-start | bytes 786440 | tf_op jit(solution)/shard_map/ppermute | solution.py:19
  8.9 16.6 %collective-permute-start.9 = (bf16[8,64,256]{2,1,0:T(8,128)(2,1)S(1)}, bf16[8,64,256]{2,1,0:T(8,128)(2,1)S(1)}, u32[]{:S(2)}, u32[]{:S(2)}) collective-permute-start(bf16[8,64,256]{2,1,0:T(8,128)(2,1)S(1)} %get-tuple-element.73), channel_id=1, source_target_pairs={{0,3},{1,2},{2,1},{3,0},{4,7},{5,6},{6,5},{7,4},{8,11},{9,10},{10,... | collective-permute-start | bytes 786440 | tf_op jit(solution)/shard_map/ppermute | solution.py:19
  9.6 19.5 %collective-permute-start.11 = (bf16[8,64,256]{2,1,0:T(8,128)(2,1)S(1)}, bf16[8,64,256]{2,1,0:T(8,128)(2,1)S(1)}, u32[]{:S(2)}, u32[]{:S(2)}) collective-permute-start(bf16[8,64,256]{2,1,0:T(8,128)(2,1)S(1)} %get-tuple-element.75), channel_id=1, source_target_pairs={{0,5},{1,4},{2,7},{3,6},{4,1},{5,0},{6,3},{7,2},{8,13},{9,12},{10,... | collective-permute-start | bytes 786440 | tf_op jit(solution)/shard_map/ppermute | solution.py:19
  11.9 17.2 %collective-permute-start.12 = (bf16[8,64,256]{2,1,0:T(8,128)(2,1)S(1)}, bf16[8,64,256]{2,1,0:T(8,128)(2,1)S(1)}, u32[]{:S(2)}, u32[]{:S(2)}) collective-permute-start(bf16[8,64,256]{2,1,0:T(8,128)(2,1)S(1)} %get-tuple-element.76), channel_id=1, source_target_pairs={{0,6},{1,7},{2,4},{3,5},{4,2},{5,3},{6,0},{7,1},{8,14},{9,15},{10,... | collective-permute-start | bytes 786440 | tf_op jit(solution)/shard_map/ppermute | solution.py:19
  15.5 13.5 %collective-permute-start.13 = (bf16[8,64,256]{2,1,0:T(8,128)(2,1)S(1)}, bf16[8,64,256]{2,1,0:T(8,128)(2,1)S(1)}, u32[]{:S(2)}, u32[]{:S(2)}) collective-permute-start(bf16[8,64,256]{2,1,0:T(8,128)(2,1)S(1)} %get-tuple-element.77), channel_id=1, source_target_pairs={{0,7},{1,6},{2,5},{3,4},{4,3},{5,2},{6,1},{7,0},{8,15},{9,14},{10,... | collective-permute-start | bytes 786440 | tf_op jit(solution)/shard_map/ppermute | solution.py:19
  35.1 9.2 %collective-permute-start.1 = (bf16[8,64,256]{2,1,0:T(8,128)(2,1)S(1)}, bf16[8,64,256]{2,1,0:T(8,128)(2,1)S(1)}, u32[]{:S(2)}, u32[]{:S(2)}) collective-permute-start(bf16[8,64,256]{2,1,0:T(8,128)(2,1)S(1)} %get-tuple-element.62), channel_id=1, source_target_pairs={{0,2},{1,3},{2,0},{3,1},{4,6},{5,7},{6,4},{7,5},{8,10},{9,11},{10,... | collective-permute-start | bytes 786440 | tf_op jit(solution)/shard_map/ppermute | solution.py:19
  36.4 9.4 %collective-permute-start.15 = (bf16[256,128]{1,0:T(8,128)(2,1)S(1)}, bf16[256,128]{1,0:T(8,128)(2,1)S(1)}, u32[]{:S(2)}, u32[]{:S(2)}) collective-permute-start(bf16[256,128]{1,0:T(8,128)(2,1)S(1)} %get-tuple-element.99), channel_id=1, source_target_pairs={{0,2},{1,3},{2,0},{3,1},{4,6},{5,7},{6,4},{7,5},{8,10},{9,11},{10,... | collective-permute-start | bytes 196616 | tf_op jit(solution)/shard_map/ppermute | solution.py:19
  37.3 10.8 %collective-permute-start.17 = (bf16[256,128]{1,0:T(8,128)(2,1)S(1)}, bf16[256,128]{1,0:T(8,128)(2,1)S(1)}, u32[]{:S(2)}, u32[]{:S(2)}) collective-permute-start(bf16[256,128]{1,0:T(8,128)(2,1)S(1)} %get-tuple-element.100), channel_id=1, source_target_pairs={{0,6},{1,7},{2,4},{3,5},{4,2},{5,3},{6,0},{7,1},{8,14},{9,15},{10,... | collective-permute-start | bytes 196616 | tf_op jit(solution)/shard_map/ppermute | solution.py:19
  38.8 10.5 %collective-permute-start.16 = (bf16[256,128]{1,0:T(8,128)(2,1)S(1)}, bf16[256,128]{1,0:T(8,128)(2,1)S(1)}, u32[]{:S(2)}, u32[]{:S(2)}) collective-permute-start(bf16[256,128]{1,0:T(8,128)(2,1)S(1)} %get-tuple-element.101), channel_id=1, source_target_pairs={{0,4},{1,5},{2,6},{3,7},{4,0},{5,1},{6,2},{7,3},{8,12},{9,13},{10,... | collective-permute-start | bytes 196616 | tf_op jit(solution)/shard_map/ppermute | solution.py:19
  40.0 11.7 %collective-permute-start.2 = (bf16[8,64,256]{2,1,0:T(8,128)(2,1)S(1)}, bf16[8,64,256]{2,1,0:T(8,128)(2,1)S(1)}, u32[]{:S(2)}, u32[]{:S(2)}) collective-permute-start(bf16[8,64,256]{2,1,0:T(8,128)(2,1)S(1)} %get-tuple-element.63), channel_id=1, source_target_pairs={{0,3},{1,2},{2,1},{3,0},{4,7},{5,6},{6,5},{7,4},{8,11},{9,10},{10,... | collective-permute-start | bytes 786440 | tf_op jit(solution)/shard_map/ppermute | solution.py:19
  44.3 20.5 %collective-permute-start.3 = (bf16[8,64,256]{2,1,0:T(8,128)(2,1)S(1)}, bf16[8,64,256]{2,1,0:T(8,128)(2,1)S(1)}, u32[]{:S(2)}, u32[]{:S(2)}) collective-permute-start(bf16[8,64,256]{2,1,0:T(8,128)(2,1)S(1)} %get-tuple-element.64), channel_id=1, source_target_pairs={{0,4},{1,5},{2,6},{3,7},{4,0},{5,1},{6,2},{7,3},{8,12},{9,13},{10,... | collective-permute-start | bytes 786440 | tf_op jit(solution)/shard_map/ppermute | solution.py:19
  45.8 23.0 %collective-permute-start.4 = (bf16[8,64,256]{2,1,0:T(8,128)(2,1)S(1)}, bf16[8,64,256]{2,1,0:T(8,128)(2,1)S(1)}, u32[]{:S(2)}, u32[]{:S(2)}) collective-permute-start(bf16[8,64,256]{2,1,0:T(8,128)(2,1)S(1)} %get-tuple-element.65), channel_id=1, source_target_pairs={{0,5},{1,4},{2,7},{3,6},{4,1},{5,0},{6,3},{7,2},{8,13},{9,12},{10,... | collective-permute-start | bytes 786440 | tf_op jit(solution)/shard_map/ppermute | solution.py:19
  48.1 20.8 %collective-permute-start.5 = (bf16[8,64,256]{2,1,0:T(8,128)(2,1)S(1)}, bf16[8,64,256]{2,1,0:T(8,128)(2,1)S(1)}, u32[]{:S(2)}, u32[]{:S(2)}) collective-permute-start(bf16[8,64,256]{2,1,0:T(8,128)(2,1)S(1)} %get-tuple-element.66), channel_id=1, source_target_pairs={{0,6},{1,7},{2,4},{3,5},{4,2},{5,3},{6,0},{7,1},{8,14},{9,15},{10,... | collective-permute-start | bytes 786440 | tf_op jit(solution)/shard_map/ppermute | solution.py:19
  49.2 19.6 %collective-permute-start.6 = (bf16[8,64,256]{2,1,0:T(8,128)(2,1)S(1)}, bf16[8,64,256]{2,1,0:T(8,128)(2,1)S(1)}, u32[]{:S(2)}, u32[]{:S(2)}) collective-permute-start(bf16[8,64,256]{2,1,0:T(8,128)(2,1)S(1)} %get-tuple-element.67), channel_id=1, source_target_pairs={{0,7},{1,6},{2,5},{3,4},{4,3},{5,2},{6,1},{7,0},{8,15},{9,14},{10,... | collective-permute-start | bytes 786440 | tf_op jit(solution)/shard_map/ppermute | solution.py:19
  72.9 7.2 %collective-permute-start.19 = (bf16[272,128]{1,0:T(8,128)(2,1)S(1)}, bf16[272,128]{1,0:T(8,128)(2,1)S(1)}, u32[]{:S(2)}, u32[]{:S(2)}) collective-permute-start(bf16[272,128]{1,0:T(8,128)(2,1)S(1)} %get-tuple-element.96), channel_id=1, source_target_pairs={{0,2},{1,3},{2,0},{3,1},{4,6},{5,7},{6,4},{7,5},{8,10},{9,11},{10,... | collective-permute-start | bytes 208904 | tf_op jit(solution)/shard_map/ppermute | solution.py:19
  73.9 7.0 %collective-permute-start.21 = (bf16[272,128]{1,0:T(8,128)(2,1)S(1)}, bf16[272,128]{1,0:T(8,128)(2,1)S(1)}, u32[]{:S(2)}, u32[]{:S(2)}) collective-permute-start(bf16[272,128]{1,0:T(8,128)(2,1)S(1)} %get-tuple-element.97), channel_id=1, source_target_pairs={{0,6},{1,7},{2,4},{3,5},{4,2},{5,3},{6,0},{7,1},{8,14},{9,15},{10,... | collective-permute-start | bytes 208904 | tf_op jit(solution)/shard_map/ppermute | solution.py:19
  76.5 8.1 %collective-permute-start.34 = (bf16[256,128]{1,0:T(8,128)(2,1)S(1)}, bf16[256,128]{1,0:T(8,128)(2,1)S(1)}, u32[]{:S(2)}, u32[]{:S(2)}) collective-permute-start(bf16[256,128]{1,0:T(8,128)(2,1)S(1)} %fusion.3), channel_id=1, source_target_pairs={{0,24},{8,16},{16,8},{24,0},{1,25},{9,17},{17,9},{25,1},{2,26},{10... | collective-permute-start | bytes 196616 | tf_op jit(solution)/shard_map/ppermute | solution.py:19
  80.1 7.1 %collective-permute-start.33 = (bf16[256,128]{1,0:T(8,128)(2,1)S(1)}, bf16[256,128]{1,0:T(8,128)(2,1)S(1)}, u32[]{:S(2)}, u32[]{:S(2)}) collective-permute-start(bf16[256,128]{1,0:T(8,128)(2,1)S(1)} %fusion.3), channel_id=1, source_target_pairs={{0,16},{8,24},{16,0},{24,8},{1,17},{9,25},{17,1},{25,9},{2,18},{10... | collective-permute-start | bytes 196616 | tf_op jit(solution)/shard_map/ppermute | solution.py:19
  80.1 7.1 %collective-permute-start.32 = (bf16[256,128]{1,0:T(8,128)(2,1)S(1)}, bf16[256,128]{1,0:T(8,128)(2,1)S(1)}, u32[]{:S(2)}, u32[]{:S(2)}) collective-permute-start(bf16[256,128]{1,0:T(8,128)(2,1)S(1)} %fusion.3), channel_id=1, source_target_pairs={{0,8},{8,0},{16,24},{24,16},{1,9},{9,1},{17,25},{25,17},{2,10},{10... | collective-permute-start | bytes 196616 | tf_op jit(solution)/shard_map/ppermute | solution.py:19
  80.9 8.4 %collective-permute-start.24 = (bf16[272,128]{1,0:T(8,128)(2,1)S(1)}, bf16[272,128]{1,0:T(8,128)(2,1)S(1)}, u32[]{:S(2)}, u32[]{:S(2)}) collective-permute-start(bf16[272,128]{1,0:T(8,128)(2,1)S(1)} %fusion.1), channel_id=1, source_target_pairs={{0,24},{8,16},{16,8},{24,0},{1,25},{9,17},{17,9},{25,1},{2,26},{10... | collective-permute-start | bytes 208904 | tf_op jit(solution)/shard_map/ppermute | solution.py:19
  96.1 9.1 %collective-permute-start.25 = (bf16[272,128]{1,0:T(8,128)(2,1)S(1)}, bf16[272,128]{1,0:T(8,128)(2,1)S(1)}, u32[]{:S(2)}, u32[]{:S(2)}) collective-permute-start(bf16[272,128]{1,0:T(8,128)(2,1)S(1)} %add_convert_fusion.refs_1_), channel_id=1, source_target_pairs={{0,1},{1,0},{2,3},{3,2},{4,5},{5,4},{6,7},{7,6},{8,9},{9,8},{10,11... | collective-permute-start | bytes 208904 | tf_op jit(solution)/shard_map/ppermute | solution.py:19
  97.0 8.2 %collective-permute-start.31 = (bf16[272,128]{1,0:T(8,128)(2,1)S(1)}, bf16[272,128]{1,0:T(8,128)(2,1)S(1)}, u32[]{:S(2)}, u32[]{:S(2)}) collective-permute-start(bf16[272,128]{1,0:T(8,128)(2,1)S(1)} %collective-permute-done.30.refs_7_), channel_id=1, source_target_pairs={{0,1},{1,0},{2,3},{3,2},{4,5},{5,4},{6,7},{7,6},{8,9},{9,8},{10,11... | collective-permute-start | bytes 208904 | tf_op jit(solution)/shard_map/ppermute | solution.py:19
  (23 other events, 151.3 us)

commit v4 on v3

--- a/solution.py
+++ b/solution.py
@@ -12,6 +12,7 @@
 TN = (((0,), (0,)), ((), ()))
 BIAS_ROWS = 16
 FINE_SHARES = (8, 8, 8, 8)
+HELD_BACK = [7, 5]
 
 
 def swap(value, axis, step):
@@ -51,15 +52,14 @@
     conv[at, :] = lax.dot_general(cot_slots[at, :], wide[...], NT, preferred_element_type=F32)
 
 
-def each_block(table, received, body):
-    capacity = received[0].shape[0]
-    for k, ref in enumerate(received):
-        count = table[len(received) * capacity + k]
-
-        def one(j, _, k=k, ref=ref):
+def each_block(table, count, received, body):
+    for k, ref in received.items():
+        capacity = ref.shape[0]
+
+        def one(j, _, k=k, ref=ref, capacity=capacity):
             body(ref, j, table[k * capacity + j])
 
-        lax.fori_loop(0, count, one, None)
+        lax.fori_loop(0, table[count * capacity + k], one, None)
 
 
 def deal(tiles, ids, mine, other):
@@ -85,7 +85,7 @@
         slope[at, :] = sig * (1.0 + pre * (1.0 - sig))
         act[at, :] = (pre * sig).astype(BF16)
 
-    each_block(table, received, silu)
+    each_block(table, count, dict(enumerate(received)), silu)
     total[...] = lax.dot_general(act[...], cot_slots[...], TN, preferred_element_type=F32)
     pieces, rows, width = 2 * mine.shape[0], mine.shape[1], mine.shape[2]
     per = pieces // 8
@@ -96,20 +96,29 @@
     deal(tiles, ids, mine, other)
 
 
-def pre_kernel(count, table, ids, *refs):
-    received, rest = refs[:count], refs[count:]
-    feat_slots, conv, slope, pre_grad, other, extra, bias = rest
-    bias[...] = jnp.zeros_like(bias)
-    parents = received[0].shape[1]
-
+def grad_blocks(table, count, received, conv, slope, pre_grad, bias):
     def one(ref, j, block):
+        parents = ref.shape[1]
         at = pl.ds(pl.multiple_of(block * parents, parents), parents)
         grad = ((ref[j].astype(F32) + conv[at, :]) * slope[at, :]).astype(BF16)
         pre_grad[at, :] = grad
         wide = grad.astype(F32)
         bias[...] += jnp.sum(wide.reshape(-1, 8, wide.shape[1]), axis=0)
 
-    each_block(table, received, one)
+    each_block(table, count, received, one)
+
+
+def early_kernel(count, distances, table, *refs):
+    *received, conv, slope, pre_grad, bias = refs
+    bias[...] = jnp.zeros_like(bias)
+    grad_blocks(table, count, dict(zip(distances, received)), conv, slope, pre_grad, bias)
+
+
+def pre_kernel(count, distances, table, ids, *refs):
+    received, rest = refs[: len(distances)], refs[len(distances) :]
+    feat_slots, conv, slope, _, half_bias, pre_grad, other, extra, bias = rest
+    bias[...] = half_bias[...]
+    grad_blocks(table, count, dict(zip(distances, received)), conv, slope, pre_grad, bias)
     line = jnp.sum(bias[...], axis=0, keepdims=True)
     high = line.astype(BF16).astype(F32)
     width = extra.shape[1]
@@ -301,6 +310,10 @@
         for k, part in zip(group, cut(array, ids, group)):
             out[k] = part if k == 0 else swap(part, "scene", k)
     return [out[k] for k in range(array.shape[0])]
+
+
+def held_back(count):
+    return HELD_BACK if count == 8 else [count - 1]
 
 
 def exchange_order(count):
@@ -417,24 +430,31 @@
         compiler_params=grant(12),
     )(table, ids, *pre_received, cot_slots)
     up_part = sum_plane(chip_peers, up_mine, up_other)
-    slope, up_part = lax.optimization_barrier((slope, up_part))
+    late = held_back(scene_count)
+    early = [k for k in range(scene_count) if k not in late]
+    pre_grad_shape = pltpu.VMEM((total_rows, out_width), BF16)
+    pre_half, bias_half = pl.pallas_call(
+        lambda *refs: early_kernel(scene_count, early, *refs),
+        in_specs=[smem] + [vmem] * (len(early) + 2),
+        out_specs=[vmem] * 2,
+        out_shape=[pre_grad_shape, pltpu.VMEM((8, out_width), F32)],
+        compiler_params=grant(12),
+    )(table, *[deep_received[k] for k in early], conv, slope)
+    pre_half, bias_half, up_part = lax.optimization_barrier((pre_half, bias_half, up_part))
     up_done = sum_crops(up_part)
 
     mine_shape, other_shape = dealt(
         out_width // width * down_rows + BIAS_ROWS, width
     )
     pre_grad, down_other, extra = pl.pallas_call(
-        lambda *refs: pre_kernel(scene_count, *refs),
-        in_specs=[smem, smem] + [vmem] * (scene_count + 3),
+        lambda *refs: pre_kernel(scene_count, late, *refs),
+        in_specs=[smem, smem] + [vmem] * (len(late) + 5),
         out_specs=[vmem] * 3,
-        out_shape=[
-            pltpu.VMEM((total_rows, out_width), BF16),
-            other_shape,
-            pltpu.VMEM((BIAS_ROWS, width), F32),
-        ],
+        out_shape=[pre_grad_shape, other_shape, pltpu.VMEM((BIAS_ROWS, width), F32)],
         scratch_shapes=[pltpu.VMEM((8, out_width), F32)],
-        compiler_params=grant(12),
-    )(table, ids, *deep_received, feat_slots, conv, slope)
+        input_output_aliases={len(late) + 5: 0},
+        compiler_params=grant(12),
+    )(table, ids, *[deep_received[k] for k in late], feat_slots, conv, slope, pre_half, bias_half)
     down_mine = pl.pallas_call(
         own_kernel,
         in_specs=[smem] + [vmem] * 3,

time: 107 us -> 108 us (level)
    pallas_call x1 -> x2, Pallas kernels: 2.03 us -> 2.57 us  [the longest x1 1.46 us: on_device(): pl.pallas_call(lambda *refs: pre_kernel(scene_count, late, *refs), in_spe...]
  transfers between devices with their start and end apart: 42 -> 42, of which waited for: 12 -> 14; matrix products, arithmetic and copies ran while one was open for 2% -> 2% of each run, Pallas kernels for 19% -> 20%
where the time goes in v4:
time: 108 us; the launch traced here: 107 us
  starting transfers between devices  39.6 us (37%)
  waiting for transfers between devices  36 us (33%)
  Pallas kernels  28.8 us (27%)
  local copies, waits for them, and re-layouts  1.18 us (1%)
    ppermute x42, starting transfers between devices, swap(): return lax.ppermute(value, axis, [(i, i ^ step) for i in range(size)])  39.6 us
    ppermute x42, waiting for transfers between devices, swap(): return lax.ppermute(value, axis, [(i, i ^ step) for i in range(size)])  36 us
    pallas_call x1, Pallas kernels, on_device(): pl.pallas_call(expand_kernel, grid=(steps,), in_specs=[place_spec, fine_s...  9.32 us
    pallas_call x3, Pallas kernels, cut(): pl.pallas_call(kernel, in_specs=[pl.BlockSpec(memory_space=pltpu.SMEM), p...  5.64 us
    pallas_call x4, Pallas kernels, on_device(): pl.pallas_call(lambda *refs, first=first, group=group: fine_kernel(first,...  3.47 us
    pallas_call x2, Pallas kernels, finish(): pl.pallas_call(kernel, grid_spec=pltpu.PrefetchScalarGridSpec(num_scalar_...  3.22 us
    pallas_call x1, Pallas kernels, on_device(): pl.pallas_call(lambda *refs: act_kernel(scene_count, *refs), in_specs=[sm...  2.94 us
  transfers between devices with their start and end apart: 42, of which 14 were waited for; matrix products, arithmetic and copies ran while one was open for 2% of the time, Pallas kernels for 20%

profile of v4, /device:TPU:0, one launch (start us, length us, event | category | flops | bytes accessed | tf_op | source)
XLA Modules:
  0.0 107.3 jit_solution(6817005548773835823)
XLA Ops:
  0.7 1.6 %shard_map.124 = (bf16[8,64,256]{2,1,0:T(8,128)(2,1)S(1)}, bf16[8,64,256]{2,1,0:T(8,128)(2,1)S(1)}) custom-call(s32[2]{0:T(128)S(1)} %pad_add_fusion.ids.refs_1_.refs_0_, bf16[8,8,64,256]{3,2,1,0:T(8,128)(2,1)} %bitcast.36), custom_call_target="tpu_custom_call" | custom-call | tf_op jit(solution)/shard_map/pallas_call | solution.py:294
  2.4 3.0 %collective-permute-start.3 = (bf16[8,64,256]{2,1,0:T(8,128)(2,1)S(1)}, bf16[8,64,256]{2,1,0:T(8,128)(2,1)S(1)}, u32[]{:S(2)}, u32[]{:S(2)}) collective-permute-start(bf16[8,64,256]{2,1,0:T(8,128)(2,1)S(1)} %get-tuple-element.69), channel_id=1, source_target_pairs={{0,2},{1,3},{2,0},{3,1},{4,6},{5,7},{6,4},{7,5},{8,10},{9,11},{10,... | collective-permute-start | bytes 786440 | tf_op jit(solution)/shard_map/ppermute | solution.py:20
  6.9 1.9 %shard_map.123 = (bf16[8,64,256]{2,1,0:T(8,128)(2,1)S(1)}, bf16[8,64,256]{2,1,0:T(8,128)(2,1)S(1)}, bf16[8,64,256]{2,1,0:T(8,128)(2,1)S(1)}, bf16[8,64,256]{2,1,...) custom-call(s32[2]{0:T(128)S(1)} %pad_add_fusion.ids.refs_1_.refs_0_, ...), custom_call_target="tpu_custom_call" | custom-call | tf_op jit(solution)/shard_map/pallas_call | solution.py:294
  9.8 2.1 %collective-permute-done.3.refs_4_ = bf16[8,64,256]{2,1,0:T(8,128)(2,1)S(1)} collective-permute-done((bf16[8,64,256]{2,1,0:T(8,128)(2,1)S(1)}, bf16[8,64,256]{2,1,0:T(8,128)(2,1)S(1)}, u32[]{:S(2)}, u32[]{:S(2)}) %collective-permute-start.3) | collective-permute-done | bytes 262176 | tf_op jit(solution)/shard_map/ppermute | solution.py:20
  11.9 3.7 %collective-permute-start.7 = (bf16[8,64,256]{2,1,0:T(8,128)(2,1)S(1)}, bf16[8,64,256]{2,1,0:T(8,128)(2,1)S(1)}, u32[]{:S(2)}, u32[]{:S(2)}) collective-permute-start(bf16[8,64,256]{2,1,0:T(8,128)(2,1)S(1)} %get-tuple-element.73), channel_id=1, source_target_pairs={{0,6},{1,7},{2,4},{3,5},{4,2},{5,3},{6,0},{7,1},{8,14},{9,15},{10,... | collective-permute-start | bytes 786440 | tf_op jit(solution)/shard_map/ppermute | solution.py:20
  16.2 9.3 %shard_map.121 = (bf16[1024,2048]{1,0:T(8,128)(2,1)S(1)}, bf16[2048,1024]{1,0:T(8,128)(2,1)S(1)}, f32[2048,256]{1,0:T(8,128)S(1)}) custom-call(s32[8,4,192]{2,1,0:T(4,128)S(1)} %get-tuple-element.60.places, bf16[6144,128]{1,0:T(8,128)(2,1)} %bitcast.39, bf16[6144,128]{1,0:T(8,128)(2,1)} %bitcast.40, bf16[8,256,128]{2,1,0:T(8,128)(2,1)S(1)} %copy-done), custom_call_target="tpu_custom_call" | custom-call | tf_op jit(solution)/shard_map/pallas_call | solution.py:390
  25.5 3.5 %collective-permute-done.6.refs_7_ = bf16[8,64,256]{2,1,0:T(8,128)(2,1)S(1)} collective-permute-done((bf16[8,64,256]{2,1,0:T(8,128)(2,1)S(1)}, bf16[8,64,256]{2,1,0:T(8,128)(2,1)S(1)}, u32[]{:S(2)}, u32[]{:S(2)}) %collective-permute-start.6) | collective-permute-done | bytes 262176 | tf_op jit(solution)/shard_map/ppermute | solution.py:20
  29.1 2.9 %shard_map.125 = (f32[2048,256]{1,0:T(8,128)S(1)}, f32[4,256,128]{2,1,0:T(8,128)S(1)}, bf16[4,256,128]{2,1,0:T(8,128)(2,1)S(1)}) custom-call(s32[72]{0:T(128)S(1)} %pad_add_fusion.1.refs_0_, s32[2]{0:T(128)S(1)} %pad_add_fusion.ids.refs_1_.refs_0_, bf16[8,64,256]{2,1,0:T(8,128)(2,1)S(1)} %get-tuple-element.67.refs_2_, ...), custom_call_target="tpu_custom_call" | custom-call | tf_op jit(solution)/shard_map/pallas_call | solution.py:421
  32.9 2.1 %shard_map.122 = (bf16[8,64,256]{2,1,0:T(8,128)(2,1)S(1)}, bf16[8,64,256]{2,1,0:T(8,128)(2,1)S(1)}, bf16[8,64,256]{2,1,0:T(8,128)(2,1)S(1)}, bf16[8,64,256]{2,1,...) custom-call(s32[2]{0:T(128)S(1)} %pad_add_fusion.ids.refs_1_.refs_0_, ...), custom_call_target="tpu_custom_call" | custom-call | tf_op jit(solution)/shard_map/pallas_call | solution.py:294
  36.9 1.5 %collective-permute-start.12 = (bf16[8,64,256]{2,1,0:T(8,128)(2,1)S(1)}, bf16[8,64,256]{2,1,0:T(8,128)(2,1)S(1)}, u32[]{:S(2)}, u32[]{:S(2)}) collective-permute-start(bf16[8,64,256]{2,1,0:T(8,128)(2,1)S(1)} %get-tuple-element.81), channel_id=1, source_target_pairs={{0,4},{1,5},{2,6},{3,7},{4,0},{5,1},{6,2},{7,3},{8,12},{9,13},{10,... | collective-permute-start | bytes 786440 | tf_op jit(solution)/shard_map/ppermute | solution.py:20
  40.5 3.8 %collective-permute-done.10.refs_3_ = bf16[8,64,256]{2,1,0:T(8,128)(2,1)S(1)} collective-permute-done((bf16[8,64,256]{2,1,0:T(8,128)(2,1)S(1)}, bf16[8,64,256]{2,1,0:T(8,128)(2,1)S(1)}, u32[]{:S(2)}, u32[]{:S(2)}) %collective-permute-start.10) | collective-permute-done | bytes 262176 | tf_op jit(solution)/shard_map/ppermute | solution.py:20
  45.8 3.0 %collective-permute-done.11.refs_4_ = bf16[8,64,256]{2,1,0:T(8,128)(2,1)S(1)} collective-permute-done((bf16[8,64,256]{2,1,0:T(8,128)(2,1)S(1)}, bf16[8,64,256]{2,1,0:T(8,128)(2,1)S(1)}, u32[]{:S(2)}, u32[]{:S(2)}) %collective-permute-start.11) | collective-permute-done | bytes 262176 | tf_op jit(solution)/shard_map/ppermute | solution.py:20
  48.8 1.5 %collective-permute-start.16 = (bf16[256,128]{1,0:T(8,128)(2,1)S(1)}, bf16[256,128]{1,0:T(8,128)(2,1)S(1)}, u32[]{:S(2)}, u32[]{:S(2)}) collective-permute-start(bf16[256,128]{1,0:T(8,128)(2,1)S(1)} %get-tuple-element.107), channel_id=1, source_target_pairs={{0,4},{1,5},{2,6},{3,7},{4,0},{5,1},{6,2},{7,3},{8,12},{9,13},{10,... | collective-permute-start | bytes 196616 | tf_op jit(solution)/shard_map/ppermute | solution.py:20
  51.8 4.8 %collective-permute-done.13.refs_6_ = bf16[8,64,256]{2,1,0:T(8,128)(2,1)S(1)} collective-permute-done((bf16[8,64,256]{2,1,0:T(8,128)(2,1)S(1)}, bf16[8,64,256]{2,1,0:T(8,128)(2,1)S(1)}, u32[]{:S(2)}, u32[]{:S(2)}) %collective-permute-start.13) | collective-permute-done | bytes 262176 | tf_op jit(solution)/shard_map/ppermute | solution.py:20
  57.7 1.7 %collective-permute-done.17 = bf16[256,128]{1,0:T(8,128)(2,1)S(1)} collective-permute-done((bf16[256,128]{1,0:T(8,128)(2,1)S(1)}, bf16[256,128]{1,0:T(8,128)(2,1)S(1)}, u32[]{:S(2)}, u32[]{:S(2)}) %collective-permute-start.17) | collective-permute-done | bytes 65568 | tf_op jit(solution)/shard_map/ppermute | solution.py:20
  59.4 4.5 %collective-permute-done.refs_2_ = bf16[8,64,256]{2,1,0:T(8,128)(2,1)S(1)} collective-permute-done((bf16[8,64,256]{2,1,0:T(8,128)(2,1)S(1)}, bf16[8,64,256]{2,1,0:T(8,128)(2,1)S(1)}, u32[]{:S(2)}, u32[]{:S(2)}) %collective-permute-start) | collective-permute-done | bytes 262176 | tf_op jit(solution)/shard_map/ppermute | solution.py:20
  63.9 6.2 %collective-permute-done.1.refs_3_ = bf16[8,64,256]{2,1,0:T(8,128)(2,1)S(1)} collective-permute-done((bf16[8,64,256]{2,1,0:T(8,128)(2,1)S(1)}, bf16[8,64,256]{2,1,0:T(8,128)(2,1)S(1)}, u32[]{:S(2)}, u32[]{:S(2)}) %collective-permute-start.1) | collective-permute-done | bytes 262176 | tf_op jit(solution)/shard_map/ppermute | solution.py:20
  76.8 3.6 %collective-permute-start.34 = (bf16[256,128]{1,0:T(8,128)(2,1)S(1)}, bf16[256,128]{1,0:T(8,128)(2,1)S(1)}, u32[]{:S(2)}, u32[]{:S(2)}) collective-permute-start(bf16[256,128]{1,0:T(8,128)(2,1)S(1)} %fusion.3), channel_id=1, source_target_pairs={{0,24},{8,16},{16,8},{24,0},{1,25},{9,17},{17,9},{25,1},{2,26},{10... | collective-permute-start | bytes 196616 | tf_op jit(solution)/shard_map/ppermute | solution.py:20
  81.2 3.7 %collective-permute-start.24 = (bf16[272,128]{1,0:T(8,128)(2,1)S(1)}, bf16[272,128]{1,0:T(8,128)(2,1)S(1)}, u32[]{:S(2)}, u32[]{:S(2)}) collective-permute-start(bf16[272,128]{1,0:T(8,128)(2,1)S(1)} %fusion.1), channel_id=1, source_target_pairs={{0,24},{8,16},{16,8},{24,0},{1,25},{9,17},{17,9},{25,1},{2,26},{10... | collective-permute-start | bytes 208904 | tf_op jit(solution)/shard_map/ppermute | solution.py:20
  85.7 3.0 %collective-permute-done.33 = bf16[256,128]{1,0:T(8,128)(2,1)S(1)} collective-permute-done((bf16[256,128]{1,0:T(8,128)(2,1)S(1)}, bf16[256,128]{1,0:T(8,128)(2,1)S(1)}, u32[]{:S(2)}, u32[]{:S(2)}) %collective-permute-start.33) | collective-permute-done | bytes 65568 | tf_op jit(solution)/shard_map/ppermute | solution.py:20
  89.1 3.1 %collective-permute-start.36 = (bf16[256,128]{1,0:T(8,128)(2,1)S(1)}, bf16[256,128]{1,0:T(8,128)(2,1)S(1)}, u32[]{:S(2)}, u32[]{:S(2)}) collective-permute-start(bf16[256,128]{1,0:T(8,128)(2,1)S(1)} %add_convert_fusion.4.refs_1_), channel_id=1, source_target_pairs={{0,2},{1,3},{2,0},{3,1},{4,6},{5,7},{6,4},{7,5},{8,10},{9,11},{10,... | collective-permute-start | bytes 196616 | tf_op jit(solution)/shard_map/ppermute | solution.py:20
  94.0 1.9 %collective-permute-start.26 = (bf16[272,128]{1,0:T(8,128)(2,1)S(1)}, bf16[272,128]{1,0:T(8,128)(2,1)S(1)}, u32[]{:S(2)}, u32[]{:S(2)}) collective-permute-start(bf16[272,128]{1,0:T(8,128)(2,1)S(1)} %add_convert_fusion.refs_1_), channel_id=1, source_target_pairs={{0,2},{1,3},{2,0},{3,1},{4,6},{5,7},{6,4},{7,5},{8,10},{9,11},{10,... | collective-permute-start | bytes 208904 | tf_op jit(solution)/shard_map/ppermute | solution.py:20
  104.0 1.6 %shard_map.134 = f32[8,256,128]{2,1,0:T(8,128)} custom-call(s32[2]{0:T(128)S(1)} %pad_add_fusion.ids.refs_1_.refs_0_, bf16[256,128]{1,0:T(8,128)(2,1)S(1)} %add_convert_fusion.4.refs_1_, bf16[256,128]{1,0:T(8,128)(2,1)S(1)} %collective-permute-done.35.refs_2_, bf16[256,128]{1,0:T(8,128)(2,1)S(1)} %collective-permute-done.36.refs_3_, ...), custom_call_target="tpu_custom_call" | custom-call | tf_op jit(solution)/shard_map/pallas_call | solution.py:222
  105.7 1.6 %shard_map.133 = (f32[8,128,256]{2,1,0:T(8,128)}, f32[1,256]{1,0:T(1,128)}) custom-call(s32[2]{0:T(128)S(1)} %pad_add_fusion.ids.refs_1_.refs_0_, bf16[272,128]{1,0:T(8,128)(2,1)S(1)} %add_convert_fusion.refs_1_, bf16[272,128]{1,0:T(8,128)(2,1)S(1)} %collective-permute-done.25.refs_2_, bf16[272,128]{1,0:T(8,128)(2,1)S(1)} %collective-permute-done.26.refs_3_, ...), custom_call_target="tpu_custom_call" | custom-call | tf_op jit(solution)/shard_map/pallas_call | solution.py:222
  (98 shorter events, 30.6 us)
Async XLA Ops:
  2.4 9.5 %collective-permute-start.3 = (bf16[8,64,256]{2,1,0:T(8,128)(2,1)S(1)}, bf16[8,64,256]{2,1,0:T(8,128)(2,1)S(1)}, u32[]{:S(2)}, u32[]{:S(2)}) collective-permute-start(bf16[8,64,256]{2,1,0:T(8,128)(2,1)S(1)} %get-tuple-element.69), channel_id=1, source_target_pairs={{0,2},{1,3},{2,0},{3,1},{4,6},{5,7},{6,4},{7,5},{8,10},{9,11},{10,... | collective-permute-start | bytes 786440 | tf_op jit(solution)/shard_map/ppermute | solution.py:20
  5.4 10.1 %collective-permute-start.5 = (bf16[8,64,256]{2,1,0:T(8,128)(2,1)S(1)}, bf16[8,64,256]{2,1,0:T(8,128)(2,1)S(1)}, u32[]{:S(2)}, u32[]{:S(2)}) collective-permute-start(bf16[8,64,256]{2,1,0:T(8,128)(2,1)S(1)} %get-tuple-element.71), channel_id=1, source_target_pairs={{0,4},{1,5},{2,6},{3,7},{4,0},{5,1},{6,2},{7,3},{8,12},{9,13},{10,... | collective-permute-start | bytes 786440 | tf_op jit(solution)/shard_map/ppermute | solution.py:20
  8.9 16.6 %collective-permute-start.2 = (bf16[8,64,256]{2,1,0:T(8,128)(2,1)S(1)}, bf16[8,64,256]{2,1,0:T(8,128)(2,1)S(1)}, u32[]{:S(2)}, u32[]{:S(2)}) collective-permute-start(bf16[8,64,256]{2,1,0:T(8,128)(2,1)S(1)} %get-tuple-element.68), channel_id=1, source_target_pairs={{0,1},{1,0},{2,3},{3,2},{4,5},{5,4},{6,7},{7,6},{8,9},{9,8},{10,11... | collective-permute-start | bytes 786440 | tf_op jit(solution)/shard_map/ppermute | solution.py:20
  8.9 16.6 %collective-permute-start.4 = (bf16[8,64,256]{2,1,0:T(8,128)(2,1)S(1)}, bf16[8,64,256]{2,1,0:T(8,128)(2,1)S(1)}, u32[]{:S(2)}, u32[]{:S(2)}) collective-permute-start(bf16[8,64,256]{2,1,0:T(8,128)(2,1)S(1)} %get-tuple-element.70), channel_id=1, source_target_pairs={{0,3},{1,2},{2,1},{3,0},{4,7},{5,6},{6,5},{7,4},{8,11},{9,10},{10,... | collective-permute-start | bytes 786440 | tf_op jit(solution)/shard_map/ppermute | solution.py:20
  9.6 19.5 %collective-permute-start.6 = (bf16[8,64,256]{2,1,0:T(8,128)(2,1)S(1)}, bf16[8,64,256]{2,1,0:T(8,128)(2,1)S(1)}, u32[]{:S(2)}, u32[]{:S(2)}) collective-permute-start(bf16[8,64,256]{2,1,0:T(8,128)(2,1)S(1)} %get-tuple-element.72), channel_id=1, source_target_pairs={{0,5},{1,4},{2,7},{3,6},{4,1},{5,0},{6,3},{7,2},{8,13},{9,12},{10,... | collective-permute-start | bytes 786440 | tf_op jit(solution)/shard_map/ppermute | solution.py:20
  11.9 17.2 %collective-permute-start.7 = (bf16[8,64,256]{2,1,0:T(8,128)(2,1)S(1)}, bf16[8,64,256]{2,1,0:T(8,128)(2,1)S(1)}, u32[]{:S(2)}, u32[]{:S(2)}) collective-permute-start(bf16[8,64,256]{2,1,0:T(8,128)(2,1)S(1)} %get-tuple-element.73), channel_id=1, source_target_pairs={{0,6},{1,7},{2,4},{3,5},{4,2},{5,3},{6,0},{7,1},{8,14},{9,15},{10,... | collective-permute-start | bytes 786440 | tf_op jit(solution)/shard_map/ppermute | solution.py:20
  15.5 13.5 %collective-permute-start.8 = (bf16[8,64,256]{2,1,0:T(8,128)(2,1)S(1)}, bf16[8,64,256]{2,1,0:T(8,128)(2,1)S(1)}, u32[]{:S(2)}, u32[]{:S(2)}) collective-permute-start(bf16[8,64,256]{2,1,0:T(8,128)(2,1)S(1)} %get-tuple-element.74), channel_id=1, source_target_pairs={{0,7},{1,6},{2,5},{3,4},{4,3},{5,2},{6,1},{7,0},{8,15},{9,14},{10,... | collective-permute-start | bytes 786440 | tf_op jit(solution)/shard_map/ppermute | solution.py:20
  35.1 9.2 %collective-permute-start.10 = (bf16[8,64,256]{2,1,0:T(8,128)(2,1)S(1)}, bf16[8,64,256]{2,1,0:T(8,128)(2,1)S(1)}, u32[]{:S(2)}, u32[]{:S(2)}) collective-permute-start(bf16[8,64,256]{2,1,0:T(8,128)(2,1)S(1)} %get-tuple-element.79), channel_id=1, source_target_pairs={{0,2},{1,3},{2,0},{3,1},{4,6},{5,7},{6,4},{7,5},{8,10},{9,11},{10,... | collective-permute-start | bytes 786440 | tf_op jit(solution)/shard_map/ppermute | solution.py:20
  36.4 12.5 %collective-permute-start.11 = (bf16[8,64,256]{2,1,0:T(8,128)(2,1)S(1)}, bf16[8,64,256]{2,1,0:T(8,128)(2,1)S(1)}, u32[]{:S(2)}, u32[]{:S(2)}) collective-permute-start(bf16[8,64,256]{2,1,0:T(8,128)(2,1)S(1)} %get-tuple-element.80), channel_id=1, source_target_pairs={{0,3},{1,2},{2,1},{3,0},{4,7},{5,6},{6,5},{7,4},{8,11},{9,10},{10,... | collective-permute-start | bytes 786440 | tf_op jit(solution)/shard_map/ppermute | solution.py:20
  36.9 13.5 %collective-permute-start.12 = (bf16[8,64,256]{2,1,0:T(8,128)(2,1)S(1)}, bf16[8,64,256]{2,1,0:T(8,128)(2,1)S(1)}, u32[]{:S(2)}, u32[]{:S(2)}) collective-permute-start(bf16[8,64,256]{2,1,0:T(8,128)(2,1)S(1)} %get-tuple-element.81), channel_id=1, source_target_pairs={{0,4},{1,5},{2,6},{3,7},{4,0},{5,1},{6,2},{7,3},{8,12},{9,13},{10,... | collective-permute-start | bytes 786440 | tf_op jit(solution)/shard_map/ppermute | solution.py:20
  38.4 18.1 %collective-permute-start.13 = (bf16[8,64,256]{2,1,0:T(8,128)(2,1)S(1)}, bf16[8,64,256]{2,1,0:T(8,128)(2,1)S(1)}, u32[]{:S(2)}, u32[]{:S(2)}) collective-permute-start(bf16[8,64,256]{2,1,0:T(8,128)(2,1)S(1)} %get-tuple-element.82), channel_id=1, source_target_pairs={{0,6},{1,7},{2,4},{3,5},{4,2},{5,3},{6,0},{7,1},{8,14},{9,15},{10,... | collective-permute-start | bytes 786440 | tf_op jit(solution)/shard_map/ppermute | solution.py:20
  39.7 18.0 %collective-permute-start.15 = (bf16[256,128]{1,0:T(8,128)(2,1)S(1)}, bf16[256,128]{1,0:T(8,128)(2,1)S(1)}, u32[]{:S(2)}, u32[]{:S(2)}) collective-permute-start(bf16[256,128]{1,0:T(8,128)(2,1)S(1)} %get-tuple-element.105), channel_id=1, source_target_pairs={{0,2},{1,3},{2,0},{3,1},{4,6},{5,7},{6,4},{7,5},{8,10},{9,11},{10,... | collective-permute-start | bytes 196616 | tf_op jit(solution)/shard_map/ppermute | solution.py:20
  44.3 15.0 %collective-permute-start.17 = (bf16[256,128]{1,0:T(8,128)(2,1)S(1)}, bf16[256,128]{1,0:T(8,128)(2,1)S(1)}, u32[]{:S(2)}, u32[]{:S(2)}) collective-permute-start(bf16[256,128]{1,0:T(8,128)(2,1)S(1)} %get-tuple-element.106), channel_id=1, source_target_pairs={{0,6},{1,7},{2,4},{3,5},{4,2},{5,3},{6,0},{7,1},{8,14},{9,15},{10,... | collective-permute-start | bytes 196616 | tf_op jit(solution)/shard_map/ppermute | solution.py:20
  48.8 10.5 %collective-permute-start.16 = (bf16[256,128]{1,0:T(8,128)(2,1)S(1)}, bf16[256,128]{1,0:T(8,128)(2,1)S(1)}, u32[]{:S(2)}, u32[]{:S(2)}) collective-permute-start(bf16[256,128]{1,0:T(8,128)(2,1)S(1)} %get-tuple-element.107), channel_id=1, source_target_pairs={{0,4},{1,5},{2,6},{3,7},{4,0},{5,1},{6,2},{7,3},{8,12},{9,13},{10,... | collective-permute-start | bytes 196616 | tf_op jit(solution)/shard_map/ppermute | solution.py:20
  50.4 13.5 %collective-permute-start = (bf16[8,64,256]{2,1,0:T(8,128)(2,1)S(1)}, bf16[8,64,256]{2,1,0:T(8,128)(2,1)S(1)}, u32[]{:S(2)}, u32[]{:S(2)}) collective-permute-start(bf16[8,64,256]{2,1,0:T(8,128)(2,1)S(1)} %get-tuple-element.63), channel_id=1, source_target_pairs={{0,7},{1,6},{2,5},{3,4},{4,3},{5,2},{6,1},{7,0},{8,15},{9,14},{10,... | collective-permute-start | bytes 786440 | tf_op jit(solution)/shard_map/ppermute | solution.py:20
  56.5 13.5 %collective-permute-start.1 = (bf16[8,64,256]{2,1,0:T(8,128)(2,1)S(1)}, bf16[8,64,256]{2,1,0:T(8,128)(2,1)S(1)}, u32[]{:S(2)}, u32[]{:S(2)}) collective-permute-start(bf16[8,64,256]{2,1,0:T(8,128)(2,1)S(1)} %get-tuple-element.64), channel_id=1, source_target_pairs={{0,5},{1,4},{2,7},{3,6},{4,1},{5,0},{6,3},{7,2},{8,13},{9,12},{10,... | collective-permute-start | bytes 786440 | tf_op jit(solution)/shard_map/ppermute | solution.py:20
  73.8 7.3 %collective-permute-start.21 = (bf16[272,128]{1,0:T(8,128)(2,1)S(1)}, bf16[272,128]{1,0:T(8,128)(2,1)S(1)}, u32[]{:S(2)}, u32[]{:S(2)}) collective-permute-start(bf16[272,128]{1,0:T(8,128)(2,1)S(1)} %get-tuple-element.103), channel_id=1, source_target_pairs={{0,6},{1,7},{2,4},{3,5},{4,2},{5,3},{6,0},{7,1},{8,14},{9,15},{10,... | collective-permute-start | bytes 208904 | tf_op jit(solution)/shard_map/ppermute | solution.py:20
  76.8 8.1 %collective-permute-start.34 = (bf16[256,128]{1,0:T(8,128)(2,1)S(1)}, bf16[256,128]{1,0:T(8,128)(2,1)S(1)}, u32[]{:S(2)}, u32[]{:S(2)}) collective-permute-start(bf16[256,128]{1,0:T(8,128)(2,1)S(1)} %fusion.3), channel_id=1, source_target_pairs={{0,24},{8,16},{16,8},{24,0},{1,25},{9,17},{17,9},{25,1},{2,26},{10... | collective-permute-start | bytes 196616 | tf_op jit(solution)/shard_map/ppermute | solution.py:20
  80.4 8.3 %collective-permute-start.33 = (bf16[256,128]{1,0:T(8,128)(2,1)S(1)}, bf16[256,128]{1,0:T(8,128)(2,1)S(1)}, u32[]{:S(2)}, u32[]{:S(2)}) collective-permute-start(bf16[256,128]{1,0:T(8,128)(2,1)S(1)} %fusion.3), channel_id=1, source_target_pairs={{0,16},{8,24},{16,0},{24,8},{1,17},{9,25},{17,1},{25,9},{2,18},{10... | collective-permute-start | bytes 196616 | tf_op jit(solution)/shard_map/ppermute | solution.py:20
  80.4 8.3 %collective-permute-start.32 = (bf16[256,128]{1,0:T(8,128)(2,1)S(1)}, bf16[256,128]{1,0:T(8,128)(2,1)S(1)}, u32[]{:S(2)}, u32[]{:S(2)}) collective-permute-start(bf16[256,128]{1,0:T(8,128)(2,1)S(1)} %fusion.3), channel_id=1, source_target_pairs={{0,8},{8,0},{16,24},{24,16},{1,9},{9,1},{17,25},{25,17},{2,10},{10... | collective-permute-start | bytes 196616 | tf_op jit(solution)/shard_map/ppermute | solution.py:20
  81.2 7.9 %collective-permute-start.24 = (bf16[272,128]{1,0:T(8,128)(2,1)S(1)}, bf16[272,128]{1,0:T(8,128)(2,1)S(1)}, u32[]{:S(2)}, u32[]{:S(2)}) collective-permute-start(bf16[272,128]{1,0:T(8,128)(2,1)S(1)} %fusion.1), channel_id=1, source_target_pairs={{0,24},{8,16},{16,8},{24,0},{1,25},{9,17},{17,9},{25,1},{2,26},{10... | collective-permute-start | bytes 208904 | tf_op jit(solution)/shard_map/ppermute | solution.py:20
  84.9 7.4 %collective-permute-start.23 = (bf16[272,128]{1,0:T(8,128)(2,1)S(1)}, bf16[272,128]{1,0:T(8,128)(2,1)S(1)}, u32[]{:S(2)}, u32[]{:S(2)}) collective-permute-start(bf16[272,128]{1,0:T(8,128)(2,1)S(1)} %fusion.1), channel_id=1, source_target_pairs={{0,16},{8,24},{16,0},{24,8},{1,17},{9,25},{17,1},{25,9},{2,18},{10... | collective-permute-start | bytes 208904 | tf_op jit(solution)/shard_map/ppermute | solution.py:20
  84.9 7.4 %collective-permute-start.22 = (bf16[272,128]{1,0:T(8,128)(2,1)S(1)}, bf16[272,128]{1,0:T(8,128)(2,1)S(1)}, u32[]{:S(2)}, u32[]{:S(2)}) collective-permute-start(bf16[272,128]{1,0:T(8,128)(2,1)S(1)} %fusion.1), channel_id=1, source_target_pairs={{0,8},{8,0},{16,24},{24,16},{1,9},{9,1},{17,25},{25,17},{2,10},{10... | collective-permute-start | bytes 208904 | tf_op jit(solution)/shard_map/ppermute | solution.py:20
  97.2 8.5 %collective-permute-start.25 = (bf16[272,128]{1,0:T(8,128)(2,1)S(1)}, bf16[272,128]{1,0:T(8,128)(2,1)S(1)}, u32[]{:S(2)}, u32[]{:S(2)}) collective-permute-start(bf16[272,128]{1,0:T(8,128)(2,1)S(1)} %add_convert_fusion.refs_1_), channel_id=1, source_target_pairs={{0,1},{1,0},{2,3},{3,2},{4,5},{5,4},{6,7},{7,6},{8,9},{9,8},{10,11... | collective-permute-start | bytes 208904 | tf_op jit(solution)/shard_map/ppermute | solution.py:20
  (23 other events, 154.2 us)

commit v5 on v4

--- a/solution.py
+++ b/solution.py
@@ -10,8 +10,8 @@
 BF16 = jnp.bfloat16
 NT = (((1,), (1,)), ((), ()))
 TN = (((0,), (0,)), ((), ()))
-BIAS_ROWS = 16
-FINE_SHARES = (8, 8, 8, 8)
+BIAS_ROWS = 8
+FINE_SHARES = (16, 12, 4)
 HELD_BACK = [7, 5]
 
 
@@ -62,19 +62,24 @@
         lax.fori_loop(0, table[count * capacity + k], one, None)
 
 
-def deal(tiles, ids, mine, other):
+def scene_here():
+    return lax.axis_index("scene").astype(jnp.int32)
+
+
+def deal(tiles, mine, other):
+    core = scene_here() % 2
     for m, tile in enumerate(tiles):
 
-        @pl.when(ids[1] == m % 2)
+        @pl.when(core == m % 2)
         def _():
             mine[m // 2] = tile
 
-        @pl.when(ids[1] != m % 2)
+        @pl.when(core != m % 2)
         def _():
             other[m // 2] = tile.astype(BF16)
 
 
-def act_kernel(count, table, ids, *refs):
+def act_kernel(count, table, *refs):
     received, (cot_slots, slope, mine, other, act, total) = refs[:count], refs[count:]
     parents = received[0].shape[1]
 
@@ -93,7 +98,7 @@
         total[(m % per) * rows : (m % per + 1) * rows, m // per * width : (m // per + 1) * width]
         for m in range(pieces)
     ]
-    deal(tiles, ids, mine, other)
+    deal(tiles, mine, other)
 
 
 def grad_blocks(table, count, received, conv, slope, pre_grad, bias):
@@ -114,7 +119,7 @@
     grad_blocks(table, count, dict(zip(distances, received)), conv, slope, pre_grad, bias)
 
 
-def pre_kernel(count, distances, table, ids, *refs):
+def pre_kernel(count, distances, table, *refs):
     received, rest = refs[: len(distances)], refs[len(distances) :]
     feat_slots, conv, slope, _, half_bias, pre_grad, other, extra, bias = rest
     bias[...] = half_bias[...]
@@ -127,11 +132,11 @@
         for j in range(line.shape[1] // width):
             at = i * (line.shape[1] // width) + j
             extra[at : at + 1, :] = part[:, j * width : (j + 1) * width]
-    down_pieces(1 - ids[1], feat_slots, pre_grad, extra, other)
-
-
-def own_kernel(ids, feat_slots, pre_grad, extra, mine):
-    down_pieces(ids[1], feat_slots, pre_grad, extra, mine)
+    down_pieces(1 - scene_here() % 2, feat_slots, pre_grad, extra, other)
+
+
+def own_kernel(feat_slots, pre_grad, extra, mine):
+    down_pieces(scene_here() % 2, feat_slots, pre_grad, extra, mine)
 
 
 def down_pieces(core, feat_slots, pre_grad, extra, out):
@@ -192,18 +197,20 @@
     return values[0]
 
 
-def up_end_kernel(scale, ids, *refs):
+def up_end_kernel(scale, *refs):
     *pieces, up_grad = refs
+    me = scene_here()
     for i, piece in enumerate(pieces):
-        up_grad[ids[0] ^ i] = piece[...].astype(F32) * scale
-
-
-def down_end_kernel(scale, ids, *refs):
+        up_grad[me ^ i] = piece[...].astype(F32) * scale
+
+
+def down_end_kernel(scale, *refs):
+    me = scene_here()
     *pieces, down_grad, bias_grad = refs
     rows, out_width = down_grad.shape[1:]
     width = pieces[0].shape[1]
     for i, piece in enumerate(pieces):
-        m = ids[0] ^ i
+        m = me ^ i
         parts = out_width // width
         for j in range(parts):
             tile = piece[j * rows : (j + 1) * rows, :].astype(F32)
@@ -217,19 +224,16 @@
                 bias_grad[:, j * width : (j + 1) * width] = pair * scale
 
 
-def finish(kernel, ids, pieces, shapes):
+def finish(kernel, pieces, shapes):
     vmem = pl.BlockSpec(memory_space=pltpu.VMEM)
     return pl.pallas_call(
         kernel,
-        grid_spec=pltpu.PrefetchScalarGridSpec(
-            num_scalar_prefetch=1,
-            grid=(1,),
-            in_specs=[vmem] * len(pieces),
-            out_specs=[whole_spec(shape) for shape in shapes],
-        ),
+        grid=(1,),
+        in_specs=[vmem] * len(pieces),
+        out_specs=[whole_spec(shape) for shape in shapes],
         out_shape=[jax.ShapeDtypeStruct(shape, F32) for shape in shapes],
         compiler_params=grant(12),
-    )(ids, *pieces)
+    )(*pieces)
 
 
 def grant(mebibytes):
@@ -279,11 +283,12 @@
     return [x for d in range(chips) for x in (even[d], odd[d])]
 
 
-def cut(array, ids, distances):
-    def kernel(ids, array, *refs):
+def cut(array, distances):
+    def kernel(array, *refs):
         *parts, sems = refs
+        me = scene_here()
         copies = [
-            pltpu.make_async_copy(array.at[ids[0] ^ k], part, sems.at[i])
+            pltpu.make_async_copy(array.at[me ^ k], part, sems.at[i])
             for i, (k, part) in enumerate(zip(distances, parts))
         ]
         for copy in copies:
@@ -293,21 +298,18 @@
 
     return pl.pallas_call(
         kernel,
-        in_specs=[
-            pl.BlockSpec(memory_space=pltpu.SMEM),
-            pl.BlockSpec(memory_space=pltpu.HBM),
-        ],
+        in_specs=[pl.BlockSpec(memory_space=pltpu.HBM)],
         out_specs=[pl.BlockSpec(memory_space=pltpu.VMEM)] * len(distances),
         out_shape=[pltpu.VMEM(array.shape[1:], array.dtype)] * len(distances),
         scratch_shapes=[pltpu.SemaphoreType.DMA((len(distances),))],
         compiler_params=grant(12),
-    )(ids, pltpu.with_memory_space_constraint(array, pltpu.HBM))
-
-
-def exchange(array, ids, groups):
+    )(pltpu.with_memory_space_constraint(array, pltpu.HBM))
+
+
+def exchange(array, groups):
     out = {}
     for group in groups:
-        for k, part in zip(group, cut(array, ids, group)):
+        for k, part in zip(group, cut(array, group)):
             out[k] = part if k == 0 else swap(part, "scene", k)
     return [out[k] for k in range(array.shape[0])]
 
@@ -347,10 +349,11 @@
     me = lax.axis_index("scene").astype(jnp.uint32)
     chip_peers = [(me >> 1) ^ jnp.uint32(k) for k in range(scene_count // 2)]
     whole_me = me.astype(jnp.int32)
-    ids = jnp.stack([whole_me, whole_me & 1])
-    ids, chip_peers = lax.optimization_barrier((ids, chip_peers))
+    pre_whole, whole_me, chip_peers = lax.optimization_barrier(
+        (pre_act[0, 0], whole_me, chip_peers)
+    )
     order = exchange_order(scene_count)
-    pre_received = exchange(pre_act[0, 0], ids, [order[:2], order[2:] + [0]])
+    pre_received = exchange(pre_whole, [order[:2], order[2:] + [0]])
 
     earlier = jnp.arange(blocks)[None, :] < jnp.arange(blocks)[:, None]
     same_owner = owners[:, None] == owners[None, :]
@@ -364,7 +367,7 @@
     ).astype(jnp.int32)
     table = jnp.concatenate([table, counts])
 
-    ids, table, chip_peers = lax.optimization_barrier((ids, table, chip_peers))
+    table, chip_peers = lax.optimization_barrier((table, chip_peers))
     lanes = -(-rows // 128) * 128
     vmem = pl.BlockSpec(memory_space=pltpu.VMEM)
     places, columns, down_wide = pl.pallas_call(
@@ -409,7 +412,7 @@
         up_weight,
     )
     deep_whole, conv = lax.optimization_barrier((deep_grad[0, 0], conv))
-    deep_received = exchange(deep_whole, ids, [order + [0]])
+    deep_received = exchange(deep_whole, [order + [0]])
 
     chips = scene_count // 2
 
@@ -420,7 +423,7 @@
     up_rows, down_rows = 8 * out_width // scene_count, 8 * width // scene_count
     slope, up_mine, up_other = pl.pallas_call(
         lambda *refs: act_kernel(scene_count, *refs),
-        in_specs=[smem, smem] + [vmem] * (scene_count + 1),
+        in_specs=[smem] + [vmem] * (scene_count + 1),
         out_specs=[vmem] * 3,
         out_shape=[coarse_f32] + dealt(up_rows, width),
         scratch_shapes=[
@@ -428,7 +431,7 @@
             pltpu.VMEM((out_width, 8 * width), F32),
         ],
         compiler_params=grant(12),
-    )(table, ids, *pre_received, cot_slots)
+    )(table, *pre_received, cot_slots)
     up_part = sum_plane(chip_peers, up_mine, up_other)
     late = held_back(scene_count)
     early = [k for k in range(scene_count) if k not in late]
@@ -448,20 +451,28 @@
     )
     pre_grad, down_other, extra = pl.pallas_call(
         lambda *refs: pre_kernel(scene_count, late, *refs),
-        in_specs=[smem, smem] + [vmem] * (len(late) + 5),
+        in_specs=[smem] + [vmem] * (len(late) + 5),
         out_specs=[vmem] * 3,
         out_shape=[pre_grad_shape, other_shape, pltpu.VMEM((BIAS_ROWS, width), F32)],
         scratch_shapes=[pltpu.VMEM((8, out_width), F32)],
-        input_output_aliases={len(late) + 5: 0},
-        compiler_params=grant(12),
-    )(table, ids, *[deep_received[k] for k in late], feat_slots, conv, slope, pre_half, bias_half)
+        input_output_aliases={len(late) + 4: 0},
+        compiler_params=grant(12),
+    )(
+        table,
+        *[deep_received[k] for k in late],
+        feat_slots,
+        conv,
+        slope,
+        pre_half,
+        bias_half,
+    )
     down_mine = pl.pallas_call(
         own_kernel,
-        in_specs=[smem] + [vmem] * 3,
+        in_specs=[vmem] * 3,
         out_specs=vmem,
         out_shape=mine_shape,
         compiler_params=grant(12),
-    )(ids, feat_slots, pre_grad, extra)
+    )(feat_slots, pre_grad, extra)
     down_part = sum_plane(chip_peers, down_mine, down_other)
     down_done = sum_crops(down_part)
     down_pieces = spread(down_done)
@@ -485,13 +496,11 @@
     scale = float(crop_count * scene_count * fine_rows) ** (-0.5)
     (up_grad,) = finish(
         lambda *refs: up_end_kernel(scale, *refs),
-        ids,
         up_pieces,
         [(scene_count, up_rows, width)],
     )
     down_grad, bias_grad = finish(
         lambda *refs: down_end_kernel(scale, *refs),
-        ids,
         down_pieces,
         [(scene_count, down_rows, out_width), (1, out_width)],
     )

time: 108 us -> 106 us (0.981)
  Pallas kernels: 28.8 us -> 25.4 us
  waiting for transfers between devices: 36 us -> 38 us
    pallas_call x6, Pallas kernels: 10.1 us -> 6.96 us  [the longest x3 4.1 us: cut(): pl.pallas_call(kernel, in_specs=[pl.BlockSpec(memory_space=pltpu.HBM)], o...]
    ppermute x42, waiting for transfers between devices: 36 us -> 38 us  [swap(): return lax.ppermute(value, axis, [(i, i ^ step) for i in range(size)])]
    pallas_call x4 -> x3, Pallas kernels: 3.47 us -> 3.35 us  [on_device(): pl.pallas_call(lambda *refs, first=first, group=group: fine_kernel(first,...]
  transfers between devices with their start and end apart: 42 -> 42, of which waited for: 14 -> 15; matrix products, arithmetic and copies ran while one was open for 2% -> 2% of each run, Pallas kernels for 20% -> 18%
where the time goes in v5:
time: 106 us; the launch traced here: 105 us
  starting transfers between devices  39.1 us (37%)
  waiting for transfers between devices  38 us (36%)
  Pallas kernels  25.4 us (24%)
  local copies, waits for them, and re-layouts  1.17 us (1%)
    ppermute x42, starting transfers between devices, swap(): return lax.ppermute(value, axis, [(i, i ^ step) for i in range(size)])  39.1 us
    ppermute x42, waiting for transfers between devices, swap(): return lax.ppermute(value, axis, [(i, i ^ step) for i in range(size)])  38 us
    pallas_call x1, Pallas kernels, on_device(): pl.pallas_call(expand_kernel, grid=(steps,), in_specs=[place_spec, fine_s...  9.32 us
    pallas_call x3, Pallas kernels, cut(): pl.pallas_call(kernel, in_specs=[pl.BlockSpec(memory_space=pltpu.HBM)], o...  4.1 us
    pallas_call x3, Pallas kernels, on_device(): pl.pallas_call(lambda *refs, first=first, group=group: fine_kernel(first,...  3.35 us
    pallas_call x1, Pallas kernels, on_device(): pl.pallas_call(lambda *refs: act_kernel(scene_count, *refs), in_specs=[sm...  2.88 us
    pallas_call x2, Pallas kernels, finish(): pl.pallas_call(kernel, grid=(1,), in_specs=[vmem] * len(pieces), out_spec...  2.14 us
  transfers between devices with their start and end apart: 42, of which 15 were waited for; matrix products, arithmetic and copies ran while one was open for 2% of the time, Pallas kernels for 18%

profile of v5, /device:TPU:0, one launch (start us, length us, event | category | flops | bytes accessed | tf_op | source)
XLA Modules:
  0.0 105.3 jit_solution(16575251171405237976)
XLA Ops:
  1.8 3.0 %collective-permute-start.3 = (bf16[8,64,256]{2,1,0:T(8,128)(2,1)S(1)}, bf16[8,64,256]{2,1,0:T(8,128)(2,1)S(1)}, u32[]{:S(2)}, u32[]{:S(2)}) collective-permute-start(bf16[8,64,256]{2,1,0:T(8,128)(2,1)S(1)} %get-tuple-element.69), channel_id=1, source_target_pairs={{0,2},{1,3},{2,0},{3,1},{4,6},{5,7},{6,4},{7,5},{8,10},{9,11},{10,... | collective-permute-start | bytes 786440 | tf_op jit(solution)/shard_map/ppermute | solution.py:20
  4.9 1.5 %collective-permute-start.5 = (bf16[8,64,256]{2,1,0:T(8,128)(2,1)S(1)}, bf16[8,64,256]{2,1,0:T(8,128)(2,1)S(1)}, u32[]{:S(2)}, u32[]{:S(2)}) collective-permute-start(bf16[8,64,256]{2,1,0:T(8,128)(2,1)S(1)} %get-tuple-element.71), channel_id=1, source_target_pairs={{0,4},{1,5},{2,6},{3,7},{4,0},{5,1},{6,2},{7,3},{8,12},{9,13},{10,... | collective-permute-start | bytes 786440 | tf_op jit(solution)/shard_map/ppermute | solution.py:20
  8.7 2.9 %collective-permute-done.3.refs_3_ = bf16[8,64,256]{2,1,0:T(8,128)(2,1)S(1)} collective-permute-done((bf16[8,64,256]{2,1,0:T(8,128)(2,1)S(1)}, bf16[8,64,256]{2,1,0:T(8,128)(2,1)S(1)}, u32[]{:S(2)}, u32[]{:S(2)}) %collective-permute-start.3) | collective-permute-done | bytes 262176 | tf_op jit(solution)/shard_map/ppermute | solution.py:20
  11.6 3.4 %collective-permute-start.7 = (bf16[8,64,256]{2,1,0:T(8,128)(2,1)S(1)}, bf16[8,64,256]{2,1,0:T(8,128)(2,1)S(1)}, u32[]{:S(2)}, u32[]{:S(2)}) collective-permute-start(bf16[8,64,256]{2,1,0:T(8,128)(2,1)S(1)} %get-tuple-element.73), channel_id=1, source_target_pairs={{0,6},{1,7},{2,4},{3,5},{4,2},{5,3},{6,0},{7,1},{8,14},{9,15},{10,... | collective-permute-start | bytes 786440 | tf_op jit(solution)/shard_map/ppermute | solution.py:20
  15.6 9.3 %shard_map.121 = (bf16[1024,2048]{1,0:T(8,128)(2,1)S(1)}, bf16[2048,1024]{1,0:T(8,128)(2,1)S(1)}, f32[2048,256]{1,0:T(8,128)S(1)}) custom-call(s32[8,4,192]{2,1,0:T(4,128)S(1)} %get-tuple-element.59.places, bf16[6144,128]{1,0:T(8,128)(2,1)} %bitcast.37, bf16[6144,128]{1,0:T(8,128)(2,1)} %bitcast.38, bf16[8,256,128]{2,1,0:T(8,128)(2,1)S(1)} %copy-done), custom_call_target="tpu_custom_call" | custom-call | tf_op jit(solution)/shard_map/pallas_call | solution.py:393
  25.0 3.5 %collective-permute-done.6.refs_6_ = bf16[8,64,256]{2,1,0:T(8,128)(2,1)S(1)} collective-permute-done((bf16[8,64,256]{2,1,0:T(8,128)(2,1)S(1)}, bf16[8,64,256]{2,1,0:T(8,128)(2,1)S(1)}, u32[]{:S(2)}, u32[]{:S(2)}) %collective-permute-start.6) | collective-permute-done | bytes 262176 | tf_op jit(solution)/shard_map/ppermute | solution.py:20
  28.5 2.9 %shard_map.125 = (f32[2048,256]{1,0:T(8,128)S(1)}, f32[4,256,128]{2,1,0:T(8,128)S(1)}, bf16[4,256,128]{2,1,0:T(8,128)(2,1)S(1)}) custom-call(s32[72]{0:T(128)S(1)} %pad_add_fusion.refs_0_, bf16[8,64,256]{2,1,0:T(8,128)(2,1)S(1)} %get-tuple-element.67.refs_1_, bf16[8,64,256]{2,1,0:T(8,128)(2,1)S(1)} %collective-permute-done.2.refs_2_, ...), custom_call_target="tpu_custom_call" | custom-call | tf_op jit(solution)/shard_map/pallas_call | solution.py:424
  32.3 1.6 %shard_map.122 = (bf16[8,64,256]{2,1,0:T(8,128)(2,1)S(1)}, bf16[8,64,256]{2,1,0:T(8,128)(2,1)S(1)}, bf16[8,64,256]{2,1,0:T(8,128)(2,1)S(1)}, bf16[8,64,256]{2,1,...) custom-call(bf16[8,8,64,256]{3,2,1,0:T(8,128)(2,1)} %bitcast.36), custom_call_target="tpu_custom_call" | custom-call | tf_op jit(solution)/shard_map/pallas_call | solution.py:299
  35.8 1.5 %collective-permute-start.12 = (bf16[8,64,256]{2,1,0:T(8,128)(2,1)S(1)}, bf16[8,64,256]{2,1,0:T(8,128)(2,1)S(1)}, u32[]{:S(2)}, u32[]{:S(2)}) collective-permute-start(bf16[8,64,256]{2,1,0:T(8,128)(2,1)S(1)} %get-tuple-element.81), channel_id=1, source_target_pairs={{0,4},{1,5},{2,6},{3,7},{4,0},{5,1},{6,2},{7,3},{8,12},{9,13},{10,... | collective-permute-start | bytes 786440 | tf_op jit(solution)/shard_map/ppermute | solution.py:20
  39.4 3.8 %collective-permute-done.10.refs_3_ = bf16[8,64,256]{2,1,0:T(8,128)(2,1)S(1)} collective-permute-done((bf16[8,64,256]{2,1,0:T(8,128)(2,1)S(1)}, bf16[8,64,256]{2,1,0:T(8,128)(2,1)S(1)}, u32[]{:S(2)}, u32[]{:S(2)}) %collective-permute-start.10) | collective-permute-done | bytes 262176 | tf_op jit(solution)/shard_map/ppermute | solution.py:20
  43.2 1.5 %collective-permute-start.17 = (bf16[256,128]{1,0:T(8,128)(2,1)S(1)}, bf16[256,128]{1,0:T(8,128)(2,1)S(1)}, u32[]{:S(2)}, u32[]{:S(2)}) collective-permute-start(bf16[256,128]{1,0:T(8,128)(2,1)S(1)} %get-tuple-element.106), channel_id=1, source_target_pairs={{0,6},{1,7},{2,4},{3,5},{4,2},{5,3},{6,0},{7,1},{8,14},{9,15},{10,... | collective-permute-start | bytes 196616 | tf_op jit(solution)/shard_map/ppermute | solution.py:20
  44.7 3.1 %collective-permute-done.11.refs_4_ = bf16[8,64,256]{2,1,0:T(8,128)(2,1)S(1)} collective-permute-done((bf16[8,64,256]{2,1,0:T(8,128)(2,1)S(1)}, bf16[8,64,256]{2,1,0:T(8,128)(2,1)S(1)}, u32[]{:S(2)}, u32[]{:S(2)}) %collective-permute-start.11) | collective-permute-done | bytes 262176 | tf_op jit(solution)/shard_map/ppermute | solution.py:20
  47.7 1.5 %collective-permute-start.16 = (bf16[256,128]{1,0:T(8,128)(2,1)S(1)}, bf16[256,128]{1,0:T(8,128)(2,1)S(1)}, u32[]{:S(2)}, u32[]{:S(2)}) collective-permute-start(bf16[256,128]{1,0:T(8,128)(2,1)S(1)} %get-tuple-element.107), channel_id=1, source_target_pairs={{0,4},{1,5},{2,6},{3,7},{4,0},{5,1},{6,2},{7,3},{8,12},{9,13},{10,... | collective-permute-start | bytes 196616 | tf_op jit(solution)/shard_map/ppermute | solution.py:20
  50.6 4.8 %collective-permute-done.13.refs_6_ = bf16[8,64,256]{2,1,0:T(8,128)(2,1)S(1)} collective-permute-done((bf16[8,64,256]{2,1,0:T(8,128)(2,1)S(1)}, bf16[8,64,256]{2,1,0:T(8,128)(2,1)S(1)}, u32[]{:S(2)}, u32[]{:S(2)}) %collective-permute-start.13) | collective-permute-done | bytes 262176 | tf_op jit(solution)/shard_map/ppermute | solution.py:20
  56.5 1.7 %collective-permute-done.17 = bf16[256,128]{1,0:T(8,128)(2,1)S(1)} collective-permute-done((bf16[256,128]{1,0:T(8,128)(2,1)S(1)}, bf16[256,128]{1,0:T(8,128)(2,1)S(1)}, u32[]{:S(2)}, u32[]{:S(2)}) %collective-permute-start.17) | collective-permute-done | bytes 65568 | tf_op jit(solution)/shard_map/ppermute | solution.py:20
  58.3 4.5 %collective-permute-done.refs_1_ = bf16[8,64,256]{2,1,0:T(8,128)(2,1)S(1)} collective-permute-done((bf16[8,64,256]{2,1,0:T(8,128)(2,1)S(1)}, bf16[8,64,256]{2,1,0:T(8,128)(2,1)S(1)}, u32[]{:S(2)}, u32[]{:S(2)}) %collective-permute-start) | collective-permute-done | bytes 262176 | tf_op jit(solution)/shard_map/ppermute | solution.py:20
  62.8 6.2 %collective-permute-done.1.refs_2_ = bf16[8,64,256]{2,1,0:T(8,128)(2,1)S(1)} collective-permute-done((bf16[8,64,256]{2,1,0:T(8,128)(2,1)S(1)}, bf16[8,64,256]{2,1,0:T(8,128)(2,1)S(1)}, u32[]{:S(2)}, u32[]{:S(2)}) %collective-permute-start.1) | collective-permute-done | bytes 262176 | tf_op jit(solution)/shard_map/ppermute | solution.py:20
  72.6 1.5 %collective-permute-start.21 = (bf16[264,128]{1,0:T(8,128)(2,1)S(1)}, bf16[264,128]{1,0:T(8,128)(2,1)S(1)}, u32[]{:S(2)}, u32[]{:S(2)}) collective-permute-start(bf16[264,128]{1,0:T(8,128)(2,1)S(1)} %get-tuple-element.103), channel_id=1, source_target_pairs={{0,6},{1,7},{2,4},{3,5},{4,2},{5,3},{6,0},{7,1},{8,14},{9,15},{10,... | collective-permute-start | bytes 202760 | tf_op jit(solution)/shard_map/ppermute | solution.py:20
  74.1 1.5 %collective-permute-start.20 = (bf16[264,128]{1,0:T(8,128)(2,1)S(1)}, bf16[264,128]{1,0:T(8,128)(2,1)S(1)}, u32[]{:S(2)}, u32[]{:S(2)}) collective-permute-start(bf16[264,128]{1,0:T(8,128)(2,1)S(1)} %get-tuple-element.104), channel_id=1, source_target_pairs={{0,4},{1,5},{2,6},{3,7},{4,0},{5,1},{6,2},{7,3},{8,12},{9,13},{10,... | collective-permute-start | bytes 202760 | tf_op jit(solution)/shard_map/ppermute | solution.py:20
  75.6 3.6 %collective-permute-start.34 = (bf16[256,128]{1,0:T(8,128)(2,1)S(1)}, bf16[256,128]{1,0:T(8,128)(2,1)S(1)}, u32[]{:S(2)}, u32[]{:S(2)}) collective-permute-start(bf16[256,128]{1,0:T(8,128)(2,1)S(1)} %fusion.3), channel_id=1, source_target_pairs={{0,24},{8,16},{16,8},{24,0},{1,25},{9,17},{17,9},{25,1},{2,26},{10... | collective-permute-start | bytes 196616 | tf_op jit(solution)/shard_map/ppermute | solution.py:20
  80.1 3.7 %collective-permute-start.24 = (bf16[264,128]{1,0:T(8,128)(2,1)S(1)}, bf16[264,128]{1,0:T(8,128)(2,1)S(1)}, u32[]{:S(2)}, u32[]{:S(2)}) collective-permute-start(bf16[264,128]{1,0:T(8,128)(2,1)S(1)} %fusion.1), channel_id=1, source_target_pairs={{0,24},{8,16},{16,8},{24,0},{1,25},{9,17},{17,9},{25,1},{2,26},{10... | collective-permute-start | bytes 202760 | tf_op jit(solution)/shard_map/ppermute | solution.py:20
  84.5 3.2 %collective-permute-done.33 = bf16[256,128]{1,0:T(8,128)(2,1)S(1)} collective-permute-done((bf16[256,128]{1,0:T(8,128)(2,1)S(1)}, bf16[256,128]{1,0:T(8,128)(2,1)S(1)}, u32[]{:S(2)}, u32[]{:S(2)}) %collective-permute-start.33) | collective-permute-done | bytes 65568 | tf_op jit(solution)/shard_map/ppermute | solution.py:20
  88.7 2.6 %collective-permute-start.36 = (bf16[256,128]{1,0:T(8,128)(2,1)S(1)}, bf16[256,128]{1,0:T(8,128)(2,1)S(1)}, u32[]{:S(2)}, u32[]{:S(2)}) collective-permute-start(bf16[256,128]{1,0:T(8,128)(2,1)S(1)} %add_convert_fusion.4.refs_0_), channel_id=1, source_target_pairs={{0,2},{1,3},{2,0},{3,1},{4,6},{5,7},{6,4},{7,5},{8,10},{9,11},{10,... | collective-permute-start | bytes 196616 | tf_op jit(solution)/shard_map/ppermute | solution.py:20
  98.7 1.5 %shard_map.128.refs_3_ = bf16[6144,128]{1,0:T(8,128)(2,1)S(1)} custom-call(s32[256,32]{1,0:T(8,128)S(1)} %get-tuple-element.52.refs_0_, bf16[2048,256]{1,0:T(8,128)(2,1)S(1)} %get-tuple-element.93.refs_1_.pre_grad, bf16[256,1024]{1,0:T(8,128)(2,1)S(1)} %get-tuple-element.94.refs_2_), custom_call_target="tpu_custom_call" | custom-call | tf_op jit(solution)/shard_map/pallas_call | solution.py:486
  (96 shorter events, 30.3 us)
Async XLA Ops:
  1.8 9.7 %collective-permute-start.3 = (bf16[8,64,256]{2,1,0:T(8,128)(2,1)S(1)}, bf16[8,64,256]{2,1,0:T(8,128)(2,1)S(1)}, u32[]{:S(2)}, u32[]{:S(2)}) collective-permute-start(bf16[8,64,256]{2,1,0:T(8,128)(2,1)S(1)} %get-tuple-element.69), channel_id=1, source_target_pairs={{0,2},{1,3},{2,0},{3,1},{4,6},{5,7},{6,4},{7,5},{8,10},{9,11},{10,... | collective-permute-start | bytes 786440 | tf_op jit(solution)/shard_map/ppermute | solution.py:20
  4.9 10.1 %collective-permute-start.5 = (bf16[8,64,256]{2,1,0:T(8,128)(2,1)S(1)}, bf16[8,64,256]{2,1,0:T(8,128)(2,1)S(1)}, u32[]{:S(2)}, u32[]{:S(2)}) collective-permute-start(bf16[8,64,256]{2,1,0:T(8,128)(2,1)S(1)} %get-tuple-element.71), channel_id=1, source_target_pairs={{0,4},{1,5},{2,6},{3,7},{4,0},{5,1},{6,2},{7,3},{8,12},{9,13},{10,... | collective-permute-start | bytes 786440 | tf_op jit(solution)/shard_map/ppermute | solution.py:20
  7.8 17.2 %collective-permute-start.2 = (bf16[8,64,256]{2,1,0:T(8,128)(2,1)S(1)}, bf16[8,64,256]{2,1,0:T(8,128)(2,1)S(1)}, u32[]{:S(2)}, u32[]{:S(2)}) collective-permute-start(bf16[8,64,256]{2,1,0:T(8,128)(2,1)S(1)} %get-tuple-element.68), channel_id=1, source_target_pairs={{0,1},{1,0},{2,3},{3,2},{4,5},{5,4},{6,7},{7,6},{8,9},{9,8},{10,11... | collective-permute-start | bytes 786440 | tf_op jit(solution)/shard_map/ppermute | solution.py:20
  7.9 17.1 %collective-permute-start.4 = (bf16[8,64,256]{2,1,0:T(8,128)(2,1)S(1)}, bf16[8,64,256]{2,1,0:T(8,128)(2,1)S(1)}, u32[]{:S(2)}, u32[]{:S(2)}) collective-permute-start(bf16[8,64,256]{2,1,0:T(8,128)(2,1)S(1)} %get-tuple-element.70), channel_id=1, source_target_pairs={{0,3},{1,2},{2,1},{3,0},{4,7},{5,6},{6,5},{7,4},{8,11},{9,10},{10,... | collective-permute-start | bytes 786440 | tf_op jit(solution)/shard_map/ppermute | solution.py:20
  8.5 20.0 %collective-permute-start.6 = (bf16[8,64,256]{2,1,0:T(8,128)(2,1)S(1)}, bf16[8,64,256]{2,1,0:T(8,128)(2,1)S(1)}, u32[]{:S(2)}, u32[]{:S(2)}) collective-permute-start(bf16[8,64,256]{2,1,0:T(8,128)(2,1)S(1)} %get-tuple-element.72), channel_id=1, source_target_pairs={{0,5},{1,4},{2,7},{3,6},{4,1},{5,0},{6,3},{7,2},{8,13},{9,12},{10,... | collective-permute-start | bytes 786440 | tf_op jit(solution)/shard_map/ppermute | solution.py:20
  11.6 17.0 %collective-permute-start.7 = (bf16[8,64,256]{2,1,0:T(8,128)(2,1)S(1)}, bf16[8,64,256]{2,1,0:T(8,128)(2,1)S(1)}, u32[]{:S(2)}, u32[]{:S(2)}) collective-permute-start(bf16[8,64,256]{2,1,0:T(8,128)(2,1)S(1)} %get-tuple-element.73), channel_id=1, source_target_pairs={{0,6},{1,7},{2,4},{3,5},{4,2},{5,3},{6,0},{7,1},{8,14},{9,15},{10,... | collective-permute-start | bytes 786440 | tf_op jit(solution)/shard_map/ppermute | solution.py:20
  15.0 13.5 %collective-permute-start.8 = (bf16[8,64,256]{2,1,0:T(8,128)(2,1)S(1)}, bf16[8,64,256]{2,1,0:T(8,128)(2,1)S(1)}, u32[]{:S(2)}, u32[]{:S(2)}) collective-permute-start(bf16[8,64,256]{2,1,0:T(8,128)(2,1)S(1)} %get-tuple-element.74), channel_id=1, source_target_pairs={{0,7},{1,6},{2,5},{3,4},{4,3},{5,2},{6,1},{7,0},{8,15},{9,14},{10,... | collective-permute-start | bytes 786440 | tf_op jit(solution)/shard_map/ppermute | solution.py:20
  33.9 9.2 %collective-permute-start.10 = (bf16[8,64,256]{2,1,0:T(8,128)(2,1)S(1)}, bf16[8,64,256]{2,1,0:T(8,128)(2,1)S(1)}, u32[]{:S(2)}, u32[]{:S(2)}) collective-permute-start(bf16[8,64,256]{2,1,0:T(8,128)(2,1)S(1)} %get-tuple-element.79), channel_id=1, source_target_pairs={{0,2},{1,3},{2,0},{3,1},{4,6},{5,7},{6,4},{7,5},{8,10},{9,11},{10,... | collective-permute-start | bytes 786440 | tf_op jit(solution)/shard_map/ppermute | solution.py:20
  35.2 12.5 %collective-permute-start.11 = (bf16[8,64,256]{2,1,0:T(8,128)(2,1)S(1)}, bf16[8,64,256]{2,1,0:T(8,128)(2,1)S(1)}, u32[]{:S(2)}, u32[]{:S(2)}) collective-permute-start(bf16[8,64,256]{2,1,0:T(8,128)(2,1)S(1)} %get-tuple-element.80), channel_id=1, source_target_pairs={{0,3},{1,2},{2,1},{3,0},{4,7},{5,6},{6,5},{7,4},{8,11},{9,10},{10,... | collective-permute-start | bytes 786440 | tf_op jit(solution)/shard_map/ppermute | solution.py:20
  35.8 13.5 %collective-permute-start.12 = (bf16[8,64,256]{2,1,0:T(8,128)(2,1)S(1)}, bf16[8,64,256]{2,1,0:T(8,128)(2,1)S(1)}, u32[]{:S(2)}, u32[]{:S(2)}) collective-permute-start(bf16[8,64,256]{2,1,0:T(8,128)(2,1)S(1)} %get-tuple-element.81), channel_id=1, source_target_pairs={{0,4},{1,5},{2,6},{3,7},{4,0},{5,1},{6,2},{7,3},{8,12},{9,13},{10,... | collective-permute-start | bytes 786440 | tf_op jit(solution)/shard_map/ppermute | solution.py:20
  37.3 18.1 %collective-permute-start.13 = (bf16[8,64,256]{2,1,0:T(8,128)(2,1)S(1)}, bf16[8,64,256]{2,1,0:T(8,128)(2,1)S(1)}, u32[]{:S(2)}, u32[]{:S(2)}) collective-permute-start(bf16[8,64,256]{2,1,0:T(8,128)(2,1)S(1)} %get-tuple-element.82), channel_id=1, source_target_pairs={{0,6},{1,7},{2,4},{3,5},{4,2},{5,3},{6,0},{7,1},{8,14},{9,15},{10,... | collective-permute-start | bytes 786440 | tf_op jit(solution)/shard_map/ppermute | solution.py:20
  38.5 18.0 %collective-permute-start.15 = (bf16[256,128]{1,0:T(8,128)(2,1)S(1)}, bf16[256,128]{1,0:T(8,128)(2,1)S(1)}, u32[]{:S(2)}, u32[]{:S(2)}) collective-permute-start(bf16[256,128]{1,0:T(8,128)(2,1)S(1)} %get-tuple-element.105), channel_id=1, source_target_pairs={{0,2},{1,3},{2,0},{3,1},{4,6},{5,7},{6,4},{7,5},{8,10},{9,11},{10,... | collective-permute-start | bytes 196616 | tf_op jit(solution)/shard_map/ppermute | solution.py:20
  43.2 15.0 %collective-permute-start.17 = (bf16[256,128]{1,0:T(8,128)(2,1)S(1)}, bf16[256,128]{1,0:T(8,128)(2,1)S(1)}, u32[]{:S(2)}, u32[]{:S(2)}) collective-permute-start(bf16[256,128]{1,0:T(8,128)(2,1)S(1)} %get-tuple-element.106), channel_id=1, source_target_pairs={{0,6},{1,7},{2,4},{3,5},{4,2},{5,3},{6,0},{7,1},{8,14},{9,15},{10,... | collective-permute-start | bytes 196616 | tf_op jit(solution)/shard_map/ppermute | solution.py:20
  47.7 10.5 %collective-permute-start.16 = (bf16[256,128]{1,0:T(8,128)(2,1)S(1)}, bf16[256,128]{1,0:T(8,128)(2,1)S(1)}, u32[]{:S(2)}, u32[]{:S(2)}) collective-permute-start(bf16[256,128]{1,0:T(8,128)(2,1)S(1)} %get-tuple-element.107), channel_id=1, source_target_pairs={{0,4},{1,5},{2,6},{3,7},{4,0},{5,1},{6,2},{7,3},{8,12},{9,13},{10,... | collective-permute-start | bytes 196616 | tf_op jit(solution)/shard_map/ppermute | solution.py:20
  49.2 13.5 %collective-permute-start = (bf16[8,64,256]{2,1,0:T(8,128)(2,1)S(1)}, bf16[8,64,256]{2,1,0:T(8,128)(2,1)S(1)}, u32[]{:S(2)}, u32[]{:S(2)}) collective-permute-start(bf16[8,64,256]{2,1,0:T(8,128)(2,1)S(1)} %get-tuple-element.62), channel_id=1, source_target_pairs={{0,7},{1,6},{2,5},{3,4},{4,3},{5,2},{6,1},{7,0},{8,15},{9,14},{10,... | collective-permute-start | bytes 786440 | tf_op jit(solution)/shard_map/ppermute | solution.py:20
  55.4 13.5 %collective-permute-start.1 = (bf16[8,64,256]{2,1,0:T(8,128)(2,1)S(1)}, bf16[8,64,256]{2,1,0:T(8,128)(2,1)S(1)}, u32[]{:S(2)}, u32[]{:S(2)}) collective-permute-start(bf16[8,64,256]{2,1,0:T(8,128)(2,1)S(1)} %get-tuple-element.63), channel_id=1, source_target_pairs={{0,5},{1,4},{2,7},{3,6},{4,1},{5,0},{6,3},{7,2},{8,13},{9,12},{10,... | collective-permute-start | bytes 786440 | tf_op jit(solution)/shard_map/ppermute | solution.py:20
  72.6 7.4 %collective-permute-start.21 = (bf16[264,128]{1,0:T(8,128)(2,1)S(1)}, bf16[264,128]{1,0:T(8,128)(2,1)S(1)}, u32[]{:S(2)}, u32[]{:S(2)}) collective-permute-start(bf16[264,128]{1,0:T(8,128)(2,1)S(1)} %get-tuple-element.103), channel_id=1, source_target_pairs={{0,6},{1,7},{2,4},{3,5},{4,2},{5,3},{6,0},{7,1},{8,14},{9,15},{10,... | collective-permute-start | bytes 202760 | tf_op jit(solution)/shard_map/ppermute | solution.py:20
  75.6 8.1 %collective-permute-start.34 = (bf16[256,128]{1,0:T(8,128)(2,1)S(1)}, bf16[256,128]{1,0:T(8,128)(2,1)S(1)}, u32[]{:S(2)}, u32[]{:S(2)}) collective-permute-start(bf16[256,128]{1,0:T(8,128)(2,1)S(1)} %fusion.3), channel_id=1, source_target_pairs={{0,24},{8,16},{16,8},{24,0},{1,25},{9,17},{17,9},{25,1},{2,26},{10... | collective-permute-start | bytes 196616 | tf_op jit(solution)/shard_map/ppermute | solution.py:20
  79.2 8.5 %collective-permute-start.33 = (bf16[256,128]{1,0:T(8,128)(2,1)S(1)}, bf16[256,128]{1,0:T(8,128)(2,1)S(1)}, u32[]{:S(2)}, u32[]{:S(2)}) collective-permute-start(bf16[256,128]{1,0:T(8,128)(2,1)S(1)} %fusion.3), channel_id=1, source_target_pairs={{0,16},{8,24},{16,0},{24,8},{1,17},{9,25},{17,1},{25,9},{2,18},{10... | collective-permute-start | bytes 196616 | tf_op jit(solution)/shard_map/ppermute | solution.py:20
  79.2 8.5 %collective-permute-start.32 = (bf16[256,128]{1,0:T(8,128)(2,1)S(1)}, bf16[256,128]{1,0:T(8,128)(2,1)S(1)}, u32[]{:S(2)}, u32[]{:S(2)}) collective-permute-start(bf16[256,128]{1,0:T(8,128)(2,1)S(1)} %fusion.3), channel_id=1, source_target_pairs={{0,8},{8,0},{16,24},{24,16},{1,9},{9,1},{17,25},{25,17},{2,10},{10... | collective-permute-start | bytes 196616 | tf_op jit(solution)/shard_map/ppermute | solution.py:20
  80.1 8.7 %collective-permute-start.24 = (bf16[264,128]{1,0:T(8,128)(2,1)S(1)}, bf16[264,128]{1,0:T(8,128)(2,1)S(1)}, u32[]{:S(2)}, u32[]{:S(2)}) collective-permute-start(bf16[264,128]{1,0:T(8,128)(2,1)S(1)} %fusion.1), channel_id=1, source_target_pairs={{0,24},{8,16},{16,8},{24,0},{1,25},{9,17},{17,9},{25,1},{2,26},{10... | collective-permute-start | bytes 202760 | tf_op jit(solution)/shard_map/ppermute | solution.py:20
  83.7 7.6 %collective-permute-start.23 = (bf16[264,128]{1,0:T(8,128)(2,1)S(1)}, bf16[264,128]{1,0:T(8,128)(2,1)S(1)}, u32[]{:S(2)}, u32[]{:S(2)}) collective-permute-start(bf16[264,128]{1,0:T(8,128)(2,1)S(1)} %fusion.1), channel_id=1, source_target_pairs={{0,16},{8,24},{16,0},{24,8},{1,17},{9,25},{17,1},{25,9},{2,18},{10... | collective-permute-start | bytes 202760 | tf_op jit(solution)/shard_map/ppermute | solution.py:20
  83.7 7.6 %collective-permute-start.22 = (bf16[264,128]{1,0:T(8,128)(2,1)S(1)}, bf16[264,128]{1,0:T(8,128)(2,1)S(1)}, u32[]{:S(2)}, u32[]{:S(2)}) collective-permute-start(bf16[264,128]{1,0:T(8,128)(2,1)S(1)} %fusion.1), channel_id=1, source_target_pairs={{0,8},{8,0},{16,24},{24,16},{1,9},{9,1},{17,25},{25,17},{2,10},{10... | collective-permute-start | bytes 202760 | tf_op jit(solution)/shard_map/ppermute | solution.py:20
  96.2 8.0 %collective-permute-start.25 = (bf16[264,128]{1,0:T(8,128)(2,1)S(1)}, bf16[264,128]{1,0:T(8,128)(2,1)S(1)}, u32[]{:S(2)}, u32[]{:S(2)}) collective-permute-start(bf16[264,128]{1,0:T(8,128)(2,1)S(1)} %add_convert_fusion.refs_0_), channel_id=1, source_target_pairs={{0,1},{1,0},{2,3},{3,2},{4,5},{5,4},{6,7},{7,6},{8,9},{9,8},{10,11... | collective-permute-start | bytes 202760 | tf_op jit(solution)/shard_map/ppermute | solution.py:20
  (23 other events, 156.1 us)
